TPU v7x, 128 devices: a whole 4x4x4 slice. The times are simulated.
128 devices in a mesh: row: 8 (over y, x_lo), col: 16 (over z, x_hi, core).
Axes of the slice: x: 4 (x_hi: 2, x_lo: 2; x = x_hi * 2 + x_lo), y: 4, z: 4, core: 2. Of those that a mesh axis runs over, the one named last changes fastest.
Arguments:
- teacher_feats: bfloat16 [64, 128, 4096], P(None, 'row', 'col'), may hold values from -6 to 6
- teacher_probs: float32 [8, 128, 4096], P(None, 'row', 'col'), may hold values from 0 to 1, as said below
- student_feats: bfloat16 [256, 128, 4096], P(None, 'row', 'col'), may hold values from 0 to 8
- conv_weight: bfloat16 [9, 256, 256], replicated, may hold values from -0.125 to 0.125
- class_weight: bfloat16 [256, 8], replicated, may hold values from -3 to 3
Outputs:
- refined: float32 [8, 128, 4096], P(None, 'row', 'col')
- feature_grad: bfloat16 [256, 128, 4096], P(None, 'row', 'col')
- grad_conv: float32 [9, 256, 256], replicated
- grad_class: float32 [256, 8], replicated
Inputs may be any that keep to these rules, and one draw needn't show every extreme that they name: `teacher_probs`: at every pixel the 8 values are positive and sum to one.
All inputs are finite; a program needn't handle non-finite values.
Results may differ from a plain program's by a relative error of at most 0.002.
The roundings to bfloat16 on the way count: a program that leaves them out, or rounds other values in their place, can miss the bound.
Values may be sent and summed in bfloat16 or wider, within the bound.
No kernel may reach another device: no remote copies, remote signals or barrier semaphores. Data moves between devices by JAX's collectives and lax.ppermute only.
A program may use at most 128 MiB of HBM per device.

v0:
```python
import functools

import jax
import jax.numpy as jnp
from jax import lax
from jax.experimental import pallas as pl
from jax.experimental.pallas import tpu as pltpu
from jax.sharding import PartitionSpec as P


EDGE_ROWS = 8
EDGE_COLS = 16
SPAN = 384
PAIR_TAPS = [tap for s in (1, 2, 4) for tap in ((0, s), (s, -s), (s, 0), (s, s))]


def shifted_by(cells, off_x):
    return cells if off_x == 0 else pltpu.roll(cells, (-off_x) % cells.shape[-1], cells.ndim - 1)


def vmem_of(mib):
    return pltpu.CompilerParams(vmem_limit_bytes=mib * 2**20)


def lane_of(shape):
    return lax.broadcasted_iota(jnp.int32, shape, len(shape) - 1)


def edges_kernel(up_ref, mid_ref, down_ref, left_ref, right_ref):
    channels = mid_ref.shape[1]
    group = lane_of((channels, 128)) // EDGE_COLS
    sources = [up_ref] + [mid_ref.at[pl.ds(8 * g, 8)] for g in range(mid_ref.shape[0] // 8)] + [down_ref]
    for g, source in enumerate(sources):
        left = jnp.zeros((channels, 128), jnp.float32)
        right = jnp.zeros((channels, 128), jnp.float32)
        for i in range(8):
            first = source[i, :, :128].astype(jnp.float32)
            last = source[i, :, -128:].astype(jnp.float32)
            left = jnp.where(group == i, pltpu.roll(first, EDGE_COLS * i, 1), left)
            right = jnp.where(group == i, pltpu.roll(last, (EDGE_COLS * (i + 1)) % 128, 1), right)
        left_ref[g] = left.astype(left_ref.dtype)
        right_ref[g] = right.astype(right_ref.dtype)


def sweep_row(weights, center_row, read_row):
    total = weights(0) * read_row(center_row)
    for index, (off_y, off_x) in enumerate(PAIR_TAPS):
        total += weights(1 + index) * shifted_by(read_row(center_row + off_y), off_x)
        total += weights(13 + index) * shifted_by(read_row(center_row - off_y), -off_x)
    return total


def affinity_kernel(
    place_ref, up_ref, mid_ref, down_ref, left_ref, right_ref, current_ref, weights_ref,
    feats, probs, next_probs, pairs, *, full_rows, full_cols, feat_channels, classes,
):
    rows = mid_ref.shape[0]
    cols = mid_ref.shape[2]
    tall = rows + 2 * EDGE_ROWS
    channels = mid_ref.shape[1]
    lanes = lane_of((channels, 128))

    def gather(i, carry):
        for g in range(tall // 8):
            if g == 0:
                body = up_ref[i]
            elif g == tall // 8 - 1:
                body = down_ref[i]
            else:
                body = mid_ref[8 * (g - 1) + i]
            from_right = pltpu.roll(right_ref[g].astype(jnp.float32), (128 - EDGE_COLS * i) % 128, 1)
            from_left = pltpu.roll(left_ref[g].astype(jnp.float32), (240 - EDGE_COLS * i) % 128, 1)
            side = jnp.where(lanes < EDGE_COLS, from_right, jnp.where(lanes >= 128 - EDGE_COLS, from_left, 0.0))
            body = body.astype(jnp.float32)
            row = 8 * g + i
            high, low = feat_channels, feat_channels + classes
            feats[row, :, :cols] = body[:high]
            feats[row, :, cols:] = side[:high]
            probs[row, :, :cols] = body[high:low] + body[low:]
            probs[row, :, cols:] = side[high:low] + side[low:]
        return carry

    lax.fori_loop(0, 8, gather, 0)
    pairs[:, tall - 8 :, :] = jnp.zeros((len(PAIR_TAPS), 8, SPAN), jnp.float32)

    def distances(row, carry):
        sums = [jnp.zeros((8, SPAN), jnp.float32) for _ in PAIR_TAPS]
        for c in range(feat_channels // 8):
            here = feats[row, 8 * c : 8 * c + 8, :]
            there = {0: here}
            for index, (off_y, off_x) in enumerate(PAIR_TAPS):
                if off_y not in there:
                    there[off_y] = feats[row + off_y, 8 * c : 8 * c + 8, :]
                gap = here - shifted_by(there[off_y], off_x)
                sums[index] += gap * gap
        for index in range(len(PAIR_TAPS)):
            pairs[index, pl.ds(row, 1), :] = jnp.sum(sums[index], axis=0, keepdims=True)
        return carry

    lax.fori_loop(0, tall - 4, distances, 0)

    shape = (tall, SPAN)
    lane = lane_of(shape)
    row_at = place_ref[0] - EDGE_ROWS + lax.broadcasted_iota(jnp.int32, shape, 0)
    col_at = place_ref[1] + jnp.where(lane < cols + EDGE_COLS, lane, lane - SPAN)

    def inside(off_y, off_x):
        y, x = row_at + off_y, col_at + off_x
        return (y >= 0) & (y < full_rows) & (x >= 0) & (x < full_cols)

    here_inside = inside(0, 0)
    for index, (off_y, off_x) in enumerate(PAIR_TAPS):
        present = here_inside & inside(off_y, off_x)
        pairs[index] = jnp.where(present, jnp.exp(pairs[index] * (-1.0 / feat_channels)), 0.0)
    wide = rows + EDGE_ROWS
    total = jnp.ones((wide, SPAN), jnp.float32)
    for index, (off_y, off_x) in enumerate(PAIR_TAPS):
        ahead = pairs[index, 4 : 4 + wide, :]
        behind = shifted_by(pairs[index, 4 - off_y : 4 - off_y + wide, :], -off_x)
        weights_ref[1 + index] = ahead
        weights_ref[13 + index] = behind
        total = total + (ahead + behind)
    scale = 1.0 / total
    weights_ref[0] = scale
    for index in range(1, 25):
        weights_ref[index] = weights_ref[index] * scale
    two_sweeps(weights_ref, lambda row: probs[row], next_probs, current_ref, rows)


def two_sweeps(weights_ref, read_row, middle, out_ref, rows):
    def first(row, carry):
        middle[row] = sweep_row(lambda o: weights_ref[o, pl.ds(row, 1), :], row + 4, read_row)
        return carry

    lax.fori_loop(0, rows + 8, first, 0)

    def second(row, carry):
        value = sweep_row(lambda o: weights_ref[o, pl.ds(row + 4, 1), :], row + 4, lambda r: middle[r])
        out_ref[row] = value[:, : out_ref.shape[2]]
        return carry

    lax.fori_loop(0, rows, second, 0)


def finish_kernel(weights_ref, up_ref, mid_ref, down_ref, out_ref, probs, next_probs):
    rows = mid_ref.shape[0]
    probs[:EDGE_ROWS] = up_ref[...]
    probs[EDGE_ROWS : EDGE_ROWS + rows] = mid_ref[...]
    probs[EDGE_ROWS + rows :] = down_ref[...]
    two_sweeps(weights_ref, lambda row: probs[row], next_probs, out_ref, rows)


def pass_on(cells, axis, step):
    ends = lax.axis_size(axis) - 1
    if step > 0:
        return lax.ppermute(cells, axis, [(i, i + 1) for i in range(ends)])
    return lax.ppermute(cells, axis, [(i + 1, i) for i in range(ends)])


def refine(teacher_feats, teacher_probs):
    feat_channels, rows, cols = teacher_feats.shape
    classes = teacher_probs.shape[0]
    high = lax.reduce_precision(teacher_probs, 8, 7)
    low = teacher_probs - high
    mid = jnp.concatenate(
        [teacher_feats, high.astype(jnp.bfloat16), low.astype(jnp.bfloat16)], axis=0
    ).transpose(1, 0, 2)
    up = pass_on(mid[rows - EDGE_ROWS :], "row", 1)
    down = pass_on(mid[:EDGE_ROWS], "row", -1)
    channels = mid.shape[1]
    groups = (rows + 2 * EDGE_ROWS) // 8
    edge = jax.ShapeDtypeStruct((groups, channels, 128), jnp.bfloat16)
    to_left, to_right = pl.pallas_call(edges_kernel, out_shape=(edge, edge), name="edges", compiler_params=vmem_of(12))(up, mid, down)
    left = pass_on(to_right, "col", 1)
    right = pass_on(to_left, "col", -1)
    place = jnp.stack([lax.axis_index("row") * rows, lax.axis_index("col") * cols]).astype(jnp.int32)
    tall = rows + 2 * EDGE_ROWS
    vmem = pl.BlockSpec(memory_space=pltpu.VMEM)
    current, weights = pl.pallas_call(
        functools.partial(
            affinity_kernel,
            full_rows=rows * lax.axis_size("row"),
            full_cols=cols * lax.axis_size("col"),
            feat_channels=feat_channels,
            classes=classes,
        ),
        out_shape=(
            jax.ShapeDtypeStruct((rows, classes, SPAN), jnp.float32),
            jax.ShapeDtypeStruct((25, rows + EDGE_ROWS, SPAN), jnp.float32),
        ),
        in_specs=[pl.BlockSpec(memory_space=pltpu.SMEM)] + [vmem] * 5,
        out_specs=(vmem, vmem),
        scratch_shapes=[
            pltpu.VMEM((tall, feat_channels, SPAN), jnp.float32),
            pltpu.VMEM((tall, classes, SPAN), jnp.float32),
            pltpu.VMEM((rows + 8, classes, SPAN), jnp.float32),
            pltpu.VMEM((len(PAIR_TAPS), tall, SPAN), jnp.float32),
        ],
        name="affinity",
        compiler_params=vmem_of(20),
    )(place, up, mid, down, left, right)
    up = pass_on(current[rows - EDGE_ROWS :], "row", 1)
    down = pass_on(current[:EDGE_ROWS], "row", -1)
    refined = pl.pallas_call(
        finish_kernel,
        out_shape=jax.ShapeDtypeStruct((rows, classes, cols), jnp.float32),
        scratch_shapes=[
            pltpu.VMEM((tall, classes, SPAN), jnp.float32),
            pltpu.VMEM((rows + 8, classes, SPAN), jnp.float32),
        ],
        name="finish",
        compiler_params=vmem_of(12),
    )(weights, up, current, down)
    return refined


def split_chunks(conv_part, class_part, devices):
    height, width = conv_part.shape
    tiles = conv_part.reshape(height // 8, 8, width // 128, 128).transpose(0, 2, 1, 3)
    tiles = tiles.reshape(-1, 8, 128)
    whole = (tiles.shape[0] // devices) * devices
    head = tiles[:whole].reshape(devices, -1, 128)
    rest = tiles[whole:].reshape(devices, -1, 128)
    small = class_part.reshape(devices, -1)
    small = jnp.pad(small, ((0, 0), (0, 128 - small.shape[1])))[:, None, :]
    return head, rest, small


def join_chunks(chunks, shapes, devices):
    conv_shape, class_shape = shapes
    channels, hidden = conv_shape[0] // 3, conv_shape[1] // 3
    n_tiles = 9 * channels * hidden // 1024
    head_rows = (n_tiles // devices) * 8
    conv_rows = n_tiles * 8 // devices
    head = chunks[:, :head_rows].reshape(-1, 8, 128)
    rest = chunks[:, head_rows:conv_rows].reshape(-1, 8, 128)
    tiles = jnp.concatenate([head, rest], axis=0)
    tiles = tiles.reshape(3, channels // 8, 3, hidden // 128, 8, 128).transpose(0, 2, 1, 4, 3, 5)
    small = chunks[:, conv_rows, : class_shape[0] * class_shape[1] // devices]
    return tiles.reshape(9, channels, hidden), small.reshape(class_shape)


def shift_of(largest):
    return jnp.clip(jnp.ceil(jnp.log2(jnp.maximum(largest, 1e-30))), -100.0, 120.0)


def pack_half(values, exponent):
    scaled = (values * jnp.exp2(14.0 - exponent)).astype(jnp.float16)
    marks = jnp.broadcast_to(exponent, values.shape[:-2] + (1, 128)).astype(jnp.float16)
    rows = values.shape[-2]
    fill = -(-(rows + 1) // 8) * 8 - rows - 1
    zeros = jnp.zeros(values.shape[:-2] + (fill, 128), jnp.float16)
    return jnp.concatenate([scaled, marks, zeros], axis=-2)


def unpack_half(packed, rows):
    exponent = packed[..., rows : rows + 1, :1].astype(jnp.float32)
    return packed[..., :rows, :].astype(jnp.float32) * jnp.exp2(exponent - 14.0)


def sum_everywhere(conv_part, class_part, axes):
    devices = 1
    for axis in axes:
        devices = devices * lax.axis_size(axis)
    head, rest, small = split_chunks(conv_part, class_part, devices)
    values = jnp.concatenate([head, rest, small], axis=1)
    rows = values.shape[1]
    largest = jnp.maximum(jnp.max(jnp.abs(conv_part)), jnp.max(jnp.abs(class_part)))
    sent = pack_half(values, shift_of(largest))
    got = lax.all_to_all(sent, axes, split_axis=0, concat_axis=0, tiled=True)
    total = jnp.sum(unpack_half(got, rows), axis=0)
    mine = pack_half(total, shift_of(jnp.max(jnp.abs(total))))
    spread = jnp.broadcast_to(mine[None], (devices,) + mine.shape)
    everyone = lax.all_to_all(spread, axes, split_axis=0, concat_axis=0, tiled=True)
    return join_chunks(unpack_half(everyone, rows), (conv_part.shape, class_part.shape), devices)


def unit_edges_kernel(up_ref, mid_ref, down_ref, left_ref, right_ref):
    rows, channels, cols = mid_ref.shape
    lanes = lane_of((channels, 128))
    left = jnp.zeros((channels, 128), jnp.float32)
    right = jnp.zeros((channels, 128), jnp.float32)
    for i in range(rows + 2):
        source = up_ref.at[0] if i == 0 else down_ref.at[0] if i == rows + 1 else mid_ref.at[i - 1]
        first = source[:, :128].astype(jnp.float32)
        last = source[:, cols - 128 :].astype(jnp.float32)
        left = jnp.where(lanes == i, pltpu.roll(first, i, 1), left)
        right = jnp.where(lanes == i, pltpu.roll(last, i + 1, 1), right)
    left_ref[...] = left.astype(left_ref.dtype)
    right_ref[...] = right.astype(right_ref.dtype)


def side_sums(side_ref, weights):
    side = side_ref[...].astype(jnp.float32)
    moved = [pltpu.roll(side, (128 - a) % 128, 1).astype(jnp.bfloat16) for a in range(3)]
    return jnp.dot(weights, jnp.concatenate(moved, axis=0), preferred_element_type=jnp.float32)


def conv_start(up_ref, mid_ref, down_ref, left_ref, right_ref, weights_ref, padded, left_sum, right_sum):
    rows, channels, _ = mid_ref.shape
    out = weights_ref.shape[0] // 3

    @pl.when(pl.program_id(0) == 0)
    def _():
        padded[0] = up_ref[0]
        padded[pl.ds(1, rows)] = mid_ref[...]
        padded[rows + 1] = down_ref[0]
        left_sum[...] = side_sums(left_ref, weights_ref[:out])
        right_sum[...] = side_sums(right_ref, weights_ref[2 * out :])


def conv_row(row, weights_ref, padded, left_sum, right_sum):
    out = weights_ref.shape[0] // 3
    cols = padded.shape[2]
    stack = jnp.concatenate([padded[row], padded[row + 1], padded[row + 2]], axis=0)
    parts = jnp.dot(weights_ref[...], stack, preferred_element_type=jnp.float32)
    lanes = lane_of((out, cols))
    left = jnp.concatenate([pltpu.roll(left_sum[...], (128 - row) % 128, 1), jnp.zeros((out, cols - 128), jnp.float32)], axis=1)
    right = jnp.concatenate([jnp.zeros((out, cols - 128), jnp.float32), pltpu.roll(right_sum[...], 127 - row, 1)], axis=1)
    before = jnp.where(lanes == 0, left, pltpu.roll(parts[:out], 1, 1))
    after = jnp.where(lanes == cols - 1, right, pltpu.roll(parts[2 * out :], cols - 1, 1))
    return parts[out : 2 * out] + (before + after)


STEP_ROWS = 2


def forward_kernel(
    up_ref, mid_ref, down_ref, left_ref, right_ref, weights_ref, class_ref,
    slope_ref, hidden_ref, guess_ref, padded, left_sum, right_sum,
):
    conv_start(up_ref, mid_ref, down_ref, left_ref, right_ref, weights_ref, padded, left_sum, right_sum)
    for k in range(STEP_ROWS):
        pre_act = conv_row(pl.program_id(0) * STEP_ROWS + k, weights_ref, padded, left_sum, right_sum)
        logistic = jax.nn.sigmoid(pre_act)
        slope_ref[k] = logistic * (1.0 + pre_act * (1.0 - logistic))
        hidden = (pre_act * logistic).astype(jnp.bfloat16)
        hidden_ref[k] = hidden
        logit = jnp.dot(class_ref[...], hidden, preferred_element_type=jnp.float32)
        guess_ref[k] = jax.nn.sigmoid(logit)


def back_kernel(guess_ref, refined_ref, slope_ref, class_ref, back_ref, error_ref):
    for k in range(STEP_ROWS):
        error = (guess_ref[k] - refined_ref[k]).astype(jnp.bfloat16)
        error_ref[k] = error
        summed = jnp.dot(class_ref[...], error, preferred_element_type=jnp.float32)
        back_ref[k] = (summed * slope_ref[k]).astype(jnp.bfloat16)


CONTRACT_LAST = (((1,), (1,)), ((), ()))


def grads_kernel(
    up_ref, mid_ref, down_ref, left_ref, right_ref, back_ref, hidden_ref, error_ref,
    conv_ref, class_ref, padded, first_cols, last_cols,
):
    rows, channels, cols = mid_ref.shape
    step = pl.program_id(0)

    @pl.when(step == 0)
    def _():
        padded[0] = up_ref[0]
        padded[pl.ds(1, rows)] = mid_ref[...]
        padded[rows + 1] = down_ref[0]
        conv_ref[...] = jnp.zeros(conv_ref.shape, jnp.float32)
        class_ref[...] = jnp.zeros(class_ref.shape, jnp.float32)
        first_cols[...] = jnp.zeros(first_cols.shape, jnp.float32)
        last_cols[...] = jnp.zeros(last_cols.shape, jnp.float32)

    lanes = lane_of((back_ref.shape[1], cols))
    narrow = lane_of((back_ref.shape[1], 128))
    images, backs = [], []
    for k in range(STEP_ROWS):
        row = step * STEP_ROWS + k
        images.append(jnp.concatenate([padded[row], padded[row + 1], padded[row + 2]], axis=0))
        back = back_ref[k].astype(jnp.float32)
        first_cols[...] = jnp.where(narrow == row + 1, pltpu.roll(back[:, :128], row + 1, 1), first_cols[...])
        last_cols[...] = jnp.where(narrow == row + 1, pltpu.roll(back[:, cols - 128 :], row + 2, 1), last_cols[...])
        below = jnp.where(lanes == cols - 1, 0.0, pltpu.roll(back, cols - 1, 1))
        above = jnp.where(lanes == 0, 0.0, pltpu.roll(back, 1, 1))
        backs.append(
            jnp.concatenate([below.astype(jnp.bfloat16), back_ref[k], above.astype(jnp.bfloat16)], axis=0)
        )
        class_ref[...] += lax.dot_general(
            hidden_ref[k], error_ref[k], CONTRACT_LAST, preferred_element_type=jnp.float32
        )
    conv_ref[...] += lax.dot_general(
        jnp.concatenate(images, axis=1), jnp.concatenate(backs, axis=1), CONTRACT_LAST,
        preferred_element_type=jnp.float32,
    )

    @pl.when(step == pl.num_programs(0) - 1)
    def _():
        hidden = back_ref.shape[1]
        for side_ref, cells, place in ((left_ref, first_cols, 0), (right_ref, last_cols, 2 * hidden)):
            side = side_ref[...].astype(jnp.float32)
            moved = [pltpu.roll(side, (1 - a) % 128, 1).astype(jnp.bfloat16) for a in range(3)]
            conv_ref[:, pl.ds(place, hidden)] += lax.dot_general(
                jnp.concatenate(moved, axis=0), cells[...].astype(jnp.bfloat16), CONTRACT_LAST,
                preferred_element_type=jnp.float32,
            )


def feature_kernel(
    up_ref, mid_ref, down_ref, left_ref, right_ref, weights_ref, out_ref, padded, left_sum, right_sum
):
    conv_start(up_ref, mid_ref, down_ref, left_ref, right_ref, weights_ref, padded, left_sum, right_sum)
    for k in range(STEP_ROWS):
        row = pl.program_id(0) * STEP_ROWS + k
        out_ref[k] = conv_row(row, weights_ref, padded, left_sum, right_sum).astype(out_ref.dtype)


def whole(array):
    return pl.BlockSpec(array.shape, lambda i: (0,) * array.ndim)


def by_rows(shape):
    return pl.BlockSpec((STEP_ROWS,) + shape[1:], lambda i: (i, 0, 0))


def unit_rows(cells):
    return pass_on(cells[-1:], "row", 1), pass_on(cells[:1], "row", -1)


def unit_cols(cells, up, down):
    edge = jax.ShapeDtypeStruct((cells.shape[1], 128), cells.dtype)
    to_left, to_right = pl.pallas_call(
        unit_edges_kernel, out_shape=(edge, edge), name="unit_edges",
        compiler_params=vmem_of(16),
    )(up, cells, down)
    return pass_on(to_right, "col", 1), pass_on(to_left, "col", -1)


def conv_scratch(rows, channels, cols, out):
    return [
        pltpu.VMEM((rows + 2, channels, cols), jnp.bfloat16),
        pltpu.VMEM((out, 128), jnp.float32),
        pltpu.VMEM((out, 128), jnp.float32),
    ]


def row_call(kernel, name, rows, args, arg_rows, outs, out_rows, scratch, vmem):
    return pl.pallas_call(
        kernel,
        grid=(rows // STEP_ROWS,),
        in_specs=[by_rows(a.shape) if split else whole(a) for a, split in zip(args, arg_rows)],
        out_specs=tuple(by_rows(o.shape) if split else whole(o) for o, split in zip(outs, out_rows)),
        out_shape=tuple(outs),
        scratch_shapes=scratch,
        name=name,
        compiler_params=vmem_of(vmem),
    )(*args)


def shards(teacher_feats, teacher_probs, student_feats, conv_weight, class_weight):
    channels, rows, cols = student_feats.shape
    hidden_size, classes = class_weight.shape
    pixel_count = float(rows * cols)
    taps = conv_weight.reshape(3, 3, channels, hidden_size)
    forward_weight = taps.transpose(1, 3, 0, 2).reshape(3 * hidden_size, 3 * channels)
    back_weight = taps[::-1, ::-1].transpose(1, 2, 0, 3).reshape(3 * channels, 3 * hidden_size)
    student = student_feats.transpose(1, 0, 2)
    student_up, student_down = unit_rows(student)
    student_left, student_right = unit_cols(student, student_up, student_down)
    halo = (student_up, student, student_down, student_left, student_right)
    f32, bf16 = jnp.float32, jnp.bfloat16
    slope, hidden, guess = row_call(
        forward_kernel, "forward", rows,
        halo + (forward_weight, class_weight.T), [False] * 7,
        [
            jax.ShapeDtypeStruct((rows, hidden_size, cols), f32),
            jax.ShapeDtypeStruct((rows, hidden_size, cols), bf16),
            jax.ShapeDtypeStruct((rows, classes, cols), f32),
        ],
        [True] * 3, conv_scratch(rows, channels, cols, hidden_size), 32,
    )
    refined = refine(teacher_feats, teacher_probs)
    back, error = row_call(
        back_kernel, "back", rows, (guess, refined, slope, class_weight), [True, True, True, False],
        [
            jax.ShapeDtypeStruct((rows, hidden_size, cols), bf16),
            jax.ShapeDtypeStruct((rows, classes, cols), bf16),
        ],
        [True] * 2, [], 16,
    )
    back_up, back_down = unit_rows(back)
    conv_part, class_part = row_call(
        grads_kernel, "grads", rows, halo + (back, hidden, error), [False] * 5 + [True] * 3,
        [
            jax.ShapeDtypeStruct((3 * channels, 3 * hidden_size), f32),
            jax.ShapeDtypeStruct((hidden_size, classes), f32),
        ],
        [False] * 2,
        [pltpu.VMEM((rows + 2, channels, cols), bf16)] + [pltpu.VMEM((hidden_size, 128), f32)] * 2, 40,
    )
    back_left, back_right = unit_cols(back, back_up, back_down)
    (feature_grad,) = row_call(
        feature_kernel, "feature", rows,
        (back_up, back, back_down, back_left, back_right, back_weight), [False] * 6,
        [jax.ShapeDtypeStruct((rows, channels, cols), bf16)],
        [True], conv_scratch(rows, hidden_size, cols, channels), 32,
    )
    summed_conv, summed_class = sum_everywhere(conv_part, class_part, ("row", "col"))
    grad_conv = summed_conv / pixel_count
    grad_class = summed_class / pixel_count
    return (refined.transpose(1, 0, 2), feature_grad.transpose(1, 0, 2), grad_conv, grad_class)


def solution(mesh):
    in_specs = (P(None, "row", "col"), P(None, "row", "col"), P(None, "row", "col"), P(), P())
    out_specs = (P(None, "row", "col"), P(None, "row", "col"), P(), P())
    return jax.shard_map(shards, mesh=mesh, in_specs=in_specs, out_specs=out_specs, check_vma=False)
```

profile of v0, /device:TPU:1, one launch (start us, length us, event | category | flops | bytes accessed | tf_op | source)
XLA Modules:
  0.0 211.3 jit_solution(15005076782837811021)
XLA Ops:
  3.9 3.9 %collective-permute-start = (bf16[8,80,256]{2,1,0:T(8,128)(2,1)}, bf16[8,80,256]{2,1,0:T(8,128)(2,1)S(1)}, u32[]{:S(2)}, u32[]{:S(2)}) collective-permute-start(bf16[8,80,256]{2,1,0:T(8,128)(2,1)} %get-tuple-element.59), channel_id=1, source_target_pairs={{0,16},{16,32},{32,48},{48,64},{64,80},{80,96},{96,112},{1,17},{17... | collective-permute-start | bytes 983048 | tf_op jit(solution)/shard_map/ppermute | solution.py:156
  10.6 4.0 %collective-permute-start.6 = (bf16[1,256,256]{2,1,0:T(8,128)(2,1)}, bf16[1,256,256]{2,1,0:T(8,128)(2,1)S(1)}, u32[]{:S(2)}, u32[]{:S(2)}) collective-permute-start(bf16[1,256,256]{2,1,0:T(8,128)(2,1)} %get-tuple-element.57), channel_id=1, source_target_pairs={{0,16},{16,32},{32,48},{48,64},{64,80},{80,96},{96,112},{1,17},{17... | collective-permute-start | bytes 393224 | tf_op jit(solution)/shard_map/ppermute | solution.py:156
  15.9 7.6 %collective-permute-done.1.down_ref = bf16[8,80,256]{2,1,0:T(8,128)(2,1)S(1)} collective-permute-done((bf16[8,80,256]{2,1,0:T(8,128)(2,1)}, bf16[8,80,256]{2,1,0:T(8,128)(2,1)S(1)}, u32[]{:S(2)}, u32[]{:S(2)}) %collective-permute-start.1) | collective-permute-done | bytes 327712 | tf_op jit(solution)/shard_map/ppermute | solution.py:157
  23.8 7.2 %collective-permute-start.2 = (bf16[4,80,128]{2,1,0:T(8,128)(2,1)S(1)}, bf16[4,80,128]{2,1,0:T(8,128)(2,1)S(1)}, u32[]{:S(2)}, u32[]{:S(2)}) collective-permute-start(bf16[4,80,128]{2,1,0:T(8,128)(2,1)S(1)} %get-tuple-element.19), channel_id=1, source_target_pairs={{0,1},{1,2},{2,3},{3,4},{4,5},{5,6},{6,7},{7,8},{8,9},{9,10},{10,1... | collective-permute-start | bytes 245768 | tf_op jit(solution)/shard_map/ppermute | solution.py:156
  31.0 1.9 collective-permute-start.3
  33.0 5.3 %collective-permute-done.3.right_ref = bf16[4,80,128]{2,1,0:T(8,128)(2,1)S(1)} collective-permute-done((bf16[4,80,128]{2,1,0:T(8,128)(2,1)S(1)}, bf16[4,80,128]{2,1,0:T(8,128)(2,1)S(1)}, u32[]{:S(2)}, u32[]{:S(2)}) %collective-permute-start.3) | collective-permute-done | bytes 81952 | tf_op jit(solution)/shard_map/ppermute | solution.py:157
  38.3 16.1 %affinity.1 = (f32[16,8,384]{2,1,0:T(8,128)S(1)}, f32[25,24,384]{2,1,0:T(8,128)S(1)}) custom-call(s32[2]{0:T(128)S(1)} %pad_add_fusion.place_ref, bf16[8,80,256]{2,1,0:T(8,128)(2,1)S(1)} %collective-permute-done.up_ref, bf16[16,80,256]{2,1,0:T(8,128)(2,1)S(1)} %maximum_bitcast_fusion.mid_ref, bf16[8,80,256]{2,1,0:T(8,128)(2,1)S(1)} %collective-permute-done.1.down_ref, ...), custom_call_target="tpu_custom_call" | custom-call | tf_op jit(solution)/shard_map/affinity/pallas_call | solution.py:179
  56.0 2.8 %collective-permute-start.4 = (f32[8,8,384]{2,1,0:T(8,128)}, f32[8,8,384]{2,1,0:T(8,128)}, u32[]{:S(2)}, u32[]{:S(2)}) collective-permute-start(f32[8,8,384]{2,1,0:T(8,128)} %get-tuple-element.61), channel_id=1, source_target_pairs={{0,16},{16,32},{32,48},{48,64},{64,80},{80,96},{96,112},{1,17},{17... | collective-permute-start | bytes 294920 | tf_op jit(solution)/shard_map/ppermute | solution.py:156
  60.2 2.2 %unit_edges.2 = (bf16[256,128]{1,0:T(8,128)(2,1)}, bf16[256,128]{1,0:T(8,128)(2,1)}) custom-call(bf16[1,256,256]{2,1,0:T(8,128)(2,1)S(1)} %collective-permute-done.6.up_ref, bf16[16,256,256]{2,1,0:T(8,128)(2,1)S(1)} %bitcast.40, bf16[1,256,256]{2,1,0:T(8,128)(2,1)} %collective-permute-done.7.down_ref), custom_call_target="tpu_custom_call" | custom-call | tf_op jit(solution)/shard_map/unit_edges/pallas_call | solution.py:428
  62.4 2.7 %collective-permute-start.8 = (bf16[256,128]{1,0:T(8,128)(2,1)}, bf16[256,128]{1,0:T(8,128)(2,1)S(1)}, u32[]{:S(2)}, u32[]{:S(2)}) collective-permute-start(bf16[256,128]{1,0:T(8,128)(2,1)} %get-tuple-element.23), channel_id=1, source_target_pairs={{0,1},{1,2},{2,3},{3,4},{4,5},{5,6},{6,7},{7,8},{8,9},{9,10},{10,1... | collective-permute-start | bytes 196616 | tf_op jit(solution)/shard_map/ppermute | solution.py:156
  67.0 3.6 %copy.61 = bf16[3,3,256,256]{2,0,3,1:T(4,128)(2,1)} copy(bf16[3,3,256,256]{3,2,1,0:T(8,128)(2,1)} %bitcast.55) | data formatting | bytes 2359296 | tf_op jit(solution)/shard_map/reshape | solution.py:460
  73.2 16.3 %forward.1 = (f32[16,256,256]{2,1,0:T(8,128)S(1)}, bf16[16,256,256]{2,1,0:T(8,128)(2,1)S(1)}, f32[16,8,256]{2,1,0:T(8,128)S(1)}) custom-call(bf16[1,256,256]{2,1,0:T(8,128)(2,1)S(1)} %collective-permute-done.6.up_ref, bf16[16,256,256]{2,1,0:T(8,128)(2,1)S(1)} %bitcast.41, bf16[1,256,256]{2,1,0:T(8,128)(2,1)} %collective-permute-done.7.down_ref, ...), custom_call_target="tpu_custom_call" | custom-call | tf_op jit(solution)/shard_map/forward/pallas_call | solution.py:444
  89.5 6.1 %finish.1.refined_ref = f32[16,8,256]{2,1,0:T(8,128)S(1)} custom-call(f32[25,24,384]{2,1,0:T(8,128)S(1)} %copy-done.3, f32[8,8,384]{2,1,0:T(8,128)} %collective-permute-done.4.up_ref, f32[16,8,384]{2,1,0:T(8,128)S(1)} %copy-done.5, f32[8,8,384]{2,1,0:T(8,128)} %collective-permute-done.5.down_ref), custom_call_target="tpu_custom_call" | custom-call | tf_op jit(solution)/shard_map/finish/pallas_call | solution.py:204
  97.3 9.3 %grads.1 = (f32[768,768]{1,0:T(8,128)S(1)}, f32[256,8]{1,0:T(8,128)S(1)}) custom-call(bf16[1,256,256]{2,1,0:T(8,128)(2,1)S(1)} %collective-permute-done.6.up_ref, bf16[16,256,256]{2,1,0:T(8,128)(2,1)S(1)} %bitcast.42, bf16[1,256,256]{2,1,0:T(8,128)(2,1)} %collective-permute-done.7.down_ref, bf16[256,128]{1,0:T(8,128)(2,1)S(1)} %collective-permute-done.8.left_ref, ...), custom_call_target="tpu_custom_call" | custom-call | tf_op jit(solution)/shard_map/grads/pallas_call | solution.py:444
  110.6 33.8 %all_to_all.10 = f16[128,40,128]{2,1,0:T(8,128)(2,1)S(1)} all-to-all(f16[128,40,128]{2,1,0:T(8,128)(2,1)S(1)} %maximum_maximum_fusion), channel_id=1, replica_groups=mesh['row'=8,'col'=16] {'row','col'}, dimensions={0} | all-to-all | bytes 2621440 | tf_op jit(solution)/shard_map/all_to_all | solution.py:270
  147.7 5.2 %all-to-all-start.1 = ((f16[128,40,128]{2,1,0:T(8,128)(2,1)}), f16[128,40,128]{2,1,0:T(8,128)(2,1)}, u32[]{:S(2)}, u32[]{:S(2)}) async-start(f16[128,40,128]{2,1,0:T(8,128)(2,1)} %broadcast_in_dim.26), calls=%async_computation.1 | async-start | bytes 2621440 | tf_op jit(solution)/shard_map/all_to_all | solution.py:274
  153.0 3.4 %collective-permute-start.10 = (bf16[1,256,256]{2,1,0:T(8,128)(2,1)S(1)}, bf16[1,256,256]{2,1,0:T(8,128)(2,1)S(1)}, u32[]{:S(2)}, u32[]{:S(2)}) collective-permute-start(bf16[1,256,256]{2,1,0:T(8,128)(2,1)S(1)} %get-tuple-element.55), channel_id=1, source_target_pairs={{0,16},{16,32},{32,48},{48,64},{64,80},{80,96},{96,112},{1,17},{17... | collective-permute-start | bytes 393224 | tf_op jit(solution)/shard_map/ppermute | solution.py:156
  157.9 10.1 %collective-permute-done.10.up_ref = bf16[1,256,256]{2,1,0:T(8,128)(2,1)S(1)} collective-permute-done((bf16[1,256,256]{2,1,0:T(8,128)(2,1)S(1)}, bf16[1,256,256]{2,1,0:T(8,128)(2,1)S(1)}, u32[]{:S(2)}, u32[]{:S(2)}) %collective-permute-start.10) | collective-permute-done | bytes 131104 | tf_op jit(solution)/shard_map/ppermute | solution.py:156
  168.0 6.1 %collective-permute-done.11.down_ref = bf16[1,256,256]{2,1,0:T(8,128)(2,1)S(1)} collective-permute-done((bf16[1,256,256]{2,1,0:T(8,128)(2,1)S(1)}, bf16[1,256,256]{2,1,0:T(8,128)(2,1)S(1)}, u32[]{:S(2)}, u32[]{:S(2)}) %collective-permute-start.11) | collective-permute-done | bytes 131104 | tf_op jit(solution)/shard_map/ppermute | solution.py:157
  174.8 4.7 %collective-permute-start.12 = (bf16[256,128]{1,0:T(8,128)(2,1)S(1)}, bf16[256,128]{1,0:T(8,128)(2,1)S(1)}, u32[]{:S(2)}, u32[]{:S(2)}) collective-permute-start(bf16[256,128]{1,0:T(8,128)(2,1)S(1)} %get-tuple-element.28), channel_id=1, source_target_pairs={{0,1},{1,2},{2,3},{3,4},{4,5},{5,6},{6,7},{7,8},{8,9},{9,10},{10,1... | collective-permute-start | bytes 196616 | tf_op jit(solution)/shard_map/ppermute | solution.py:156
  181.4 2.2 %copy.63 = bf16[3,3,256,256]{3,0,2,1:T(4,128)(2,1)} copy(bf16[3,3,256,256]{3,2,1,0:T(8,128)(2,1)S(1)} %bitcast.56) | data formatting | bytes 2359296 | tf_op jit(solution)/shard_map/reshape | solution.py:460
  183.6 9.0 %rev.3 = bf16[3,3,256,256]{3,0,2,1:T(4,128)(2,1)} reverse(bf16[3,3,256,256]{3,0,2,1:T(4,128)(2,1)} %copy.63), dimensions={0,1} | reverse | bytes 2359296 | tf_op jit(solution)/shard_map/rev | solution.py:462
  194.9 7.9 %feature.1 = bf16[16,256,256]{2,1,0:T(8,128)(2,1)S(1)} custom-call(bf16[1,256,256]{2,1,0:T(8,128)(2,1)S(1)} %collective-permute-done.10.up_ref, bf16[16,256,256]{2,1,0:T(8,128)(2,1)S(1)} %copy-done.1, bf16[1,256,256]{2,1,0:T(8,128)(2,1)S(1)} %collective-permute-done.11.down_ref, bf16[256,128]{1,0:T(8,128)(2,1)S(1)} %collective-permute-done.12.left_ref, ...), custom_call_target="tpu_custom_call" | custom-call | tf_op jit(solution)/shard_map/feature/pallas_call | solution.py:444
  202.9 2.5 %copy.68 = bf16[256,16,256]{2,1,0:T(8,128)(2,1)} copy(bf16[256,16,256]{2,0,1:T(8,128)(2,1)S(1)} %bitcast.45) | data formatting | bytes 4194304
  (84 shorter events, 34.3 us)
Async XLA Ops:
  0.6 8.5 %copy-start.9 = (bf16[256,16,256]{2,1,0:T(8,128)(2,1)S(1)}, bf16[256,16,256]{2,1,0:T(8,128)(2,1)}, u32[]{:S(2)}) copy-start(bf16[256,16,256]{2,1,0:T(8,128)(2,1)} %param.7) | copy-start | bytes 6291460
  3.9 12.0 %collective-permute-start = (bf16[8,80,256]{2,1,0:T(8,128)(2,1)}, bf16[8,80,256]{2,1,0:T(8,128)(2,1)S(1)}, u32[]{:S(2)}, u32[]{:S(2)}) collective-permute-start(bf16[8,80,256]{2,1,0:T(8,128)(2,1)} %get-tuple-element.59), channel_id=1, source_target_pairs={{0,16},{16,32},{32,48},{48,64},{64,80},{80,96},{96,112},{1,17},{17... | collective-permute-start | bytes 983048 | tf_op jit(solution)/shard_map/ppermute | solution.py:156
  7.9 15.6 %collective-permute-start.1 = (bf16[8,80,256]{2,1,0:T(8,128)(2,1)}, bf16[8,80,256]{2,1,0:T(8,128)(2,1)S(1)}, u32[]{:S(2)}, u32[]{:S(2)}) collective-permute-start(bf16[8,80,256]{2,1,0:T(8,128)(2,1)} %get-tuple-element.58), channel_id=1, source_target_pairs={{16,0},{32,16},{48,32},{64,48},{80,64},{96,80},{112,96},{17,1},{33... | collective-permute-start | bytes 983048 | tf_op jit(solution)/shard_map/ppermute | solution.py:157
  10.6 49.6 %collective-permute-start.6 = (bf16[1,256,256]{2,1,0:T(8,128)(2,1)}, bf16[1,256,256]{2,1,0:T(8,128)(2,1)S(1)}, u32[]{:S(2)}, u32[]{:S(2)}) collective-permute-start(bf16[1,256,256]{2,1,0:T(8,128)(2,1)} %get-tuple-element.57), channel_id=1, source_target_pairs={{0,16},{16,32},{32,48},{48,64},{64,80},{80,96},{96,112},{1,17},{17... | collective-permute-start | bytes 393224 | tf_op jit(solution)/shard_map/ppermute | solution.py:156
  14.6 45.6 %collective-permute-start.7 = (bf16[1,256,256]{2,1,0:T(8,128)(2,1)}, bf16[1,256,256]{2,1,0:T(8,128)(2,1)}, u32[]{:S(2)}, u32[]{:S(2)}) collective-permute-start(bf16[1,256,256]{2,1,0:T(8,128)(2,1)} %get-tuple-element.56), channel_id=1, source_target_pairs={{16,0},{32,16},{48,32},{64,48},{80,64},{96,80},{112,96},{17,1},{33... | collective-permute-start | bytes 393224 | tf_op jit(solution)/shard_map/ppermute | solution.py:157
  23.8 9.2 %collective-permute-start.2 = (bf16[4,80,128]{2,1,0:T(8,128)(2,1)S(1)}, bf16[4,80,128]{2,1,0:T(8,128)(2,1)S(1)}, u32[]{:S(2)}, u32[]{:S(2)}) collective-permute-start(bf16[4,80,128]{2,1,0:T(8,128)(2,1)S(1)} %get-tuple-element.19), channel_id=1, source_target_pairs={{0,1},{1,2},{2,3},{3,4},{4,5},{5,6},{6,7},{7,8},{8,9},{9,10},{10,1... | collective-permute-start | bytes 245768 | tf_op jit(solution)/shard_map/ppermute | solution.py:156
  31.0 7.3 %collective-permute-start.3 = (bf16[4,80,128]{2,1,0:T(8,128)(2,1)S(1)}, bf16[4,80,128]{2,1,0:T(8,128)(2,1)S(1)}, u32[]{:S(2)}, u32[]{:S(2)}) collective-permute-start(bf16[4,80,128]{2,1,0:T(8,128)(2,1)S(1)} %get-tuple-element.20), channel_id=1, source_target_pairs={{1,0},{2,1},{3,2},{4,3},{5,4},{6,5},{7,6},{8,7},{9,8},{10,9},{11,1... | collective-permute-start | bytes 245768 | tf_op jit(solution)/shard_map/ppermute | solution.py:157
  55.3 4.9 %copy-start.4 = (f32[16,8,384]{2,1,0:T(8,128)}, f32[16,8,384]{2,1,0:T(8,128)S(1)}, u32[]{:S(2)}) copy-start(f32[16,8,384]{2,1,0:T(8,128)S(1)} %get-tuple-element.22.mid_ref) | copy-start | bytes 589828
  56.0 33.5 %collective-permute-start.4 = (f32[8,8,384]{2,1,0:T(8,128)}, f32[8,8,384]{2,1,0:T(8,128)}, u32[]{:S(2)}, u32[]{:S(2)}) collective-permute-start(f32[8,8,384]{2,1,0:T(8,128)} %get-tuple-element.61), channel_id=1, source_target_pairs={{0,16},{16,32},{32,48},{48,64},{64,80},{80,96},{96,112},{1,17},{17... | collective-permute-start | bytes 294920 | tf_op jit(solution)/shard_map/ppermute | solution.py:156
  58.8 30.6 %collective-permute-start.5 = (f32[8,8,384]{2,1,0:T(8,128)}, f32[8,8,384]{2,1,0:T(8,128)}, u32[]{:S(2)}, u32[]{:S(2)}) collective-permute-start(f32[8,8,384]{2,1,0:T(8,128)} %get-tuple-element.60), channel_id=1, source_target_pairs={{16,0},{32,16},{48,32},{64,48},{80,64},{96,80},{112,96},{17,1},{33... | collective-permute-start | bytes 294920 | tf_op jit(solution)/shard_map/ppermute | solution.py:157
  62.4 10.8 %collective-permute-start.8 = (bf16[256,128]{1,0:T(8,128)(2,1)}, bf16[256,128]{1,0:T(8,128)(2,1)S(1)}, u32[]{:S(2)}, u32[]{:S(2)}) collective-permute-start(bf16[256,128]{1,0:T(8,128)(2,1)} %get-tuple-element.23), channel_id=1, source_target_pairs={{0,1},{1,2},{2,3},{3,4},{4,5},{5,6},{6,7},{7,8},{8,9},{9,10},{10,1... | collective-permute-start | bytes 196616 | tf_op jit(solution)/shard_map/ppermute | solution.py:156
  65.1 8.1 %collective-permute-start.9 = (bf16[256,128]{1,0:T(8,128)(2,1)}, bf16[256,128]{1,0:T(8,128)(2,1)S(1)}, u32[]{:S(2)}, u32[]{:S(2)}) collective-permute-start(bf16[256,128]{1,0:T(8,128)(2,1)} %get-tuple-element.24), channel_id=1, source_target_pairs={{1,0},{2,1},{3,2},{4,3},{5,4},{6,5},{7,6},{8,7},{9,8},{10,9},{11,1... | collective-permute-start | bytes 196616 | tf_op jit(solution)/shard_map/ppermute | solution.py:157
  67.0 5.3 %copy-start.7 = (bf16[256,8]{0,1:T(8,128)(2,1)S(1)}, bf16[256,8]{0,1:T(8,128)(2,1)}, u32[]{:S(2)}) copy-start(bf16[256,8]{0,1:T(8,128)(2,1)} %param.9) | copy-start | bytes 12292
  73.1 16.4 %copy-start.3 = (f32[25,24,384]{2,1,0:T(8,128)S(1)}, f32[25,24,384]{2,1,0:T(8,128)}, u32[]{:S(2)}) copy-start(f32[25,24,384]{2,1,0:T(8,128)} %copy-done.2) | copy-start | bytes 2764804
  73.1 16.4 %copy-start.5 = (f32[16,8,384]{2,1,0:T(8,128)S(1)}, f32[16,8,384]{2,1,0:T(8,128)}, u32[]{:S(2)}) copy-start(f32[16,8,384]{2,1,0:T(8,128)} %copy-done.4) | copy-start | bytes 589828
  73.2 22.4 %copy-start.6 = (bf16[256,8]{1,0:T(8,128)(2,1)S(1)}, bf16[256,8]{1,0:T(8,128)(2,1)}, u32[]{:S(2)}) copy-start(bf16[256,8]{1,0:T(8,128)(2,1)} %copy.62.class_ref) | copy-start | bytes 12292
  97.3 9.3 %copy-start = (bf16[16,256,256]{2,1,0:T(8,128)(2,1)}, bf16[16,256,256]{2,1,0:T(8,128)(2,1)S(1)}, u32[]{:S(2)}) copy-start(bf16[16,256,256]{2,1,0:T(8,128)(2,1)S(1)} %get-tuple-element.27.mid_ref.back_ref) | copy-start | bytes 6291460
  144.9 8.0 %copy-start.1 = (bf16[16,256,256]{2,1,0:T(8,128)(2,1)S(1)}, bf16[16,256,256]{2,1,0:T(8,128)(2,1)}, u32[]{:S(2)}) copy-start(bf16[16,256,256]{2,1,0:T(8,128)(2,1)} %copy-done) | copy-start | bytes 6291460
  147.7 57.6 %all-to-all-start.1 = ((f16[128,40,128]{2,1,0:T(8,128)(2,1)}), f16[128,40,128]{2,1,0:T(8,128)(2,1)}, u32[]{:S(2)}, u32[]{:S(2)}) async-start(f16[128,40,128]{2,1,0:T(8,128)(2,1)} %broadcast_in_dim.26), calls=%async_computation.1 | async-start | bytes 2621440 | tf_op jit(solution)/shard_map/all_to_all | solution.py:274
  153.0 28.4 %copy-start.8 = (bf16[9,256,256]{2,1,0:T(8,128)(2,1)S(1)}, bf16[9,256,256]{2,1,0:T(8,128)(2,1)}, u32[]{:S(2)}) copy-start(bf16[9,256,256]{2,1,0:T(8,128)(2,1)} %param.8) | copy-start | bytes 3538948
  153.0 15.0 %collective-permute-start.10 = (bf16[1,256,256]{2,1,0:T(8,128)(2,1)S(1)}, bf16[1,256,256]{2,1,0:T(8,128)(2,1)S(1)}, u32[]{:S(2)}, u32[]{:S(2)}) collective-permute-start(bf16[1,256,256]{2,1,0:T(8,128)(2,1)S(1)} %get-tuple-element.55), channel_id=1, source_target_pairs={{0,16},{16,32},{32,48},{48,64},{64,80},{80,96},{96,112},{1,17},{17... | collective-permute-start | bytes 393224 | tf_op jit(solution)/shard_map/ppermute | solution.py:156
  156.4 17.7 %collective-permute-start.11 = (bf16[1,256,256]{2,1,0:T(8,128)(2,1)S(1)}, bf16[1,256,256]{2,1,0:T(8,128)(2,1)S(1)}, u32[]{:S(2)}, u32[]{:S(2)}) collective-permute-start(bf16[1,256,256]{2,1,0:T(8,128)(2,1)S(1)} %get-tuple-element.54), channel_id=1, source_target_pairs={{16,0},{32,16},{48,32},{64,48},{80,64},{96,80},{112,96},{17,1},{33... | collective-permute-start | bytes 393224 | tf_op jit(solution)/shard_map/ppermute | solution.py:157
  174.8 20.2 %collective-permute-start.12 = (bf16[256,128]{1,0:T(8,128)(2,1)S(1)}, bf16[256,128]{1,0:T(8,128)(2,1)S(1)}, u32[]{:S(2)}, u32[]{:S(2)}) collective-permute-start(bf16[256,128]{1,0:T(8,128)(2,1)S(1)} %get-tuple-element.28), channel_id=1, source_target_pairs={{0,1},{1,2},{2,3},{3,4},{4,5},{5,6},{6,7},{7,8},{8,9},{9,10},{10,1... | collective-permute-start | bytes 196616 | tf_op jit(solution)/shard_map/ppermute | solution.py:156
  179.5 15.5 %collective-permute-start.13 = (bf16[256,128]{1,0:T(8,128)(2,1)S(1)}, bf16[256,128]{1,0:T(8,128)(2,1)S(1)}, u32[]{:S(2)}, u32[]{:S(2)}) collective-permute-start(bf16[256,128]{1,0:T(8,128)(2,1)S(1)} %get-tuple-element.29), channel_id=1, source_target_pairs={{1,0},{2,1},{3,2},{4,3},{5,4},{6,5},{7,6},{8,7},{9,8},{10,9},{11,1... | collective-permute-start | bytes 196616 | tf_op jit(solution)/shard_map/ppermute | solution.py:157
  (1 other events, 0.9 us)
where the time goes:
time: 213 us; the launch traced here: 211 us
  Pallas kernels  60.6 us (28%)
  starting transfers between devices  45.1 us (21%)
  blocking collectives  33.8 us (16%)
  local copies, waits for them, and re-layouts  32.9 us (15%)
  waiting for transfers between devices  29 us (14%)
  other arithmetic  6.7 us (3%)
  between operations  3.28 us (2%)
    pallas_call x4, Pallas kernels, row_call(): pl.pallas_call(kernel, grid=(rows // STEP_ROWS,), in_specs=[by_rows(a.sha...  35.2 us
    all_to_all x1, blocking collectives, sum_everywhere(): got = lax.all_to_all(sent, axes, split_axis=0, concat_axis=0, tiled=True)  33.8 us
    ppermute x7, starting transfers between devices, pass_on(): return lax.ppermute(cells, axis, [(i, i + 1) for i in range(ends)])  28.8 us
    ppermute x7, waiting for transfers between devices, pass_on(): return lax.ppermute(cells, axis, [(i + 1, i) for i in range(ends)])  18.9 us
    pallas_call x1, Pallas kernels, refine(): pl.pallas_call(functools.partial(affinity_kernel, full_rows=rows * lax.ax...  16.1 us
    ppermute x7, starting transfers between devices, pass_on(): return lax.ppermute(cells, axis, [(i + 1, i) for i in range(ends)])  11.1 us
    unnamed x30, local copies, waits for them, and re-layouts  11 us
    ppermute x7, waiting for transfers between devices, pass_on(): return lax.ppermute(cells, axis, [(i, i + 1) for i in range(ends)])  10.1 us
  transfers between devices with their start and end apart: 15, of which 4 were waited for; matrix products, arithmetic and copies ran while one was open for 12% of the time, Pallas kernels for 21%

commit v1 on v0

--- a/solution.py
+++ b/solution.py
@@ -20,6 +20,10 @@
 
 def vmem_of(mib):
     return pltpu.CompilerParams(vmem_limit_bytes=mib * 2**20)
+
+
+def cost_of(micros):
+    return pl.CostEstimate(flops=int(micros * 1e9), transcendentals=0, bytes_accessed=int(micros * 3e6))
 
 
 def lane_of(shape):
@@ -52,7 +56,7 @@
 
 def affinity_kernel(
     place_ref, up_ref, mid_ref, down_ref, left_ref, right_ref, current_ref, weights_ref,
-    feats, probs, next_probs, pairs, *, full_rows, full_cols, feat_channels, classes,
+    feats, probs, next_probs, pairs, squares, *, full_rows, full_cols, feat_channels, classes,
 ):
     rows = mid_ref.shape[0]
     cols = mid_ref.shape[2]
@@ -84,20 +88,28 @@
     pairs[:, tall - 8 :, :] = jnp.zeros((len(PAIR_TAPS), 8, SPAN), jnp.float32)
 
     def distances(row, carry):
-        sums = [jnp.zeros((8, SPAN), jnp.float32) for _ in PAIR_TAPS]
+        sums = [None for _ in PAIR_TAPS]
         for c in range(feat_channels // 8):
             here = feats[row, 8 * c : 8 * c + 8, :]
             there = {0: here}
             for index, (off_y, off_x) in enumerate(PAIR_TAPS):
                 if off_y not in there:
                     there[off_y] = feats[row + off_y, 8 * c : 8 * c + 8, :]
-                gap = here - shifted_by(there[off_y], off_x)
-                sums[index] += gap * gap
+                product = here * shifted_by(there[off_y], off_x)
+                sums[index] = product if c == 0 else sums[index] + product
         for index in range(len(PAIR_TAPS)):
             pairs[index, pl.ds(row, 1), :] = jnp.sum(sums[index], axis=0, keepdims=True)
         return carry
 
     lax.fori_loop(0, tall - 4, distances, 0)
+
+    def sizes(row, carry):
+        cells = feats[row]
+        squares[pl.ds(row, 1), :] = jnp.sum(cells * cells, axis=0, keepdims=True)
+        return carry
+
+    lax.fori_loop(0, tall, sizes, 0, unroll=4)
+    squares[tall:, :] = jnp.zeros((8, SPAN), jnp.float32)
 
     shape = (tall, SPAN)
     lane = lane_of(shape)
@@ -111,7 +123,9 @@
     here_inside = inside(0, 0)
     for index, (off_y, off_x) in enumerate(PAIR_TAPS):
         present = here_inside & inside(off_y, off_x)
-        pairs[index] = jnp.where(present, jnp.exp(pairs[index] * (-1.0 / feat_channels)), 0.0)
+        both = squares[:tall, :] + shifted_by(squares[off_y : off_y + tall, :], off_x)
+        distance = jnp.maximum(both - 2.0 * pairs[index], 0.0)
+        pairs[index] = jnp.where(present, jnp.exp(distance * (-1.0 / feat_channels)), 0.0)
     wide = rows + EDGE_ROWS
     total = jnp.ones((wide, SPAN), jnp.float32)
     for index, (off_y, off_x) in enumerate(PAIR_TAPS):
@@ -132,14 +146,14 @@
         middle[row] = sweep_row(lambda o: weights_ref[o, pl.ds(row, 1), :], row + 4, read_row)
         return carry
 
-    lax.fori_loop(0, rows + 8, first, 0)
+    lax.fori_loop(0, rows + 8, first, 0, unroll=4)
 
     def second(row, carry):
         value = sweep_row(lambda o: weights_ref[o, pl.ds(row + 4, 1), :], row + 4, lambda r: middle[r])
         out_ref[row] = value[:, : out_ref.shape[2]]
         return carry
 
-    lax.fori_loop(0, rows, second, 0)
+    lax.fori_loop(0, rows, second, 0, unroll=4)
 
 
 def finish_kernel(weights_ref, up_ref, mid_ref, down_ref, out_ref, probs, next_probs):
@@ -157,7 +171,7 @@
     return lax.ppermute(cells, axis, [(i + 1, i) for i in range(ends)])
 
 
-def refine(teacher_feats, teacher_probs):
+def refine(teacher_feats, teacher_probs, student):
     feat_channels, rows, cols = teacher_feats.shape
     classes = teacher_probs.shape[0]
     high = lax.reduce_precision(teacher_probs, 8, 7)
@@ -167,12 +181,16 @@
     ).transpose(1, 0, 2)
     up = pass_on(mid[rows - EDGE_ROWS :], "row", 1)
     down = pass_on(mid[:EDGE_ROWS], "row", -1)
+    student_rows = unit_rows(student)
     channels = mid.shape[1]
     groups = (rows + 2 * EDGE_ROWS) // 8
     edge = jax.ShapeDtypeStruct((groups, channels, 128), jnp.bfloat16)
-    to_left, to_right = pl.pallas_call(edges_kernel, out_shape=(edge, edge), name="edges", compiler_params=vmem_of(12))(up, mid, down)
+    to_left, to_right = pl.pallas_call(edges_kernel, out_shape=(edge, edge), name="edges", compiler_params=vmem_of(12), cost_estimate=cost_of(1))(up, mid, down)
     left = pass_on(to_right, "col", 1)
     right = pass_on(to_left, "col", -1)
+    left, right, student_left, student_right = lax.optimization_barrier(
+        (left, right) + unit_cols(student, *student_rows)
+    )
     place = jnp.stack([lax.axis_index("row") * rows, lax.axis_index("col") * cols]).astype(jnp.int32)
     tall = rows + 2 * EDGE_ROWS
     vmem = pl.BlockSpec(memory_space=pltpu.VMEM)
@@ -195,10 +213,18 @@
             pltpu.VMEM((tall, classes, SPAN), jnp.float32),
             pltpu.VMEM((rows + 8, classes, SPAN), jnp.float32),
             pltpu.VMEM((len(PAIR_TAPS), tall, SPAN), jnp.float32),
+            pltpu.VMEM((tall + 8, SPAN), jnp.float32),
         ],
         name="affinity",
         compiler_params=vmem_of(20),
+        cost_estimate=cost_of(12),
     )(place, up, mid, down, left, right)
+    return current, weights, student_rows + (student_left, student_right)
+
+
+def finish(current, weights, cols):
+    rows, classes, _ = current.shape
+    tall = rows + 2 * EDGE_ROWS
     up = pass_on(current[rows - EDGE_ROWS :], "row", 1)
     down = pass_on(current[:EDGE_ROWS], "row", -1)
     refined = pl.pallas_call(
@@ -210,6 +236,7 @@
         ],
         name="finish",
         compiler_params=vmem_of(12),
+        cost_estimate=cost_of(4),
     )(weights, up, current, down)
     return refined
 
@@ -296,12 +323,18 @@
     return jnp.dot(weights, jnp.concatenate(moved, axis=0), preferred_element_type=jnp.float32)
 
 
-def conv_start(up_ref, mid_ref, down_ref, left_ref, right_ref, weights_ref, padded, left_sum, right_sum):
+def conv_start(
+    up_ref, mid_ref, down_ref, left_ref, right_ref, taps_ref, padded, left_sum, right_sum, weights_ref, forward
+):
     rows, channels, _ = mid_ref.shape
     out = weights_ref.shape[0] // 3
 
     @pl.when(pl.program_id(0) == 0)
     def _():
+        for b in range(3):
+            for a in range(3):
+                tap = taps_ref[3 * a + b].T if forward else taps_ref[3 * (2 - a) + (2 - b)]
+                weights_ref[out * b : out * (b + 1), channels * a : channels * (a + 1)] = tap
         padded[0] = up_ref[0]
         padded[pl.ds(1, rows)] = mid_ref[...]
         padded[rows + 1] = down_ref[0]
@@ -314,11 +347,13 @@
     cols = padded.shape[2]
     stack = jnp.concatenate([padded[row], padded[row + 1], padded[row + 2]], axis=0)
     parts = jnp.dot(weights_ref[...], stack, preferred_element_type=jnp.float32)
-    lanes = lane_of((out, cols))
-    left = jnp.concatenate([pltpu.roll(left_sum[...], (128 - row) % 128, 1), jnp.zeros((out, cols - 128), jnp.float32)], axis=1)
-    right = jnp.concatenate([jnp.zeros((out, cols - 128), jnp.float32), pltpu.roll(right_sum[...], 127 - row, 1)], axis=1)
-    before = jnp.where(lanes == 0, left, pltpu.roll(parts[:out], 1, 1))
-    after = jnp.where(lanes == cols - 1, right, pltpu.roll(parts[2 * out :], cols - 1, 1))
+    lanes = lane_of((out, 128))
+    before = pltpu.roll(parts[:out], 1, 1)
+    after = pltpu.roll(parts[2 * out :], cols - 1, 1)
+    left = pltpu.roll(left_sum[...], (128 - row) % 128, 1)
+    right = pltpu.roll(right_sum[...], 127 - row, 1)
+    before = jnp.concatenate([jnp.where(lanes == 0, left, before[:, :128]), before[:, 128:]], axis=1)
+    after = jnp.concatenate([after[:, :-128], jnp.where(lanes == 127, right, after[:, -128:])], axis=1)
     return parts[out : 2 * out] + (before + after)
 
 
@@ -326,15 +361,18 @@
 
 
 def forward_kernel(
-    up_ref, mid_ref, down_ref, left_ref, right_ref, weights_ref, class_ref,
-    slope_ref, hidden_ref, guess_ref, padded, left_sum, right_sum,
+    up_ref, mid_ref, down_ref, left_ref, right_ref, taps_ref, class_ref,
+    slope_ref, hidden_ref, guess_ref, padded, left_sum, right_sum, weights_ref,
 ):
-    conv_start(up_ref, mid_ref, down_ref, left_ref, right_ref, weights_ref, padded, left_sum, right_sum)
+    conv_start(
+        up_ref, mid_ref, down_ref, left_ref, right_ref, taps_ref, padded, left_sum, right_sum, weights_ref, True
+    )
     for k in range(STEP_ROWS):
         pre_act = conv_row(pl.program_id(0) * STEP_ROWS + k, weights_ref, padded, left_sum, right_sum)
-        logistic = jax.nn.sigmoid(pre_act)
-        slope_ref[k] = logistic * (1.0 + pre_act * (1.0 - logistic))
-        hidden = (pre_act * logistic).astype(jnp.bfloat16)
+        logistic = 0.5 * jnp.tanh(0.5 * pre_act) + 0.5
+        silu = pre_act * logistic
+        slope_ref[k] = logistic + silu * (1.0 - logistic)
+        hidden = silu.astype(jnp.bfloat16)
         hidden_ref[k] = hidden
         logit = jnp.dot(class_ref[...], hidden, preferred_element_type=jnp.float32)
         guess_ref[k] = jax.nn.sigmoid(logit)
@@ -403,9 +441,11 @@
 
 
 def feature_kernel(
-    up_ref, mid_ref, down_ref, left_ref, right_ref, weights_ref, out_ref, padded, left_sum, right_sum
+    up_ref, mid_ref, down_ref, left_ref, right_ref, taps_ref, out_ref, padded, left_sum, right_sum, weights_ref
 ):
-    conv_start(up_ref, mid_ref, down_ref, left_ref, right_ref, weights_ref, padded, left_sum, right_sum)
+    conv_start(
+        up_ref, mid_ref, down_ref, left_ref, right_ref, taps_ref, padded, left_sum, right_sum, weights_ref, False
+    )
     for k in range(STEP_ROWS):
         row = pl.program_id(0) * STEP_ROWS + k
         out_ref[k] = conv_row(row, weights_ref, padded, left_sum, right_sum).astype(out_ref.dtype)
@@ -428,6 +468,7 @@
     to_left, to_right = pl.pallas_call(
         unit_edges_kernel, out_shape=(edge, edge), name="unit_edges",
         compiler_params=vmem_of(16),
+        cost_estimate=cost_of(1),
     )(up, cells, down)
     return pass_on(to_right, "col", 1), pass_on(to_left, "col", -1)
 
@@ -437,10 +478,11 @@
         pltpu.VMEM((rows + 2, channels, cols), jnp.bfloat16),
         pltpu.VMEM((out, 128), jnp.float32),
         pltpu.VMEM((out, 128), jnp.float32),
+        pltpu.VMEM((3 * out, 3 * channels), jnp.bfloat16),
     ]
 
 
-def row_call(kernel, name, rows, args, arg_rows, outs, out_rows, scratch, vmem):
+def row_call(kernel, name, rows, args, arg_rows, outs, out_rows, scratch, vmem, micros):
     return pl.pallas_call(
         kernel,
         grid=(rows // STEP_ROWS,),
@@ -450,6 +492,7 @@
         scratch_shapes=scratch,
         name=name,
         compiler_params=vmem_of(vmem),
+        cost_estimate=cost_of(micros),
     )(*args)
 
 
@@ -457,32 +500,28 @@
     channels, rows, cols = student_feats.shape
     hidden_size, classes = class_weight.shape
     pixel_count = float(rows * cols)
-    taps = conv_weight.reshape(3, 3, channels, hidden_size)
-    forward_weight = taps.transpose(1, 3, 0, 2).reshape(3 * hidden_size, 3 * channels)
-    back_weight = taps[::-1, ::-1].transpose(1, 2, 0, 3).reshape(3 * channels, 3 * hidden_size)
     student = student_feats.transpose(1, 0, 2)
-    student_up, student_down = unit_rows(student)
-    student_left, student_right = unit_cols(student, student_up, student_down)
-    halo = (student_up, student, student_down, student_left, student_right)
+    current, weights, student_halo = refine(teacher_feats, teacher_probs, student)
+    halo = (student_halo[0], student, student_halo[1]) + student_halo[2:]
     f32, bf16 = jnp.float32, jnp.bfloat16
     slope, hidden, guess = row_call(
         forward_kernel, "forward", rows,
-        halo + (forward_weight, class_weight.T), [False] * 7,
+        halo + (conv_weight, class_weight.T), [False] * 7,
         [
             jax.ShapeDtypeStruct((rows, hidden_size, cols), f32),
             jax.ShapeDtypeStruct((rows, hidden_size, cols), bf16),
             jax.ShapeDtypeStruct((rows, classes, cols), f32),
         ],
-        [True] * 3, conv_scratch(rows, channels, cols, hidden_size), 32,
-    )
-    refined = refine(teacher_feats, teacher_probs)
+        [True] * 3, conv_scratch(rows, channels, cols, hidden_size), 32, 12,
+    )
+    refined = finish(current, weights, cols)
     back, error = row_call(
         back_kernel, "back", rows, (guess, refined, slope, class_weight), [True, True, True, False],
         [
             jax.ShapeDtypeStruct((rows, hidden_size, cols), bf16),
             jax.ShapeDtypeStruct((rows, classes, cols), bf16),
         ],
-        [True] * 2, [], 16,
+        [True] * 2, [], 16, 2,
     )
     back_up, back_down = unit_rows(back)
     conv_part, class_part = row_call(
@@ -492,14 +531,16 @@
             jax.ShapeDtypeStruct((hidden_size, classes), f32),
         ],
         [False] * 2,
-        [pltpu.VMEM((rows + 2, channels, cols), bf16)] + [pltpu.VMEM((hidden_size, 128), f32)] * 2, 40,
-    )
-    back_left, back_right = unit_cols(back, back_up, back_down)
+        [pltpu.VMEM((rows + 2, channels, cols), bf16)] + [pltpu.VMEM((hidden_size, 128), f32)] * 2, 40, 9,
+    )
+    back_left, back_right, conv_part, class_part = lax.optimization_barrier(
+        unit_cols(back, back_up, back_down) + (conv_part, class_part)
+    )
     (feature_grad,) = row_call(
         feature_kernel, "feature", rows,
-        (back_up, back, back_down, back_left, back_right, back_weight), [False] * 6,
+        (back_up, back, back_down, back_left, back_right, conv_weight), [False] * 6,
         [jax.ShapeDtypeStruct((rows, channels, cols), bf16)],
-        [True], conv_scratch(rows, hidden_size, cols, channels), 32,
+        [True], conv_scratch(rows, hidden_size, cols, channels), 32, 8,
     )
     summed_conv, summed_class = sum_everywhere(conv_part, class_part, ("row", "col"))
     grad_conv = summed_conv / pixel_count

time: 213 us -> 193 us (0.906)
  local copies, waits for them, and re-layouts: 32.9 us -> 15.1 us
  Pallas kernels: 60.6 us -> 55.4 us
  starting transfers between devices: 45.1 us -> 47.6 us
    ppermute x7, waiting for transfers between devices: 10.1 us -> 0.96 us  [pass_on(): return lax.ppermute(cells, axis, [(i, i + 1) for i in range(ends)])]
    rev x1 -> x0, local copies, waits for them, and re-layouts: 8.98 us -> none  [shards(): taps[::-1, ::-1].transpose(1, 2, 0, 3)]
    all_to_all x1, waiting for transfers between devices: 0.01 us -> 8.03 us  [sum_everywhere(): lax.all_to_all(spread, axes, split_axis=0, concat_axis=0, tiled=True)]
    reshape x2 -> x0, local copies, waits for them, and re-layouts: 5.75 us -> none  [shards(): taps = conv_weight.reshape(3, 3, channels, hidden_size)]
    ppermute x7, waiting for transfers between devices: 18.9 us -> 22 us  [pass_on(): return lax.ppermute(cells, axis, [(i + 1, i) for i in range(ends)])]
    pallas_call x1, Pallas kernels: 6.05 us -> 3.04 us  [finish(): pl.pallas_call(finish_kernel, out_shape=jax.ShapeDtypeStruct((rows, class...]
    ppermute x7, starting transfers between devices: 28.8 us -> 31.3 us  [pass_on(): return lax.ppermute(cells, axis, [(i, i + 1) for i in range(ends)])]
    unnamed x30 -> x36, local copies, waits for them, and re-layouts: 11 us -> 8.7 us
  transfers between devices with their start and end apart: 15 -> 15, of which waited for: 4 -> 6; matrix products, arithmetic and copies ran while one was open for 12% -> 3% of each run, Pallas kernels for 21% -> 19%
where the time goes in v1:
time: 193 us; the launch traced here: 192 us
  Pallas kernels  55.4 us (29%)
  starting transfers between devices  47.6 us (25%)
  blocking collectives  33 us (17%)
  waiting for transfers between devices  31 us (16%)
  local copies, waits for them, and re-layouts  15.1 us (8%)
  other arithmetic  6.7 us (3%)
  between operations  3.28 us (2%)
    pallas_call x4, Pallas kernels, row_call(): pl.pallas_call(kernel, grid=(rows // STEP_ROWS,), in_specs=[by_rows(a.sha...  35.4 us
    all_to_all x1, blocking collectives, sum_everywhere(): got = lax.all_to_all(sent, axes, split_axis=0, concat_axis=0, tiled=True)  33 us
    ppermute x7, starting transfers between devices, pass_on(): return lax.ppermute(cells, axis, [(i, i + 1) for i in range(ends)])  31.3 us
    ppermute x7, waiting for transfers between devices, pass_on(): return lax.ppermute(cells, axis, [(i + 1, i) for i in range(ends)])  22 us
    pallas_call x1, Pallas kernels, refine(): pl.pallas_call(functools.partial(affinity_kernel, full_rows=rows * lax.ax...  14.3 us
    ppermute x7, starting transfers between devices, pass_on(): return lax.ppermute(cells, axis, [(i + 1, i) for i in range(ends)])  10.9 us
    unnamed x36, local copies, waits for them, and re-layouts  8.7 us
    all_to_all x1, waiting for transfers between devices, sum_everywhere(): lax.all_to_all(spread, axes, split_axis=0, concat_axis=0, tiled=True)  8.03 us
  transfers between devices with their start and end apart: 15, of which 6 were waited for; matrix products, arithmetic and copies ran while one was open for 3% of the time, Pallas kernels for 19%

profile of v1, /device:TPU:1, one launch (start us, length us, event | category | flops | bytes accessed | tf_op | source)
XLA Modules:
  0.0 192.1 jit_solution(17513219009805812095)
XLA Ops:
  3.9 3.9 %collective-permute-start = (bf16[8,80,256]{2,1,0:T(8,128)(2,1)}, bf16[8,80,256]{2,1,0:T(8,128)(2,1)S(1)}, u32[]{:S(2)}, u32[]{:S(2)}) collective-permute-start(bf16[8,80,256]{2,1,0:T(8,128)(2,1)} %get-tuple-element.75), channel_id=1, source_target_pairs={{0,16},{16,32},{32,48},{48,64},{64,80},{80,96},{96,112},{1,17},{17... | collective-permute-start | bytes 983048 | tf_op jit(solution)/shard_map/ppermute | solution.py:170
  10.6 4.6 %collective-permute-start.4 = (bf16[1,256,256]{2,1,0:T(8,128)(2,1)}, bf16[1,256,256]{2,1,0:T(8,128)(2,1)}, u32[]{:S(2)}, u32[]{:S(2)}) collective-permute-start(bf16[1,256,256]{2,1,0:T(8,128)(2,1)} %get-tuple-element.73), channel_id=1, source_target_pairs={{0,16},{16,32},{32,48},{48,64},{64,80},{80,96},{96,112},{1,17},{17... | collective-permute-start | bytes 393224 | tf_op jit(solution)/shard_map/ppermute | solution.py:170
  17.1 12.1 %collective-permute-done.5.down_ref = bf16[1,256,256]{2,1,0:T(8,128)(2,1)} collective-permute-done((bf16[1,256,256]{2,1,0:T(8,128)(2,1)}, bf16[1,256,256]{2,1,0:T(8,128)(2,1)}, u32[]{:S(2)}, u32[]{:S(2)}) %collective-permute-start.5) | collective-permute-done | bytes 131104 | tf_op jit(solution)/shard_map/ppermute | solution.py:171
  30.8 6.1 %collective-permute-start.6 = (bf16[256,128]{1,0:T(8,128)(2,1)S(1)}, bf16[256,128]{1,0:T(8,128)(2,1)S(1)}, u32[]{:S(2)}, u32[]{:S(2)}) collective-permute-start(bf16[256,128]{1,0:T(8,128)(2,1)S(1)} %get-tuple-element.29), channel_id=1, source_target_pairs={{0,1},{1,2},{2,3},{3,4},{4,5},{5,6},{6,7},{7,8},{8,9},{9,10},{10,1... | collective-permute-start | bytes 196616 | tf_op jit(solution)/shard_map/ppermute | solution.py:170
  36.9 1.9 collective-permute-start.7
  39.2 5.1 %collective-permute-start.2 = (bf16[4,80,128]{2,1,0:T(8,128)(2,1)S(1)}, bf16[4,80,128]{2,1,0:T(8,128)(2,1)S(1)}, u32[]{:S(2)}, u32[]{:S(2)}) collective-permute-start(bf16[4,80,128]{2,1,0:T(8,128)(2,1)S(1)} %get-tuple-element.27), channel_id=1, source_target_pairs={{0,1},{1,2},{2,3},{3,4},{4,5},{5,6},{6,7},{7,8},{8,9},{9,10},{10,1... | collective-permute-start | bytes 245768 | tf_op jit(solution)/shard_map/ppermute | solution.py:170
  44.4 1.9 collective-permute-start.3
  46.4 5.2 %collective-permute-done.3.right_ref = bf16[4,80,128]{2,1,0:T(8,128)(2,1)S(1)} collective-permute-done((bf16[4,80,128]{2,1,0:T(8,128)(2,1)S(1)}, bf16[4,80,128]{2,1,0:T(8,128)(2,1)S(1)}, u32[]{:S(2)}, u32[]{:S(2)}) %collective-permute-start.3) | collective-permute-done | bytes 81952 | tf_op jit(solution)/shard_map/ppermute | solution.py:171
  51.6 14.3 %affinity.1 = (f32[16,8,384]{2,1,0:T(8,128)S(1)}, f32[25,24,384]{2,1,0:T(8,128)S(1)}) custom-call(s32[2]{0:T(128)S(1)} %pad_add_fusion.place_ref, bf16[8,80,256]{2,1,0:T(8,128)(2,1)S(1)} %collective-permute-done.up_ref, bf16[16,80,256]{2,1,0:T(8,128)(2,1)S(1)} %maximum_bitcast_fusion.mid_ref, bf16[8,80,256]{2,1,0:T(8,128)(2,1)S(1)} %collective-permute-done.1.down_ref, ...), custom_call_target="tpu_custom_call" | custom-call | flops 12000000000 | bytes 36000000 | tf_op jit(solution)/shard_map/affinity/pallas_call | solution.py:197
  66.0 2.2 %collective-permute-start.8 = (f32[8,8,384]{2,1,0:T(8,128)S(1)}, f32[8,8,384]{2,1,0:T(8,128)S(1)}, u32[]{:S(2)}, u32[]{:S(2)}) collective-permute-start(f32[8,8,384]{2,1,0:T(8,128)S(1)} %get-tuple-element.77), channel_id=1, source_target_pairs={{0,16},{16,32},{32,48},{48,64},{64,80},{80,96},{96,112},{1,17},{17... | collective-permute-start | bytes 294920 | tf_op jit(solution)/shard_map/ppermute | solution.py:170
  69.5 16.5 %forward.1 = (f32[16,256,256]{2,1,0:T(8,128)S(1)}, bf16[16,256,256]{2,1,0:T(8,128)(2,1)S(1)}, f32[16,8,256]{2,1,0:T(8,128)S(1)}) custom-call(bf16[1,256,256]{2,1,0:T(8,128)(2,1)} %collective-permute-done.4.up_ref, bf16[16,256,256]{2,1,0:T(8,128)(2,1)S(1)} %bitcast.34, bf16[1,256,256]{2,1,0:T(8,128)(2,1)} %collective-permute-done.5.down_ref, ...), custom_call_target="tpu_custom_call" | custom-call | flops 12000000000 | bytes 36000000 | tf_op jit(solution)/shard_map/forward/pallas_call | solution.py:486
  86.1 3.0 %finish.1.refined_ref = f32[16,8,256]{2,1,0:T(8,128)S(1)} custom-call(f32[25,24,384]{2,1,0:T(8,128)S(1)} %get-tuple-element.33.weights_ref, f32[8,8,384]{2,1,0:T(8,128)S(1)} %collective-permute-done.8.up_ref, f32[16,8,384]{2,1,0:T(8,128)S(1)} %get-tuple-element.34.mid_ref, f32[8,8,384]{2,1,0:T(8,128)S(1)} %collective-permute-done.9.down_ref), custom_call_target="tpu_custom_call" | custom-call | flops 4000000000 | bytes 12000000 | tf_op jit(solution)/shard_map/finish/pallas_call | solution.py:230
  89.2 1.7 back.1
  90.9 4.7 %collective-permute-start.10 = (bf16[1,256,256]{2,1,0:T(8,128)(2,1)S(1)}, bf16[1,256,256]{2,1,0:T(8,128)(2,1)S(1)}, u32[]{:S(2)}, u32[]{:S(2)}) collective-permute-start(bf16[1,256,256]{2,1,0:T(8,128)(2,1)S(1)} %get-tuple-element.71), channel_id=1, source_target_pairs={{0,16},{16,32},{32,48},{48,64},{64,80},{80,96},{96,112},{1,17},{17... | collective-permute-start | bytes 393224 | tf_op jit(solution)/shard_map/ppermute | solution.py:170
  97.5 4.7 %collective-permute-done.11.down_ref = bf16[1,256,256]{2,1,0:T(8,128)(2,1)S(1)} collective-permute-done((bf16[1,256,256]{2,1,0:T(8,128)(2,1)S(1)}, bf16[1,256,256]{2,1,0:T(8,128)(2,1)S(1)}, u32[]{:S(2)}, u32[]{:S(2)}) %collective-permute-start.11) | collective-permute-done | bytes 131104 | tf_op jit(solution)/shard_map/ppermute | solution.py:171
  102.9 4.6 %collective-permute-start.12 = (bf16[256,128]{1,0:T(8,128)(2,1)S(1)}, bf16[256,128]{1,0:T(8,128)(2,1)S(1)}, u32[]{:S(2)}, u32[]{:S(2)}) collective-permute-start(bf16[256,128]{1,0:T(8,128)(2,1)S(1)} %get-tuple-element.40), channel_id=1, source_target_pairs={{0,1},{1,2},{2,3},{3,4},{4,5},{5,6},{6,7},{7,8},{8,9},{9,10},{10,1... | collective-permute-start | bytes 196616 | tf_op jit(solution)/shard_map/ppermute | solution.py:170
  107.5 1.9 collective-permute-start.13
  109.5 9.2 %grads.1 = (f32[768,768]{1,0:T(8,128)S(1)}, f32[256,8]{1,0:T(8,128)S(1)}) custom-call(bf16[1,256,256]{2,1,0:T(8,128)(2,1)} %collective-permute-done.4.up_ref, bf16[16,256,256]{2,1,0:T(8,128)(2,1)S(1)} %bitcast.35, bf16[1,256,256]{2,1,0:T(8,128)(2,1)} %collective-permute-done.5.down_ref, bf16[256,128]{1,0:T(8,128)(2,1)S(1)} %collective-permute-done.6.left_ref, ...), custom_call_target="tpu_custom_call" | custom-call | flops 8999999488 | bytes 27000000 | tf_op jit(solution)/shard_map/grads/pallas_call | solution.py:486
  122.7 33.0 %all_to_all.10 = f16[128,40,128]{2,1,0:T(8,128)(2,1)S(1)} all-to-all(f16[128,40,128]{2,1,0:T(8,128)(2,1)S(1)} %maximum_maximum_fusion), channel_id=1, replica_groups=mesh['row'=8,'col'=16] {'row','col'}, dimensions={0} | all-to-all | bytes 2621440 | tf_op jit(solution)/shard_map/all_to_all | solution.py:297
  159.1 5.3 %all-to-all-start.1 = ((f16[128,40,128]{2,1,0:T(8,128)(2,1)}), f16[128,40,128]{2,1,0:T(8,128)(2,1)}, u32[]{:S(2)}, u32[]{:S(2)}) async-start(f16[128,40,128]{2,1,0:T(8,128)(2,1)} %broadcast_in_dim.26), calls=%async_computation.1 | async-start | bytes 2621440 | tf_op jit(solution)/shard_map/all_to_all | solution.py:301
  167.7 7.9 %feature.1 = bf16[16,256,256]{2,1,0:T(8,128)(2,1)S(1)} custom-call(bf16[1,256,256]{2,1,0:T(8,128)(2,1)S(1)} %copy-done.6, bf16[16,256,256]{2,1,0:T(8,128)(2,1)S(1)} %copy-done.1, bf16[1,256,256]{2,1,0:T(8,128)(2,1)S(1)} %copy-done.8, bf16[256,128]{1,0:T(8,128)(2,1)S(1)} %copy-done.10, bf16[256,128]{1,0:T(8,128)(2,1)S(1)} %copy-done.12, ...), custom_call_target="tpu_custom_call" | custom-call | flops 8000000000 | bytes 24000000 | tf_op jit(solution)/shard_map/feature/pallas_call | solution.py:486
  175.6 2.5 %copy.58 = bf16[256,16,256]{2,1,0:T(8,128)(2,1)} copy(bf16[256,16,256]{2,0,1:T(8,128)(2,1)S(1)} %bitcast.36) | data formatting | bytes 4194304
  178.1 8.0 %all-to-all-done.1 = f16[128,40,128]{2,1,0:T(8,128)(2,1)} async-done(((f16[128,40,128]{2,1,0:T(8,128)(2,1)}), f16[128,40,128]{2,1,0:T(8,128)(2,1)}, u32[]{:S(2)}, u32[]{:S(2)}) %all-to-all-start.1) | async-done | bytes 1310752 | tf_op jit(solution)/shard_map/all_to_all | solution.py:301
  187.3 1.7 convert_multiply_fusion
  (87 shorter events, 26.5 us)
Async XLA Ops:
  0.6 8.5 %copy-start.13 = (bf16[256,16,256]{2,1,0:T(8,128)(2,1)S(1)}, bf16[256,16,256]{2,1,0:T(8,128)(2,1)}, u32[]{:S(2)}) copy-start(bf16[256,16,256]{2,1,0:T(8,128)(2,1)} %param.7) | copy-start | bytes 6291460
  3.9 34.9 %collective-permute-start = (bf16[8,80,256]{2,1,0:T(8,128)(2,1)}, bf16[8,80,256]{2,1,0:T(8,128)(2,1)S(1)}, u32[]{:S(2)}, u32[]{:S(2)}) collective-permute-start(bf16[8,80,256]{2,1,0:T(8,128)(2,1)} %get-tuple-element.75), channel_id=1, source_target_pairs={{0,16},{16,32},{32,48},{48,64},{64,80},{80,96},{96,112},{1,17},{17... | collective-permute-start | bytes 983048 | tf_op jit(solution)/shard_map/ppermute | solution.py:170
  7.9 8.7 %copy-start.2 = (bf16[256,8]{0,1:T(8,128)(2,1)S(1)}, bf16[256,8]{0,1:T(8,128)(2,1)}, u32[]{:S(2)}) copy-start(bf16[256,8]{0,1:T(8,128)(2,1)} %param.9) | copy-start | bytes 12292
  7.9 31.0 %collective-permute-start.1 = (bf16[8,80,256]{2,1,0:T(8,128)(2,1)}, bf16[8,80,256]{2,1,0:T(8,128)(2,1)S(1)}, u32[]{:S(2)}, u32[]{:S(2)}) collective-permute-start(bf16[8,80,256]{2,1,0:T(8,128)(2,1)} %get-tuple-element.74), channel_id=1, source_target_pairs={{16,0},{32,16},{48,32},{64,48},{80,64},{96,80},{112,96},{17,1},{33... | collective-permute-start | bytes 983048 | tf_op jit(solution)/shard_map/ppermute | solution.py:171
  10.6 6.5 %collective-permute-start.4 = (bf16[1,256,256]{2,1,0:T(8,128)(2,1)}, bf16[1,256,256]{2,1,0:T(8,128)(2,1)}, u32[]{:S(2)}, u32[]{:S(2)}) collective-permute-start(bf16[1,256,256]{2,1,0:T(8,128)(2,1)} %get-tuple-element.73), channel_id=1, source_target_pairs={{0,16},{16,32},{32,48},{48,64},{64,80},{80,96},{96,112},{1,17},{17... | collective-permute-start | bytes 393224 | tf_op jit(solution)/shard_map/ppermute | solution.py:170
  15.2 13.9 %collective-permute-start.5 = (bf16[1,256,256]{2,1,0:T(8,128)(2,1)}, bf16[1,256,256]{2,1,0:T(8,128)(2,1)}, u32[]{:S(2)}, u32[]{:S(2)}) collective-permute-start(bf16[1,256,256]{2,1,0:T(8,128)(2,1)} %get-tuple-element.72), channel_id=1, source_target_pairs={{16,0},{32,16},{48,32},{64,48},{80,64},{96,80},{112,96},{17,1},{33... | collective-permute-start | bytes 393224 | tf_op jit(solution)/shard_map/ppermute | solution.py:171
  30.8 15.6 %collective-permute-start.6 = (bf16[256,128]{1,0:T(8,128)(2,1)S(1)}, bf16[256,128]{1,0:T(8,128)(2,1)S(1)}, u32[]{:S(2)}, u32[]{:S(2)}) collective-permute-start(bf16[256,128]{1,0:T(8,128)(2,1)S(1)} %get-tuple-element.29), channel_id=1, source_target_pairs={{0,1},{1,2},{2,3},{3,4},{4,5},{5,6},{6,7},{7,8},{8,9},{9,10},{10,1... | collective-permute-start | bytes 196616 | tf_op jit(solution)/shard_map/ppermute | solution.py:170
  36.9 9.5 %collective-permute-start.7 = (bf16[256,128]{1,0:T(8,128)(2,1)S(1)}, bf16[256,128]{1,0:T(8,128)(2,1)S(1)}, u32[]{:S(2)}, u32[]{:S(2)}) collective-permute-start(bf16[256,128]{1,0:T(8,128)(2,1)S(1)} %get-tuple-element.30), channel_id=1, source_target_pairs={{1,0},{2,1},{3,2},{4,3},{5,4},{6,5},{7,6},{8,7},{9,8},{10,9},{11,1... | collective-permute-start | bytes 196616 | tf_op jit(solution)/shard_map/ppermute | solution.py:171
  39.2 7.2 %collective-permute-start.2 = (bf16[4,80,128]{2,1,0:T(8,128)(2,1)S(1)}, bf16[4,80,128]{2,1,0:T(8,128)(2,1)S(1)}, u32[]{:S(2)}, u32[]{:S(2)}) collective-permute-start(bf16[4,80,128]{2,1,0:T(8,128)(2,1)S(1)} %get-tuple-element.27), channel_id=1, source_target_pairs={{0,1},{1,2},{2,3},{3,4},{4,5},{5,6},{6,7},{7,8},{8,9},{9,10},{10,1... | collective-permute-start | bytes 245768 | tf_op jit(solution)/shard_map/ppermute | solution.py:170
  44.4 7.3 %collective-permute-start.3 = (bf16[4,80,128]{2,1,0:T(8,128)(2,1)S(1)}, bf16[4,80,128]{2,1,0:T(8,128)(2,1)S(1)}, u32[]{:S(2)}, u32[]{:S(2)}) collective-permute-start(bf16[4,80,128]{2,1,0:T(8,128)(2,1)S(1)} %get-tuple-element.28), channel_id=1, source_target_pairs={{1,0},{2,1},{3,2},{4,3},{5,4},{6,5},{7,6},{8,7},{9,8},{10,9},{11,1... | collective-permute-start | bytes 245768 | tf_op jit(solution)/shard_map/ppermute | solution.py:171
  46.4 23.1 %copy-start.3 = (bf16[9,256,256]{2,1,0:T(8,128)(2,1)S(1)}, bf16[9,256,256]{2,1,0:T(8,128)(2,1)}, u32[]{:S(2)}) copy-start(bf16[9,256,256]{2,1,0:T(8,128)(2,1)} %taps_ref.3) | copy-start | bytes 3538948
  66.0 20.1 %collective-permute-start.8 = (f32[8,8,384]{2,1,0:T(8,128)S(1)}, f32[8,8,384]{2,1,0:T(8,128)S(1)}, u32[]{:S(2)}, u32[]{:S(2)}) collective-permute-start(f32[8,8,384]{2,1,0:T(8,128)S(1)} %get-tuple-element.77), channel_id=1, source_target_pairs={{0,16},{16,32},{32,48},{48,64},{64,80},{80,96},{96,112},{1,17},{17... | collective-permute-start | bytes 294920 | tf_op jit(solution)/shard_map/ppermute | solution.py:170
  68.2 17.9 %collective-permute-start.9 = (f32[8,8,384]{2,1,0:T(8,128)S(1)}, f32[8,8,384]{2,1,0:T(8,128)S(1)}, u32[]{:S(2)}, u32[]{:S(2)}) collective-permute-start(f32[8,8,384]{2,1,0:T(8,128)S(1)} %get-tuple-element.76), channel_id=1, source_target_pairs={{16,0},{32,16},{48,32},{64,48},{80,64},{96,80},{112,96},{17,1},{33... | collective-permute-start | bytes 294920 | tf_op jit(solution)/shard_map/ppermute | solution.py:171
  90.9 18.6 %copy-start = (bf16[16,256,256]{2,1,0:T(8,128)(2,1)}, bf16[16,256,256]{2,1,0:T(8,128)(2,1)S(1)}, u32[]{:S(2)}) copy-start(bf16[16,256,256]{2,1,0:T(8,128)(2,1)S(1)} %get-tuple-element.39.mid_ref.back_ref) | copy-start | bytes 6291460
  90.9 6.6 %collective-permute-start.10 = (bf16[1,256,256]{2,1,0:T(8,128)(2,1)S(1)}, bf16[1,256,256]{2,1,0:T(8,128)(2,1)S(1)}, u32[]{:S(2)}, u32[]{:S(2)}) collective-permute-start(bf16[1,256,256]{2,1,0:T(8,128)(2,1)S(1)} %get-tuple-element.71), channel_id=1, source_target_pairs={{0,16},{16,32},{32,48},{48,64},{64,80},{80,96},{96,112},{1,17},{17... | collective-permute-start | bytes 393224 | tf_op jit(solution)/shard_map/ppermute | solution.py:170
  95.6 6.6 %collective-permute-start.11 = (bf16[1,256,256]{2,1,0:T(8,128)(2,1)S(1)}, bf16[1,256,256]{2,1,0:T(8,128)(2,1)S(1)}, u32[]{:S(2)}, u32[]{:S(2)}) collective-permute-start(bf16[1,256,256]{2,1,0:T(8,128)(2,1)S(1)} %get-tuple-element.70), channel_id=1, source_target_pairs={{16,0},{32,16},{48,32},{64,48},{80,64},{96,80},{112,96},{17,1},{33... | collective-permute-start | bytes 393224 | tf_op jit(solution)/shard_map/ppermute | solution.py:171
  97.5 11.9 %copy-start.5 = (bf16[1,256,256]{2,1,0:T(8,128)(2,1)}, bf16[1,256,256]{2,1,0:T(8,128)(2,1)S(1)}, u32[]{:S(2)}) copy-start(bf16[1,256,256]{2,1,0:T(8,128)(2,1)S(1)} %collective-permute-done.10.up_ref) | copy-start | bytes 393220
  102.2 7.2 %copy-start.7 = (bf16[1,256,256]{2,1,0:T(8,128)(2,1)}, bf16[1,256,256]{2,1,0:T(8,128)(2,1)S(1)}, u32[]{:S(2)}) copy-start(bf16[1,256,256]{2,1,0:T(8,128)(2,1)S(1)} %collective-permute-done.11.down_ref) | copy-start | bytes 393220
  102.9 15.8 %collective-permute-start.12 = (bf16[256,128]{1,0:T(8,128)(2,1)S(1)}, bf16[256,128]{1,0:T(8,128)(2,1)S(1)}, u32[]{:S(2)}, u32[]{:S(2)}) collective-permute-start(bf16[256,128]{1,0:T(8,128)(2,1)S(1)} %get-tuple-element.40), channel_id=1, source_target_pairs={{0,1},{1,2},{2,3},{3,4},{4,5},{5,6},{6,7},{7,8},{8,9},{9,10},{10,1... | collective-permute-start | bytes 196616 | tf_op jit(solution)/shard_map/ppermute | solution.py:170
  107.5 11.2 %collective-permute-start.13 = (bf16[256,128]{1,0:T(8,128)(2,1)S(1)}, bf16[256,128]{1,0:T(8,128)(2,1)S(1)}, u32[]{:S(2)}, u32[]{:S(2)}) collective-permute-start(bf16[256,128]{1,0:T(8,128)(2,1)S(1)} %get-tuple-element.41), channel_id=1, source_target_pairs={{1,0},{2,1},{3,2},{4,3},{5,4},{6,5},{7,6},{8,7},{9,8},{10,9},{11,1... | collective-permute-start | bytes 196616 | tf_op jit(solution)/shard_map/ppermute | solution.py:171
  157.8 7.3 %copy-start.1 = (bf16[16,256,256]{2,1,0:T(8,128)(2,1)S(1)}, bf16[16,256,256]{2,1,0:T(8,128)(2,1)}, u32[]{:S(2)}) copy-start(bf16[16,256,256]{2,1,0:T(8,128)(2,1)} %copy-done) | copy-start | bytes 6291460
  157.8 7.3 %copy-start.4 = (bf16[9,256,256]{2,1,0:T(8,128)(2,1)S(1)}, bf16[9,256,256]{2,1,0:T(8,128)(2,1)}, u32[]{:S(2)}) copy-start(bf16[9,256,256]{2,1,0:T(8,128)(2,1)} %taps_ref.3) | copy-start | bytes 3538948
  157.8 7.3 %copy-start.6 = (bf16[1,256,256]{2,1,0:T(8,128)(2,1)S(1)}, bf16[1,256,256]{2,1,0:T(8,128)(2,1)}, u32[]{:S(2)}) copy-start(bf16[1,256,256]{2,1,0:T(8,128)(2,1)} %copy-done.5) | copy-start | bytes 393220
  159.1 27.1 %all-to-all-start.1 = ((f16[128,40,128]{2,1,0:T(8,128)(2,1)}), f16[128,40,128]{2,1,0:T(8,128)(2,1)}, u32[]{:S(2)}, u32[]{:S(2)}) async-start(f16[128,40,128]{2,1,0:T(8,128)(2,1)} %broadcast_in_dim.26), calls=%async_computation.1 | async-start | bytes 2621440 | tf_op jit(solution)/shard_map/all_to_all | solution.py:301
  (5 other events, 4.4 us)

commit v2 on v1

--- a/solution.py
+++ b/solution.py
@@ -1,10 +1,12 @@
 import functools
+import math
 
 import jax
 import jax.numpy as jnp
 from jax import lax
 from jax.experimental import pallas as pl
 from jax.experimental.pallas import tpu as pltpu
+from jax.sharding import Mesh
 from jax.sharding import PartitionSpec as P
 
 
@@ -164,41 +166,46 @@
     two_sweeps(weights_ref, lambda row: probs[row], next_probs, out_ref, rows)
 
 
+COL = ("pair", "core")
+
+
+def size_of(axes):
+    return math.prod(lax.axis_size(a) for a in axes) if isinstance(axes, tuple) else lax.axis_size(axes)
+
+
 def pass_on(cells, axis, step):
-    ends = lax.axis_size(axis) - 1
+    ends = size_of(axis) - 1
     if step > 0:
         return lax.ppermute(cells, axis, [(i, i + 1) for i in range(ends)])
     return lax.ppermute(cells, axis, [(i + 1, i) for i in range(ends)])
 
 
-def refine(teacher_feats, teacher_probs, student):
-    feat_channels, rows, cols = teacher_feats.shape
-    classes = teacher_probs.shape[0]
+def teacher_rows(teacher_feats, teacher_probs):
+    rows = teacher_feats.shape[1]
     high = lax.reduce_precision(teacher_probs, 8, 7)
     low = teacher_probs - high
     mid = jnp.concatenate(
         [teacher_feats, high.astype(jnp.bfloat16), low.astype(jnp.bfloat16)], axis=0
     ).transpose(1, 0, 2)
-    up = pass_on(mid[rows - EDGE_ROWS :], "row", 1)
-    down = pass_on(mid[:EDGE_ROWS], "row", -1)
-    student_rows = unit_rows(student)
+    return mid, pass_on(mid[rows - EDGE_ROWS :], "row", 1), pass_on(mid[:EDGE_ROWS], "row", -1)
+
+
+def refine(mid, up, down, feat_channels, classes):
+    rows, _, cols = mid.shape
     channels = mid.shape[1]
     groups = (rows + 2 * EDGE_ROWS) // 8
     edge = jax.ShapeDtypeStruct((groups, channels, 128), jnp.bfloat16)
     to_left, to_right = pl.pallas_call(edges_kernel, out_shape=(edge, edge), name="edges", compiler_params=vmem_of(12), cost_estimate=cost_of(1))(up, mid, down)
-    left = pass_on(to_right, "col", 1)
-    right = pass_on(to_left, "col", -1)
-    left, right, student_left, student_right = lax.optimization_barrier(
-        (left, right) + unit_cols(student, *student_rows)
-    )
-    place = jnp.stack([lax.axis_index("row") * rows, lax.axis_index("col") * cols]).astype(jnp.int32)
+    left = pass_on(to_right, COL, 1)
+    right = pass_on(to_left, COL, -1)
+    place = jnp.stack([lax.axis_index("row") * rows, lax.axis_index(COL) * cols]).astype(jnp.int32)
     tall = rows + 2 * EDGE_ROWS
     vmem = pl.BlockSpec(memory_space=pltpu.VMEM)
     current, weights = pl.pallas_call(
         functools.partial(
             affinity_kernel,
             full_rows=rows * lax.axis_size("row"),
-            full_cols=cols * lax.axis_size("col"),
+            full_cols=cols * size_of(COL),
             feat_channels=feat_channels,
             classes=classes,
         ),
@@ -219,7 +226,7 @@
         compiler_params=vmem_of(20),
         cost_estimate=cost_of(12),
     )(place, up, mid, down, left, right)
-    return current, weights, student_rows + (student_left, student_right)
+    return current, weights
 
 
 def finish(current, weights, cols):
@@ -241,65 +248,92 @@
     return refined
 
 
-def split_chunks(conv_part, class_part, devices):
-    height, width = conv_part.shape
-    tiles = conv_part.reshape(height // 8, 8, width // 128, 128).transpose(0, 2, 1, 3)
-    tiles = tiles.reshape(-1, 8, 128)
-    whole = (tiles.shape[0] // devices) * devices
-    head = tiles[:whole].reshape(devices, -1, 128)
-    rest = tiles[whole:].reshape(devices, -1, 128)
-    small = class_part.reshape(devices, -1)
-    small = jnp.pad(small, ((0, 0), (0, 128 - small.shape[1])))[:, None, :]
-    return head, rest, small
-
-
-def join_chunks(chunks, shapes, devices):
-    conv_shape, class_shape = shapes
-    channels, hidden = conv_shape[0] // 3, conv_shape[1] // 3
-    n_tiles = 9 * channels * hidden // 1024
-    head_rows = (n_tiles // devices) * 8
-    conv_rows = n_tiles * 8 // devices
-    head = chunks[:, :head_rows].reshape(-1, 8, 128)
-    rest = chunks[:, head_rows:conv_rows].reshape(-1, 8, 128)
-    tiles = jnp.concatenate([head, rest], axis=0)
-    tiles = tiles.reshape(3, channels // 8, 3, hidden // 128, 8, 128).transpose(0, 2, 1, 4, 3, 5)
-    small = chunks[:, conv_rows, : class_shape[0] * class_shape[1] // devices]
-    return tiles.reshape(9, channels, hidden), small.reshape(class_shape)
-
-
-def shift_of(largest):
-    return jnp.clip(jnp.ceil(jnp.log2(jnp.maximum(largest, 1e-30))), -100.0, 120.0)
-
-
-def pack_half(values, exponent):
-    scaled = (values * jnp.exp2(14.0 - exponent)).astype(jnp.float16)
-    marks = jnp.broadcast_to(exponent, values.shape[:-2] + (1, 128)).astype(jnp.float16)
-    rows = values.shape[-2]
-    fill = -(-(rows + 1) // 8) * 8 - rows - 1
-    zeros = jnp.zeros(values.shape[:-2] + (fill, 128), jnp.float16)
-    return jnp.concatenate([scaled, marks, zeros], axis=-2)
-
-
-def unpack_half(packed, rows):
-    exponent = packed[..., rows : rows + 1, :1].astype(jnp.float32)
-    return packed[..., :rows, :].astype(jnp.float32) * jnp.exp2(exponent - 14.0)
-
-
-def sum_everywhere(conv_part, class_part, axes):
-    devices = 1
-    for axis in axes:
-        devices = devices * lax.axis_size(axis)
-    head, rest, small = split_chunks(conv_part, class_part, devices)
-    values = jnp.concatenate([head, rest, small], axis=1)
-    rows = values.shape[1]
-    largest = jnp.maximum(jnp.max(jnp.abs(conv_part)), jnp.max(jnp.abs(class_part)))
-    sent = pack_half(values, shift_of(largest))
-    got = lax.all_to_all(sent, axes, split_axis=0, concat_axis=0, tiled=True)
-    total = jnp.sum(unpack_half(got, rows), axis=0)
-    mine = pack_half(total, shift_of(jnp.max(jnp.abs(total))))
-    spread = jnp.broadcast_to(mine[None], (devices,) + mine.shape)
-    everyone = lax.all_to_all(spread, axes, split_axis=0, concat_axis=0, tiled=True)
-    return join_chunks(unpack_half(everyone, rows), (conv_part.shape, class_part.shape), devices)
+CHIPS = ("row", "pair")
+PARTNER = [(0, 1), (1, 0)]
+CLASS_ROW = 36
+MARK_ROW = 37
+CHUNK_ROWS = 40
+
+
+def tile_places(n_tiles, chips):
+    full = n_tiles // chips
+    for tile in range(n_tiles):
+        if tile < full * chips:
+            yield tile, 0, 8, tile // full, 8 * (tile % full)
+        else:
+            share = 8 * (n_tiles - full * chips) // chips
+            for part in range(8 // share):
+                chip = (tile - full * chips) * (8 // share) + part
+                yield tile, part * share, share, chip, 8 * full
+
+
+def write_chunks(chunk_ref, conv_ref, class_ref, half):
+    height, width = conv_ref.shape[0] // 2, conv_ref.shape[1]
+    chips = chunk_ref.shape[0]
+    first = pl.multiple_of(half * height, height)
+    chunk_ref[:, CLASS_ROW:, :] = jnp.zeros((chips, CHUNK_ROWS - CLASS_ROW, 128), jnp.float32)
+    for tile, skip, count, chip, row in tile_places(height * width // 1024, chips):
+        block, lane = tile // (width // 128), tile % (width // 128)
+        rows = conv_ref[pl.ds(pl.multiple_of(first + 8 * block, 8), 8), 128 * lane : 128 * (lane + 1)]
+        chunk_ref[chip, row : row + count, :] = rows[skip : skip + count]
+    sums = jnp.where(half == 0, class_ref[:, :128], class_ref[:, 128:])
+    for k in range(class_ref.shape[0]):
+        chunk_ref[k, CLASS_ROW : CLASS_ROW + 1, :] = sums[k : k + 1]
+
+
+def read_chunks(core_ref, own_ref, other_ref, conv_ref, class_ref, *, scale):
+    _, channels, hidden = conv_ref.shape
+    width = 3 * hidden
+    chips = own_ref.shape[0]
+    for half in range(2):
+        mine = core_ref[0] == half
+        for tile, skip, count, chip, row in tile_places(3 * channels * width // 2048, chips):
+            block, lane = tile // (width // 128), tile % (width // 128)
+            top = half * 3 * channels // 2 + 8 * block
+            a, b = top // channels, 128 * lane // hidden
+            value = jnp.where(mine, own_ref[chip, row : row + count, :], other_ref[chip, row : row + count, :])
+            conv_ref[
+                3 * a + b, top % channels + skip : top % channels + skip + count,
+                128 * lane % hidden : 128 * lane % hidden + 128,
+            ] = value * scale
+        for k in range(class_ref.shape[0]):
+            value = jnp.where(
+                mine, own_ref[k, CLASS_ROW : CLASS_ROW + 1, :], other_ref[k, CLASS_ROW : CLASS_ROW + 1, :]
+            )
+            class_ref[k : k + 1, 128 * half : 128 * (half + 1)] = value * scale
+
+
+def pack_half(values):
+    marks = lax.broadcasted_iota(jnp.int32, values.shape, values.ndim - 2) == MARK_ROW
+    largest = jnp.max(jnp.where(marks, 0.0, jnp.abs(values)))
+    exponent = jnp.clip(jnp.ceil(jnp.log2(jnp.maximum(largest, 1e-30))), -100.0, 120.0)
+    return jnp.where(marks, exponent, values * jnp.exp2(14.0 - exponent)).astype(jnp.float16)
+
+
+def unpack_half(packed):
+    exponent = packed[..., MARK_ROW : MARK_ROW + 1, :].astype(jnp.float32)
+    return packed.astype(jnp.float32) * jnp.exp2(exponent - 14.0)
+
+
+def gather_all(total, core, conv_shape, class_shape, scale):
+    mine = pack_half(total)
+    spread = jnp.broadcast_to(mine[None], (size_of(CHIPS),) + mine.shape)
+    own = lax.all_to_all(spread, CHIPS, split_axis=0, concat_axis=0, tiled=True)
+    other = lax.ppermute(own, "core", PARTNER)
+    vmem = pl.BlockSpec(memory_space=pltpu.VMEM)
+    conv, small = pl.pallas_call(
+        functools.partial(read_chunks, scale=scale),
+        out_shape=(
+            jax.ShapeDtypeStruct(conv_shape, jnp.float32),
+            jax.ShapeDtypeStruct(class_shape[::-1], jnp.float32),
+        ),
+        in_specs=[pl.BlockSpec(memory_space=pltpu.SMEM), vmem, vmem],
+        out_specs=(vmem, vmem),
+        name="place",
+        compiler_params=vmem_of(12),
+        cost_estimate=cost_of(2),
+    )(core, unpack_half(own), unpack_half(other))
+    return conv, small.T
 
 
 def unit_edges_kernel(up_ref, mid_ref, down_ref, left_ref, right_ref):
@@ -390,10 +424,10 @@
 
 
 def grads_kernel(
-    up_ref, mid_ref, down_ref, left_ref, right_ref, back_ref, hidden_ref, error_ref,
-    conv_ref, class_ref, padded, first_cols, last_cols,
+    core_ref, up_ref, mid_ref, down_ref, left_ref, right_ref, back_ref, hidden_ref, error_ref,
+    keep_ref, send_ref, padded, first_cols, last_cols, conv_ref, class_ref,
 ):
-    rows, channels, cols = mid_ref.shape
+    rows, _, cols = mid_ref.shape
     step = pl.program_id(0)
 
     @pl.when(step == 0)
@@ -421,7 +455,7 @@
             jnp.concatenate([below.astype(jnp.bfloat16), back_ref[k], above.astype(jnp.bfloat16)], axis=0)
         )
         class_ref[...] += lax.dot_general(
-            hidden_ref[k], error_ref[k], CONTRACT_LAST, preferred_element_type=jnp.float32
+            error_ref[k], hidden_ref[k], CONTRACT_LAST, preferred_element_type=jnp.float32
         )
     conv_ref[...] += lax.dot_general(
         jnp.concatenate(images, axis=1), jnp.concatenate(backs, axis=1), CONTRACT_LAST,
@@ -438,6 +472,8 @@
                 jnp.concatenate(moved, axis=0), cells[...].astype(jnp.bfloat16), CONTRACT_LAST,
                 preferred_element_type=jnp.float32,
             )
+        write_chunks(keep_ref, conv_ref, class_ref, core_ref[0])
+        write_chunks(send_ref, conv_ref, class_ref, 1 - core_ref[0])
 
 
 def feature_kernel(
@@ -452,7 +488,7 @@
 
 
 def whole(array):
-    return pl.BlockSpec(array.shape, lambda i: (0,) * array.ndim)
+    return pl.BlockSpec(array.shape, lambda i: (0,) * array.ndim, pipeline_mode=pl.Buffered(1))
 
 
 def by_rows(shape):
@@ -470,7 +506,7 @@
         compiler_params=vmem_of(16),
         cost_estimate=cost_of(1),
     )(up, cells, down)
-    return pass_on(to_right, "col", 1), pass_on(to_left, "col", -1)
+    return pass_on(to_right, COL, 1), pass_on(to_left, COL, -1)
 
 
 def conv_scratch(rows, channels, cols, out):
@@ -482,41 +518,46 @@
     ]
 
 
-def row_call(kernel, name, rows, args, arg_rows, outs, out_rows, scratch, vmem, micros):
+def row_call(kernel, rows, args, arg_rows, outs, out_rows, scratch, vmem, micros):
     return pl.pallas_call(
         kernel,
         grid=(rows // STEP_ROWS,),
-        in_specs=[by_rows(a.shape) if split else whole(a) for a, split in zip(args, arg_rows)],
+        in_specs=[
+            pl.BlockSpec(memory_space=pltpu.SMEM) if a.ndim == 1 else by_rows(a.shape) if split else whole(a)
+            for a, split in zip(args, arg_rows)
+        ],
         out_specs=tuple(by_rows(o.shape) if split else whole(o) for o, split in zip(outs, out_rows)),
         out_shape=tuple(outs),
         scratch_shapes=scratch,
-        name=name,
         compiler_params=vmem_of(vmem),
         cost_estimate=cost_of(micros),
     )(*args)
 
 
-def shards(teacher_feats, teacher_probs, student_feats, conv_weight, class_weight):
+def local_step(teacher_feats, teacher_probs, student_feats, conv_weight, class_weight):
     channels, rows, cols = student_feats.shape
     hidden_size, classes = class_weight.shape
     pixel_count = float(rows * cols)
     student = student_feats.transpose(1, 0, 2)
-    current, weights, student_halo = refine(teacher_feats, teacher_probs, student)
-    halo = (student_halo[0], student, student_halo[1]) + student_halo[2:]
+    student_up, student_down = unit_rows(student)
+    mid, up, down = teacher_rows(teacher_feats, teacher_probs)
+    halo = (student_up, student, student_down) + unit_cols(student, student_up, student_down)
     f32, bf16 = jnp.float32, jnp.bfloat16
     slope, hidden, guess = row_call(
-        forward_kernel, "forward", rows,
+        forward_kernel, rows,
         halo + (conv_weight, class_weight.T), [False] * 7,
         [
             jax.ShapeDtypeStruct((rows, hidden_size, cols), f32),
             jax.ShapeDtypeStruct((rows, hidden_size, cols), bf16),
             jax.ShapeDtypeStruct((rows, classes, cols), f32),
         ],
-        [True] * 3, conv_scratch(rows, channels, cols, hidden_size), 32, 12,
+        [True] * 3, conv_scratch(rows, channels, cols, hidden_size), 16, 12,
     )
+    up, down, guess = lax.optimization_barrier((up, down, guess))
+    current, weights = refine(mid, up, down, teacher_feats.shape[0], classes)
     refined = finish(current, weights, cols)
     back, error = row_call(
-        back_kernel, "back", rows, (guess, refined, slope, class_weight), [True, True, True, False],
+        back_kernel, rows, (guess, refined, slope, class_weight), [True, True, True, False],
         [
             jax.ShapeDtypeStruct((rows, hidden_size, cols), bf16),
             jax.ShapeDtypeStruct((rows, classes, cols), bf16),
@@ -524,31 +565,37 @@
         [True] * 2, [], 16, 2,
     )
     back_up, back_down = unit_rows(back)
-    conv_part, class_part = row_call(
-        grads_kernel, "grads", rows, halo + (back, hidden, error), [False] * 5 + [True] * 3,
-        [
-            jax.ShapeDtypeStruct((3 * channels, 3 * hidden_size), f32),
-            jax.ShapeDtypeStruct((hidden_size, classes), f32),
-        ],
-        [False] * 2,
-        [pltpu.VMEM((rows + 2, channels, cols), bf16)] + [pltpu.VMEM((hidden_size, 128), f32)] * 2, 40, 9,
+    core = lax.axis_index("core").astype(jnp.int32).reshape(1)
+    chunks = jax.ShapeDtypeStruct((size_of(CHIPS), CHUNK_ROWS, 128), f32)
+    keep, sent = row_call(
+        grads_kernel, rows, (core,) + halo + (back, hidden, error), [False] * 6 + [True] * 3,
+        [chunks, chunks], [False] * 2,
+        [pltpu.VMEM((rows + 2, channels, cols), bf16)]
+        + [pltpu.VMEM((hidden_size, 128), f32)] * 2
+        + [pltpu.VMEM((3 * channels, 3 * hidden_size), f32), pltpu.VMEM((classes, hidden_size), f32)], 28, 9,
     )
-    back_left, back_right, conv_part, class_part = lax.optimization_barrier(
-        unit_cols(back, back_up, back_down) + (conv_part, class_part)
-    )
+    back_up, back_down, sent = lax.optimization_barrier((back_up, back_down, sent))
+    other = lax.ppermute(sent, "core", PARTNER)
+    back_cols = unit_cols(back, back_up, back_down)
+    packed = pack_half(keep + other)
+    back_left, back_right, packed = lax.optimization_barrier(back_cols + (packed,))
     (feature_grad,) = row_call(
-        feature_kernel, "feature", rows,
+        feature_kernel, rows,
         (back_up, back, back_down, back_left, back_right, conv_weight), [False] * 6,
         [jax.ShapeDtypeStruct((rows, channels, cols), bf16)],
-        [True], conv_scratch(rows, hidden_size, cols, channels), 32, 8,
+        [True], conv_scratch(rows, hidden_size, cols, channels), 16, 8,
     )
-    summed_conv, summed_class = sum_everywhere(conv_part, class_part, ("row", "col"))
-    grad_conv = summed_conv / pixel_count
-    grad_class = summed_class / pixel_count
+    received = lax.all_to_all(packed, CHIPS, split_axis=0, concat_axis=0, tiled=True)
+    total = jnp.sum(unpack_half(received), axis=0)
+    total, feature_grad = lax.optimization_barrier((total, feature_grad))
+    grad_conv, grad_class = gather_all(total, core, conv_weight.shape, class_weight.shape, 1.0 / pixel_count)
     return (refined.transpose(1, 0, 2), feature_grad.transpose(1, 0, 2), grad_conv, grad_class)
 
 
 def solution(mesh):
-    in_specs = (P(None, "row", "col"), P(None, "row", "col"), P(None, "row", "col"), P(), P())
-    out_specs = (P(None, "row", "col"), P(None, "row", "col"), P(), P())
-    return jax.shard_map(shards, mesh=mesh, in_specs=in_specs, out_specs=out_specs, check_vma=False)
+    devices = mesh.devices
+    mesh = Mesh(devices.reshape(devices.shape[0], -1, 2), ("row",) + COL)
+    split = P(None, "row", COL)
+    in_specs = (split, split, split, P(), P())
+    out_specs = (split, split, P(), P())
+    return jax.shard_map(local_step, mesh=mesh, in_specs=in_specs, out_specs=out_specs, check_vma=False)

time: 193 us -> 180 us (0.933)
  waiting for transfers between devices: 31 us -> 19.2 us
  blocking collectives: 33 us -> 22.3 us
  starting transfers between devices: 47.6 us -> 55.3 us
  local copies, waits for them, and re-layouts: 15.1 us -> 17.1 us
    all_to_all x1, blocking collectives: 33 us -> 22.3 us  [gather_all(): own = lax.all_to_all(spread, CHIPS, split_axis=0, concat_axis=0, tiled=True)]
    unnamed x36 -> x59, local copies, waits for them, and re-layouts: 8.7 us -> 16 us
    all_to_all x1, waiting for transfers between devices: 8.03 us -> 0.73 us  [local_step(): lax.all_to_all(packed, CHIPS, split_axis=0, concat_axis=0, tiled=True)]
    all_to_all x1, starting transfers between devices: 5.34 us -> 12.2 us  [local_step(): lax.all_to_all(packed, CHIPS, split_axis=0, concat_axis=0, tiled=True)]
    ppermute x7, waiting for transfers between devices: 22 us -> 17.7 us  [pass_on(): return lax.ppermute(cells, axis, [(i + 1, i) for i in range(ends)])]
    pallas_call x4 -> x5, Pallas kernels: 35.4 us -> 35.5 us  [the longest x4 33.8 us: row_call(): pl.pallas_call(kernel, grid=(rows // STEP_ROWS,), in_specs=[pl.BlockSpec(...]
  transfers between devices with their start and end apart: 15 -> 17, of which waited for: 6 -> 8; matrix products, arithmetic and copies ran while one was open for 3% -> 4% of each run, Pallas kernels for 19% -> 18%
where the time goes in v2:
time: 180 us; the launch traced here: 179 us
  Pallas kernels  56.9 us (32%)
  starting transfers between devices  55.3 us (31%)
  blocking collectives  22.3 us (12%)
  waiting for transfers between devices  19.2 us (11%)
  local copies, waits for them, and re-layouts  17.1 us (10%)
  other arithmetic  5.71 us (3%)
  between operations  2.67 us (1%)
    pallas_call x4, Pallas kernels, row_call(): pl.pallas_call(kernel, grid=(rows // STEP_ROWS,), in_specs=[pl.BlockSpec(...  33.8 us
    ppermute x7, starting transfers between devices, pass_on(): return lax.ppermute(cells, axis, [(i, i + 1) for i in range(ends)])  32 us
    all_to_all x1, blocking collectives, gather_all(): own = lax.all_to_all(spread, CHIPS, split_axis=0, concat_axis=0, tiled=True)  22.3 us
    ppermute x7, waiting for transfers between devices, pass_on(): return lax.ppermute(cells, axis, [(i + 1, i) for i in range(ends)])  17.7 us
    unnamed x59, local copies, waits for them, and re-layouts  16 us
    pallas_call x1, Pallas kernels, refine(): pl.pallas_call(functools.partial(affinity_kernel, full_rows=rows * lax.ax...  14.8 us
    all_to_all x1, starting transfers between devices, local_step(): lax.all_to_all(packed, CHIPS, split_axis=0, concat_axis=0, tiled=True)  12.2 us
    ppermute x7, starting transfers between devices, pass_on(): return lax.ppermute(cells, axis, [(i + 1, i) for i in range(ends)])  10.9 us
  transfers between devices with their start and end apart: 17, of which 8 were waited for; matrix products, arithmetic and copies ran while one was open for 4% of the time, Pallas kernels for 18%

profile of v2, /device:TPU:1, one launch (start us, length us, event | category | flops | bytes accessed | tf_op | source)
XLA Modules:
  0.0 179.1 jit_solution(13031184787673303573)
XLA Ops:
  0.7 2.4 %copy.26 = bf16[256,16,256]{2,0,1:T(8,128)(2,1)S(1)} copy(bf16[256,16,256]{2,1,0:T(8,128)(2,1)} %param.7) | data formatting | bytes 4194304 | tf_op args[2]
  3.0 3.9 %collective-permute-start.2 = (bf16[1,256,256]{2,1,0:T(8,128)(2,1)S(1)}, bf16[1,256,256]{2,1,0:T(8,128)(2,1)S(1)}, u32[]{:S(2)}, u32[]{:S(2)}) collective-permute-start(bf16[1,256,256]{2,1,0:T(8,128)(2,1)S(1)} %get-tuple-element.73), channel_id=1, source_target_pairs={{0,16},{16,32},{32,48},{48,64},{64,80},{80,96},{96,112},{1,17},{17... | collective-permute-start | bytes 393224 | tf_op jit(solution)/shard_map/ppermute | solution.py:179
  9.1 5.2 %collective-permute-done.3.down_ref = bf16[1,256,256]{2,1,0:T(8,128)(2,1)S(1)} collective-permute-done((bf16[1,256,256]{2,1,0:T(8,128)(2,1)S(1)}, bf16[1,256,256]{2,1,0:T(8,128)(2,1)S(1)}, u32[]{:S(2)}, u32[]{:S(2)}) %collective-permute-start.3) | collective-permute-done | bytes 131104 | tf_op jit(solution)/shard_map/ppermute | solution.py:180
  15.7 5.8 %collective-permute-start.4 = (bf16[256,128]{1,0:T(8,128)(2,1)}, bf16[256,128]{1,0:T(8,128)(2,1)S(1)}, u32[]{:S(2)}, u32[]{:S(2)}) collective-permute-start(bf16[256,128]{1,0:T(8,128)(2,1)} %get-tuple-element.32), channel_id=1, source_target_pairs={{0,1},{1,2},{2,3},{3,4},{4,5},{5,6},{6,7},{7,8},{8,9},{9,10},{10,1... | collective-permute-start | bytes 196616 | tf_op jit(solution)/shard_map/ppermute | solution.py:179
  21.5 1.9 %collective-permute-start.5 = (bf16[256,128]{1,0:T(8,128)(2,1)S(1)}, bf16[256,128]{1,0:T(8,128)(2,1)S(1)}, u32[]{:S(2)}, u32[]{:S(2)}) collective-permute-start(bf16[256,128]{1,0:T(8,128)(2,1)S(1)} %get-tuple-element.33), channel_id=1, source_target_pairs={{1,0},{2,1},{3,2},{4,3},{5,4},{6,5},{7,6},{8,7},{9,8},{10,9},{11,1... | collective-permute-start | bytes 196616 | tf_op jit(solution)/shard_map/ppermute | solution.py:180
  24.3 2.8 %collective-permute-start = (bf16[8,80,256]{2,1,0:T(8,128)(2,1)}, bf16[8,80,256]{2,1,0:T(8,128)(2,1)S(1)}, u32[]{:S(2)}, u32[]{:S(2)}) collective-permute-start(bf16[8,80,256]{2,1,0:T(8,128)(2,1)} %get-tuple-element.75), channel_id=1, source_target_pairs={{0,16},{16,32},{32,48},{48,64},{64,80},{80,96},{96,112},{1,17},{17... | collective-permute-start | bytes 983048 | tf_op jit(solution)/shard_map/ppermute | solution.py:179
  29.9 15.6 %shard_map.84 = (f32[16,256,256]{2,1,0:T(8,128)S(1)}, bf16[16,256,256]{2,1,0:T(8,128)(2,1)S(1)}, f32[16,8,256]{2,1,0:T(8,128)S(1)}) custom-call(bf16[1,256,256]{2,1,0:T(8,128)(2,1)S(1)} %collective-permute-done.2.up_ref, bf16[16,256,256]{2,1,0:T(8,128)(2,1)S(1)} %bitcast.17, bf16[1,256,256]{2,1,0:T(8,128)(2,1)S(1)} %collective-permute-done.3.down_ref, ...), custom_call_target="tpu_custom_call" | custom-call | flops 12000000000 | bytes 36000000 | tf_op jit(solution)/shard_map/pallas_call | solution.py:522
  45.4 1.9 %copy-done.17 = f32[16,256,256]{2,1,0:T(8,128)} copy-done((f32[16,256,256]{2,1,0:T(8,128)}, f32[16,256,256]{2,1,0:T(8,128)S(1)}, u32[]{:S(2)}) %copy-start.17) | copy-done | bytes 4194328
  49.0 5.9 %collective-permute-start.6 = (bf16[4,80,128]{2,1,0:T(8,128)(2,1)S(1)}, bf16[4,80,128]{2,1,0:T(8,128)(2,1)S(1)}, u32[]{:S(2)}, u32[]{:S(2)}) collective-permute-start(bf16[4,80,128]{2,1,0:T(8,128)(2,1)S(1)} %get-tuple-element.37), channel_id=1, source_target_pairs={{0,1},{1,2},{2,3},{3,4},{4,5},{5,6},{6,7},{7,8},{8,9},{9,10},{10,1... | collective-permute-start | bytes 245768 | tf_op jit(solution)/shard_map/ppermute | solution.py:179
  54.9 1.9 %collective-permute-start.7 = (bf16[4,80,128]{2,1,0:T(8,128)(2,1)S(1)}, bf16[4,80,128]{2,1,0:T(8,128)(2,1)S(1)}, u32[]{:S(2)}, u32[]{:S(2)}) collective-permute-start(bf16[4,80,128]{2,1,0:T(8,128)(2,1)S(1)} %get-tuple-element.38), channel_id=1, source_target_pairs={{1,0},{2,1},{3,2},{4,3},{5,4},{6,5},{7,6},{8,7},{9,8},{10,9},{11,1... | collective-permute-start | bytes 245768 | tf_op jit(solution)/shard_map/ppermute | solution.py:180
  56.9 5.3 %collective-permute-done.7.right_ref = bf16[4,80,128]{2,1,0:T(8,128)(2,1)S(1)} collective-permute-done((bf16[4,80,128]{2,1,0:T(8,128)(2,1)S(1)}, bf16[4,80,128]{2,1,0:T(8,128)(2,1)S(1)}, u32[]{:S(2)}, u32[]{:S(2)}) %collective-permute-start.7) | collective-permute-done | bytes 81952 | tf_op jit(solution)/shard_map/ppermute | solution.py:180
  62.2 14.8 %affinity.1 = (f32[16,8,384]{2,1,0:T(8,128)S(1)}, f32[25,24,384]{2,1,0:T(8,128)S(1)}) custom-call(s32[2]{0:T(128)S(1)} %pad_add_fusion.place_ref, bf16[8,80,256]{2,1,0:T(8,128)(2,1)S(1)} %collective-permute-done.up_ref, bf16[16,80,256]{2,1,0:T(8,128)(2,1)S(1)} %maximum_bitcast_fusion.mid_ref, bf16[8,80,256]{2,1,0:T(8,128)(2,1)} %collective-permute-done.1.down_ref, ...), custom_call_target="tpu_custom_call" | custom-call | flops 12000000000 | bytes 36000000 | tf_op jit(solution)/shard_map/affinity/pallas_call | solution.py:204
  77.9 3.7 %collective-permute-start.8 = (f32[8,8,384]{2,1,0:T(8,128)S(1)}, f32[8,8,384]{2,1,0:T(8,128)S(1)}, u32[]{:S(2)}, u32[]{:S(2)}) collective-permute-start(f32[8,8,384]{2,1,0:T(8,128)S(1)} %get-tuple-element.77), channel_id=1, source_target_pairs={{0,16},{16,32},{32,48},{48,64},{64,80},{80,96},{96,112},{1,17},{17... | collective-permute-start | bytes 294920 | tf_op jit(solution)/shard_map/ppermute | solution.py:179
  83.2 4.8 %collective-permute-done.9.down_ref = f32[8,8,384]{2,1,0:T(8,128)S(1)} collective-permute-done((f32[8,8,384]{2,1,0:T(8,128)S(1)}, f32[8,8,384]{2,1,0:T(8,128)S(1)}, u32[]{:S(2)}, u32[]{:S(2)}) %collective-permute-start.9) | collective-permute-done | bytes 98336 | tf_op jit(solution)/shard_map/ppermute | solution.py:180
  89.2 3.0 %finish.1.refined_ref = f32[16,8,256]{2,1,0:T(8,128)S(1)} custom-call(f32[25,24,384]{2,1,0:T(8,128)S(1)} %copy-done.22, f32[8,8,384]{2,1,0:T(8,128)S(1)} %collective-permute-done.8.up_ref, f32[16,8,384]{2,1,0:T(8,128)S(1)} %get-tuple-element.40.mid_ref, f32[8,8,384]{2,1,0:T(8,128)S(1)} %collective-permute-done.9.down_ref), custom_call_target="tpu_custom_call" | custom-call | flops 4000000000 | bytes 12000000 | tf_op jit(solution)/shard_map/finish/pallas_call | solution.py:237
  94.0 4.3 %collective-permute-start.10 = (bf16[1,256,256]{2,1,0:T(8,128)(2,1)S(1)}, bf16[1,256,256]{2,1,0:T(8,128)(2,1)S(1)}, u32[]{:S(2)}, u32[]{:S(2)}) collective-permute-start(bf16[1,256,256]{2,1,0:T(8,128)(2,1)S(1)} %get-tuple-element.71), channel_id=1, source_target_pairs={{0,16},{16,32},{32,48},{48,64},{64,80},{80,96},{96,112},{1,17},{17... | collective-permute-start | bytes 393224 | tf_op jit(solution)/shard_map/ppermute | solution.py:179
  99.6 8.6 %shard_map.86 = (f32[64,40,128]{2,1,0:T(8,128)S(1)}, f32[64,40,128]{2,1,0:T(8,128)S(1)}) custom-call(s32[1]{0:T(128)} %bitcast.6.core_ref, bf16[1,256,256]{2,1,0:T(8,128)(2,1)S(1)} %collective-permute-done.2.up_ref, bf16[16,256,256]{2,1,0:T(8,128)(2,1)S(1)} %bitcast.18, bf16[1,256,256]{2,1,0:T(8,128)(2,1)S(1)} %collective-permute-done.3.down_ref, ...), custom_call_target="tpu_custom_call" | custom-call | flops 8999999488 | bytes 27000000 | tf_op jit(solution)/shard_map/pallas_call | solution.py:522
  109.0 5.7 %collective-permute-start.12 = (bf16[256,128]{1,0:T(8,128)(2,1)S(1)}, bf16[256,128]{1,0:T(8,128)(2,1)S(1)}, u32[]{:S(2)}, u32[]{:S(2)}) collective-permute-start(bf16[256,128]{1,0:T(8,128)(2,1)S(1)} %get-tuple-element.49), channel_id=1, source_target_pairs={{0,1},{1,2},{2,3},{3,4},{4,5},{5,6},{6,7},{7,8},{8,9},{9,10},{10,1... | collective-permute-start | bytes 196616 | tf_op jit(solution)/shard_map/ppermute | solution.py:179
  114.7 1.9 %collective-permute-start.13 = (bf16[256,128]{1,0:T(8,128)(2,1)S(1)}, bf16[256,128]{1,0:T(8,128)(2,1)S(1)}, u32[]{:S(2)}, u32[]{:S(2)}) collective-permute-start(bf16[256,128]{1,0:T(8,128)(2,1)S(1)} %get-tuple-element.50), channel_id=1, source_target_pairs={{1,0},{2,1},{3,2},{4,3},{5,4},{6,5},{7,6},{8,7},{9,8},{10,9},{11,1... | collective-permute-start | bytes 196616 | tf_op jit(solution)/shard_map/ppermute | solution.py:180
  119.5 2.3 %collective-permute-done.13.right_ref = bf16[256,128]{1,0:T(8,128)(2,1)S(1)} collective-permute-done((bf16[256,128]{1,0:T(8,128)(2,1)S(1)}, bf16[256,128]{1,0:T(8,128)(2,1)S(1)}, u32[]{:S(2)}, u32[]{:S(2)}) %collective-permute-start.13) | collective-permute-done | bytes 65568 | tf_op jit(solution)/shard_map/ppermute | solution.py:180
  122.4 12.2 %all-to-all-start = ((f16[64,40,128]{2,1,0:T(8,128)(2,1)}), f16[64,40,128]{2,1,0:T(8,128)(2,1)}, u32[]{:S(2)}, u32[]{:S(2)}) async-start(f16[64,40,128]{2,1,0:T(8,128)(2,1)} %select_convert_fusion), calls=%async_computation | async-start | bytes 1310720 | tf_op jit(solution)/shard_map/all_to_all | solution.py:588
  138.9 7.9 %shard_map.87 = bf16[16,256,256]{2,1,0:T(8,128)(2,1)S(1)} custom-call(bf16[1,256,256]{2,1,0:T(8,128)(2,1)S(1)} %copy-done.6, bf16[16,256,256]{2,1,0:T(8,128)(2,1)S(1)} %copy-done.1, bf16[1,256,256]{2,1,0:T(8,128)(2,1)S(1)} %copy-done.8, bf16[256,128]{1,0:T(8,128)(2,1)S(1)} %copy-done.14, bf16[256,128]{1,0:T(8,128)(2,1)S(1)} %copy-done.16, ...), custom_call_target="tpu_custom_call" | custom-call | flops 8000000000 | bytes 24000000 | tf_op jit(solution)/shard_map/pallas_call | solution.py:522
  151.4 22.3 %all_to_all.10 = f16[64,40,128]{2,1,0:T(8,128)(2,1)S(1)} all-to-all(f16[64,40,128]{2,1,0:T(8,128)(2,1)S(1)} %broadcast_in_dim.26), channel_id=1, replica_groups=mesh['row'=8,'pair'=8,'core'=2] {'row','pair'}, dimensions={0} | all-to-all | bytes 1310720 | tf_op jit(solution)/shard_map/all_to_all | solution.py:321
  174.4 2.5 %copy.22 = bf16[256,16,256]{2,1,0:T(8,128)(2,1)} copy(bf16[256,16,256]{2,0,1:T(8,128)(2,1)S(1)} %bitcast.19) | data formatting | bytes 4194304
  (99 shorter events, 29.9 us)
Async XLA Ops:
  0.6 7.8 %copy-start.25 = (bf16[64,16,256]{2,1,0:T(8,128)(2,1)S(1)}, bf16[64,16,256]{2,1,0:T(8,128)(2,1)}, u32[]{:S(2)}) copy-start(bf16[64,16,256]{2,1,0:T(8,128)(2,1)} %param.5) | copy-start | bytes 1572868
  3.0 6.1 %collective-permute-start.2 = (bf16[1,256,256]{2,1,0:T(8,128)(2,1)S(1)}, bf16[1,256,256]{2,1,0:T(8,128)(2,1)S(1)}, u32[]{:S(2)}, u32[]{:S(2)}) collective-permute-start(bf16[1,256,256]{2,1,0:T(8,128)(2,1)S(1)} %get-tuple-element.73), channel_id=1, source_target_pairs={{0,16},{16,32},{32,48},{48,64},{64,80},{80,96},{96,112},{1,17},{17... | collective-permute-start | bytes 393224 | tf_op jit(solution)/shard_map/ppermute | solution.py:179
  7.0 7.4 %collective-permute-start.3 = (bf16[1,256,256]{2,1,0:T(8,128)(2,1)S(1)}, bf16[1,256,256]{2,1,0:T(8,128)(2,1)S(1)}, u32[]{:S(2)}, u32[]{:S(2)}) collective-permute-start(bf16[1,256,256]{2,1,0:T(8,128)(2,1)S(1)} %get-tuple-element.72), channel_id=1, source_target_pairs={{16,0},{32,16},{48,32},{64,48},{80,64},{96,80},{112,96},{17,1},{33... | collective-permute-start | bytes 393224 | tf_op jit(solution)/shard_map/ppermute | solution.py:180
  15.7 12.9 %copy-start.2 = (bf16[256,8]{0,1:T(8,128)(2,1)S(1)}, bf16[256,8]{0,1:T(8,128)(2,1)}, u32[]{:S(2)}) copy-start(bf16[256,8]{0,1:T(8,128)(2,1)} %param.9) | copy-start | bytes 12292
  15.7 12.7 %collective-permute-start.4 = (bf16[256,128]{1,0:T(8,128)(2,1)}, bf16[256,128]{1,0:T(8,128)(2,1)S(1)}, u32[]{:S(2)}, u32[]{:S(2)}) collective-permute-start(bf16[256,128]{1,0:T(8,128)(2,1)} %get-tuple-element.32), channel_id=1, source_target_pairs={{0,1},{1,2},{2,3},{3,4},{4,5},{5,6},{6,7},{7,8},{8,9},{9,10},{10,1... | collective-permute-start | bytes 196616 | tf_op jit(solution)/shard_map/ppermute | solution.py:179
  21.5 7.1 %collective-permute-start.5 = (bf16[256,128]{1,0:T(8,128)(2,1)S(1)}, bf16[256,128]{1,0:T(8,128)(2,1)S(1)}, u32[]{:S(2)}, u32[]{:S(2)}) collective-permute-start(bf16[256,128]{1,0:T(8,128)(2,1)S(1)} %get-tuple-element.33), channel_id=1, source_target_pairs={{1,0},{2,1},{3,2},{4,3},{5,4},{6,5},{7,6},{8,7},{9,8},{10,9},{11,1... | collective-permute-start | bytes 196616 | tf_op jit(solution)/shard_map/ppermute | solution.py:180
  24.3 23.1 %collective-permute-start = (bf16[8,80,256]{2,1,0:T(8,128)(2,1)}, bf16[8,80,256]{2,1,0:T(8,128)(2,1)S(1)}, u32[]{:S(2)}, u32[]{:S(2)}) collective-permute-start(bf16[8,80,256]{2,1,0:T(8,128)(2,1)} %get-tuple-element.75), channel_id=1, source_target_pairs={{0,16},{16,32},{32,48},{48,64},{64,80},{80,96},{96,112},{1,17},{17... | collective-permute-start | bytes 983048 | tf_op jit(solution)/shard_map/ppermute | solution.py:179
  27.1 20.3 %collective-permute-start.1 = (bf16[8,80,256]{2,1,0:T(8,128)(2,1)}, bf16[8,80,256]{2,1,0:T(8,128)(2,1)}, u32[]{:S(2)}, u32[]{:S(2)}) collective-permute-start(bf16[8,80,256]{2,1,0:T(8,128)(2,1)} %get-tuple-element.74), channel_id=1, source_target_pairs={{16,0},{32,16},{48,32},{64,48},{80,64},{96,80},{112,96},{17,1},{33... | collective-permute-start | bytes 983048 | tf_op jit(solution)/shard_map/ppermute | solution.py:180
  28.4 17.0 %copy-start.9 = (bf16[256,128]{1,0:T(8,128)(2,1)}, bf16[256,128]{1,0:T(8,128)(2,1)S(1)}, u32[]{:S(2)}) copy-start(bf16[256,128]{1,0:T(8,128)(2,1)S(1)} %collective-permute-done.4.left_ref) | copy-start | bytes 196612
  28.6 16.9 %copy-start.11 = (bf16[256,128]{1,0:T(8,128)(2,1)}, bf16[256,128]{1,0:T(8,128)(2,1)S(1)}, u32[]{:S(2)}) copy-start(bf16[256,128]{1,0:T(8,128)(2,1)S(1)} %collective-permute-done.5.right_ref) | copy-start | bytes 196612
  49.0 7.9 %collective-permute-start.6 = (bf16[4,80,128]{2,1,0:T(8,128)(2,1)S(1)}, bf16[4,80,128]{2,1,0:T(8,128)(2,1)S(1)}, u32[]{:S(2)}, u32[]{:S(2)}) collective-permute-start(bf16[4,80,128]{2,1,0:T(8,128)(2,1)S(1)} %get-tuple-element.37), channel_id=1, source_target_pairs={{0,1},{1,2},{2,3},{3,4},{4,5},{5,6},{6,7},{7,8},{8,9},{9,10},{10,1... | collective-permute-start | bytes 245768 | tf_op jit(solution)/shard_map/ppermute | solution.py:179
  54.9 7.3 %collective-permute-start.7 = (bf16[4,80,128]{2,1,0:T(8,128)(2,1)S(1)}, bf16[4,80,128]{2,1,0:T(8,128)(2,1)S(1)}, u32[]{:S(2)}, u32[]{:S(2)}) collective-permute-start(bf16[4,80,128]{2,1,0:T(8,128)(2,1)S(1)} %get-tuple-element.38), channel_id=1, source_target_pairs={{1,0},{2,1},{3,2},{4,3},{5,4},{6,5},{7,6},{8,7},{9,8},{10,9},{11,1... | collective-permute-start | bytes 245768 | tf_op jit(solution)/shard_map/ppermute | solution.py:180
  77.9 5.3 %collective-permute-start.8 = (f32[8,8,384]{2,1,0:T(8,128)S(1)}, f32[8,8,384]{2,1,0:T(8,128)S(1)}, u32[]{:S(2)}, u32[]{:S(2)}) collective-permute-start(f32[8,8,384]{2,1,0:T(8,128)S(1)} %get-tuple-element.77), channel_id=1, source_target_pairs={{0,16},{16,32},{32,48},{48,64},{64,80},{80,96},{96,112},{1,17},{17... | collective-permute-start | bytes 294920 | tf_op jit(solution)/shard_map/ppermute | solution.py:179
  81.6 6.4 %collective-permute-start.9 = (f32[8,8,384]{2,1,0:T(8,128)S(1)}, f32[8,8,384]{2,1,0:T(8,128)S(1)}, u32[]{:S(2)}, u32[]{:S(2)}) collective-permute-start(f32[8,8,384]{2,1,0:T(8,128)S(1)} %get-tuple-element.76), channel_id=1, source_target_pairs={{16,0},{32,16},{48,32},{64,48},{80,64},{96,80},{112,96},{17,1},{33... | collective-permute-start | bytes 294920 | tf_op jit(solution)/shard_map/ppermute | solution.py:180
  94.0 14.4 %copy-start = (bf16[16,256,256]{2,1,0:T(8,128)(2,1)}, bf16[16,256,256]{2,1,0:T(8,128)(2,1)S(1)}, u32[]{:S(2)}) copy-start(bf16[16,256,256]{2,1,0:T(8,128)(2,1)S(1)} %get-tuple-element.43.back_ref.mid_ref) | copy-start | bytes 6291460
  94.0 14.2 %collective-permute-start.10 = (bf16[1,256,256]{2,1,0:T(8,128)(2,1)S(1)}, bf16[1,256,256]{2,1,0:T(8,128)(2,1)S(1)}, u32[]{:S(2)}, u32[]{:S(2)}) collective-permute-start(bf16[1,256,256]{2,1,0:T(8,128)(2,1)S(1)} %get-tuple-element.71), channel_id=1, source_target_pairs={{0,16},{16,32},{32,48},{48,64},{64,80},{80,96},{96,112},{1,17},{17... | collective-permute-start | bytes 393224 | tf_op jit(solution)/shard_map/ppermute | solution.py:179
  98.3 9.9 %collective-permute-start.11 = (bf16[1,256,256]{2,1,0:T(8,128)(2,1)S(1)}, bf16[1,256,256]{2,1,0:T(8,128)(2,1)S(1)}, u32[]{:S(2)}, u32[]{:S(2)}) collective-permute-start(bf16[1,256,256]{2,1,0:T(8,128)(2,1)S(1)} %get-tuple-element.70), channel_id=1, source_target_pairs={{16,0},{32,16},{48,32},{64,48},{80,64},{96,80},{112,96},{17,1},{33... | collective-permute-start | bytes 393224 | tf_op jit(solution)/shard_map/ppermute | solution.py:180
  108.2 8.4 %collective-permute-start.14 = (f32[64,40,128]{2,1,0:T(8,128)S(1)}, f32[64,40,128]{2,1,0:T(8,128)S(1)}, u32[]{:S(2)}, u32[]{:S(2)}) collective-permute-start(f32[64,40,128]{2,1,0:T(8,128)S(1)} %get-tuple-element.52), channel_id=1, source_target_pairs={{0,1},{1,0},{2,3},{3,2},{4,5},{5,4},{6,7},{7,6},{8,9},{9,8},{10,11... | collective-permute-start | bytes 3932168 | tf_op jit(solution)/shard_map/ppermute | solution.py:578
  109.0 10.5 %collective-permute-start.12 = (bf16[256,128]{1,0:T(8,128)(2,1)S(1)}, bf16[256,128]{1,0:T(8,128)(2,1)S(1)}, u32[]{:S(2)}, u32[]{:S(2)}) collective-permute-start(bf16[256,128]{1,0:T(8,128)(2,1)S(1)} %get-tuple-element.49), channel_id=1, source_target_pairs={{0,1},{1,2},{2,3},{3,4},{4,5},{5,6},{6,7},{7,8},{8,9},{9,10},{10,1... | collective-permute-start | bytes 196616 | tf_op jit(solution)/shard_map/ppermute | solution.py:179
  114.7 7.1 %collective-permute-start.13 = (bf16[256,128]{1,0:T(8,128)(2,1)S(1)}, bf16[256,128]{1,0:T(8,128)(2,1)S(1)}, u32[]{:S(2)}, u32[]{:S(2)}) collective-permute-start(bf16[256,128]{1,0:T(8,128)(2,1)S(1)} %get-tuple-element.50), channel_id=1, source_target_pairs={{1,0},{2,1},{3,2},{4,3},{5,4},{6,5},{7,6},{8,7},{9,8},{10,9},{11,1... | collective-permute-start | bytes 196616 | tf_op jit(solution)/shard_map/ppermute | solution.py:180
  118.4 16.3 %copy-start.4 = (bf16[9,256,256]{2,1,0:T(8,128)(2,1)S(1)}, bf16[9,256,256]{2,1,0:T(8,128)(2,1)}, u32[]{:S(2)}) copy-start(bf16[9,256,256]{2,1,0:T(8,128)(2,1)} %taps_ref.3) | copy-start | bytes 3538948
  118.4 16.3 %copy-start.6 = (bf16[1,256,256]{2,1,0:T(8,128)(2,1)S(1)}, bf16[1,256,256]{2,1,0:T(8,128)(2,1)}, u32[]{:S(2)}) copy-start(bf16[1,256,256]{2,1,0:T(8,128)(2,1)} %copy-done.5) | copy-start | bytes 393220
  122.4 25.1 %all-to-all-start = ((f16[64,40,128]{2,1,0:T(8,128)(2,1)}), f16[64,40,128]{2,1,0:T(8,128)(2,1)}, u32[]{:S(2)}, u32[]{:S(2)}) async-start(f16[64,40,128]{2,1,0:T(8,128)(2,1)} %select_convert_fusion), calls=%async_computation | async-start | bytes 1310720 | tf_op jit(solution)/shard_map/all_to_all | solution.py:588
  173.7 3.4 %collective-permute-start.15 = (f16[64,40,128]{2,1,0:T(8,128)(2,1)S(1)}, f16[64,40,128]{2,1,0:T(8,128)(2,1)S(1)}, u32[]{:S(2)}, u32[]{:S(2)}) collective-permute-start(f16[64,40,128]{2,1,0:T(8,128)(2,1)S(1)} %all_to_all.10), channel_id=1, source_target_pairs={{0,1},{1,0},{2,3},{3,2},{4,5},{5,4},{6,7},{7,6},{8,9},{9,8},{10,11... | collective-permute-start | bytes 1966088 | tf_op jit(solution)/shard_map/ppermute | solution.py:322
  (20 other events, 53.2 us)

commit v3 on v2

--- a/solution.py
+++ b/solution.py
@@ -32,20 +32,42 @@
     return lax.broadcasted_iota(jnp.int32, shape, len(shape) - 1)
 
 
-def edges_kernel(up_ref, mid_ref, down_ref, left_ref, right_ref):
-    channels = mid_ref.shape[1]
+def packed_row(ref, skip):
+    return jnp.concatenate([ref[i, skip:, :] for i in range(EDGE_ROWS)], axis=0)
+
+
+def edges_kernel(up_ref, mid_ref, down_ref, student_ref, left_ref, right_ref):
+    rows, channels, _ = mid_ref.shape
     group = lane_of((channels, 128)) // EDGE_COLS
-    sources = [up_ref] + [mid_ref.at[pl.ds(8 * g, 8)] for g in range(mid_ref.shape[0] // 8)] + [down_ref]
-    for g, source in enumerate(sources):
+    groups = rows // 8 + 2
+    for g in range(groups):
+        source = up_ref if g == 0 else down_ref if g == groups - 1 else mid_ref.at[pl.ds(8 * (g - 1), 8)]
         left = jnp.zeros((channels, 128), jnp.float32)
         right = jnp.zeros((channels, 128), jnp.float32)
         for i in range(8):
-            first = source[i, :, :128].astype(jnp.float32)
-            last = source[i, :, -128:].astype(jnp.float32)
+            first = source[i, :channels, :128].astype(jnp.float32)
+            last = source[i, :channels, -128:].astype(jnp.float32)
             left = jnp.where(group == i, pltpu.roll(first, EDGE_COLS * i, 1), left)
             right = jnp.where(group == i, pltpu.roll(last, (EDGE_COLS * (i + 1)) % 128, 1), right)
-        left_ref[g] = left.astype(left_ref.dtype)
-        right_ref[g] = right.astype(right_ref.dtype)
+        left_ref[channels * g : channels * (g + 1)] = left.astype(left_ref.dtype)
+        right_ref[channels * g : channels * (g + 1)] = right.astype(right_ref.dtype)
+    up, down = packed_row(up_ref, channels), packed_row(down_ref, channels)
+    left, right = border_cells([up] + [student_ref.at[i] for i in range(rows)] + [down], student_ref.shape[1:])
+    left_ref[channels * groups :] = left.astype(left_ref.dtype)
+    right_ref[channels * groups :] = right.astype(right_ref.dtype)
+
+
+def border_cells(sources, shape):
+    channels, cols = shape
+    lanes = lane_of((channels, 128))
+    left = jnp.zeros((channels, 128), jnp.float32)
+    right = jnp.zeros((channels, 128), jnp.float32)
+    for i, source in enumerate(sources):
+        first = source[:, :128].astype(jnp.float32)
+        last = source[:, cols - 128 :].astype(jnp.float32)
+        left = jnp.where(lanes == i, pltpu.roll(first, i, 1), left)
+        right = jnp.where(lanes == i, pltpu.roll(last, i + 1, 1), right)
+    return left, right
 
 
 def sweep_row(weights, center_row, read_row):
@@ -69,13 +91,13 @@
     def gather(i, carry):
         for g in range(tall // 8):
             if g == 0:
-                body = up_ref[i]
+                body = up_ref[i, :channels]
             elif g == tall // 8 - 1:
-                body = down_ref[i]
+                body = down_ref[i, :channels]
             else:
                 body = mid_ref[8 * (g - 1) + i]
-            from_right = pltpu.roll(right_ref[g].astype(jnp.float32), (128 - EDGE_COLS * i) % 128, 1)
-            from_left = pltpu.roll(left_ref[g].astype(jnp.float32), (240 - EDGE_COLS * i) % 128, 1)
+            from_right = pltpu.roll(right_ref[channels * g : channels * (g + 1)].astype(jnp.float32), (128 - EDGE_COLS * i) % 128, 1)
+            from_left = pltpu.roll(left_ref[channels * g : channels * (g + 1)].astype(jnp.float32), (240 - EDGE_COLS * i) % 128, 1)
             side = jnp.where(lanes < EDGE_COLS, from_right, jnp.where(lanes >= 128 - EDGE_COLS, from_left, 0.0))
             body = body.astype(jnp.float32)
             row = 8 * g + i
@@ -180,24 +202,36 @@
     return lax.ppermute(cells, axis, [(i + 1, i) for i in range(ends)])
 
 
-def teacher_rows(teacher_feats, teacher_probs):
+def share_rows(teacher_feats, teacher_probs, student):
     rows = teacher_feats.shape[1]
     high = lax.reduce_precision(teacher_probs, 8, 7)
     low = teacher_probs - high
     mid = jnp.concatenate(
         [teacher_feats, high.astype(jnp.bfloat16), low.astype(jnp.bfloat16)], axis=0
     ).transpose(1, 0, 2)
-    return mid, pass_on(mid[rows - EDGE_ROWS :], "row", 1), pass_on(mid[:EDGE_ROWS], "row", -1)
-
-
-def refine(mid, up, down, feat_channels, classes):
+
+    def message(first, row):
+        return jnp.concatenate(
+            [mid[first : first + EDGE_ROWS], student[row].reshape(EDGE_ROWS, -1, student.shape[2])], axis=1
+        )
+
+    up = pass_on(message(rows - EDGE_ROWS, rows - 1), "row", 1)
+    down = pass_on(message(0, 0), "row", -1)
+    return mid, up, down
+
+
+def share_cols(mid, up, down, student):
+    rows, channels, _ = mid.shape
+    groups = rows // 8 + 2
+    edge = jax.ShapeDtypeStruct((groups * channels + student.shape[1], 128), jnp.bfloat16)
+    to_left, to_right = pl.pallas_call(
+        edges_kernel, out_shape=(edge, edge), name="edges", compiler_params=vmem_of(16), cost_estimate=cost_of(2)
+    )(up, mid, down, student)
+    return pass_on(to_right, COL, 1), pass_on(to_left, COL, -1)
+
+
+def refine(mid, up, down, left, right, feat_channels, classes):
     rows, _, cols = mid.shape
-    channels = mid.shape[1]
-    groups = (rows + 2 * EDGE_ROWS) // 8
-    edge = jax.ShapeDtypeStruct((groups, channels, 128), jnp.bfloat16)
-    to_left, to_right = pl.pallas_call(edges_kernel, out_shape=(edge, edge), name="edges", compiler_params=vmem_of(12), cost_estimate=cost_of(1))(up, mid, down)
-    left = pass_on(to_right, COL, 1)
-    right = pass_on(to_left, COL, -1)
     place = jnp.stack([lax.axis_index("row") * rows, lax.axis_index(COL) * cols]).astype(jnp.int32)
     tall = rows + 2 * EDGE_ROWS
     vmem = pl.BlockSpec(memory_space=pltpu.VMEM)
@@ -229,11 +263,9 @@
     return current, weights
 
 
-def finish(current, weights, cols):
+def finish(current, weights, cols, up, down):
     rows, classes, _ = current.shape
     tall = rows + 2 * EDGE_ROWS
-    up = pass_on(current[rows - EDGE_ROWS :], "row", 1)
-    down = pass_on(current[:EDGE_ROWS], "row", -1)
     refined = pl.pallas_call(
         finish_kernel,
         out_shape=jax.ShapeDtypeStruct((rows, classes, cols), jnp.float32),
@@ -337,28 +369,20 @@
 
 
 def unit_edges_kernel(up_ref, mid_ref, down_ref, left_ref, right_ref):
-    rows, channels, cols = mid_ref.shape
-    lanes = lane_of((channels, 128))
-    left = jnp.zeros((channels, 128), jnp.float32)
-    right = jnp.zeros((channels, 128), jnp.float32)
-    for i in range(rows + 2):
-        source = up_ref.at[0] if i == 0 else down_ref.at[0] if i == rows + 1 else mid_ref.at[i - 1]
-        first = source[:, :128].astype(jnp.float32)
-        last = source[:, cols - 128 :].astype(jnp.float32)
-        left = jnp.where(lanes == i, pltpu.roll(first, i, 1), left)
-        right = jnp.where(lanes == i, pltpu.roll(last, i + 1, 1), right)
+    sources = [up_ref.at[0]] + [mid_ref.at[i] for i in range(mid_ref.shape[0])] + [down_ref.at[0]]
+    left, right = border_cells(sources, mid_ref.shape[1:])
     left_ref[...] = left.astype(left_ref.dtype)
     right_ref[...] = right.astype(right_ref.dtype)
 
 
-def side_sums(side_ref, weights):
-    side = side_ref[...].astype(jnp.float32)
+def side_sums(side, weights):
+    side = side.astype(jnp.float32)
     moved = [pltpu.roll(side, (128 - a) % 128, 1).astype(jnp.bfloat16) for a in range(3)]
     return jnp.dot(weights, jnp.concatenate(moved, axis=0), preferred_element_type=jnp.float32)
 
 
 def conv_start(
-    up_ref, mid_ref, down_ref, left_ref, right_ref, taps_ref, padded, left_sum, right_sum, weights_ref, forward
+    up_ref, mid_ref, down_ref, left_ref, right_ref, taps_ref, padded, left_sum, right_sum, weights_ref
 ):
     rows, channels, _ = mid_ref.shape
     out = weights_ref.shape[0] // 3
@@ -367,13 +391,13 @@
     def _():
         for b in range(3):
             for a in range(3):
-                tap = taps_ref[3 * a + b].T if forward else taps_ref[3 * (2 - a) + (2 - b)]
+                tap = taps_ref[3 * (2 - a) + (2 - b)]
                 weights_ref[out * b : out * (b + 1), channels * a : channels * (a + 1)] = tap
         padded[0] = up_ref[0]
         padded[pl.ds(1, rows)] = mid_ref[...]
         padded[rows + 1] = down_ref[0]
-        left_sum[...] = side_sums(left_ref, weights_ref[:out])
-        right_sum[...] = side_sums(right_ref, weights_ref[2 * out :])
+        left_sum[...] = side_sums(left_ref[...], weights_ref[:out])
+        right_sum[...] = side_sums(right_ref[...], weights_ref[2 * out :])
 
 
 def conv_row(row, weights_ref, padded, left_sum, right_sum):
@@ -394,22 +418,67 @@
 STEP_ROWS = 2
 
 
-def forward_kernel(
-    up_ref, mid_ref, down_ref, left_ref, right_ref, taps_ref, class_ref,
-    slope_ref, hidden_ref, guess_ref, padded, left_sum, right_sum, weights_ref,
+def joined(parts, out):
+    cols = parts.shape[1]
+    lanes = lane_of((out, cols))
+    before = jnp.where(lanes == 0, 0.0, pltpu.roll(parts[:out], 1, 1))
+    after = jnp.where(lanes == cols - 1, 0.0, pltpu.roll(parts[2 * out :], cols - 1, 1))
+    return parts[out : 2 * out] + (before + after)
+
+
+def convolve_kernel(mid_ref, taps_ref, pre_ref, weights_ref, padded):
+    rows, channels, cols = mid_ref.shape
+    out = weights_ref.shape[0] // 3
+
+    @pl.when(pl.program_id(0) == 0)
+    def _():
+        for b in range(3):
+            for a in range(3):
+                weights_ref[out * b : out * (b + 1), channels * a : channels * (a + 1)] = taps_ref[3 * a + b].T
+        padded[0] = jnp.zeros((channels, cols), padded.dtype)
+        padded[pl.ds(1, rows)] = mid_ref[...]
+        padded[rows + 1] = jnp.zeros((channels, cols), padded.dtype)
+
+    for k in range(STEP_ROWS):
+        row = pl.program_id(0) * STEP_ROWS + k
+        stack = jnp.concatenate([padded[row], padded[row + 1], padded[row + 2]], axis=0)
+        pre_ref[k] = joined(jnp.dot(weights_ref[...], stack, preferred_element_type=jnp.float32), out)
+
+
+def activate_kernel(
+    up_ref, down_ref, left_ref, right_ref, weights_ref, class_ref, pre_ref,
+    slope_ref, hidden_ref, guess_ref, left_sum, right_sum, borders, *, skip,
 ):
-    conv_start(
-        up_ref, mid_ref, down_ref, left_ref, right_ref, taps_ref, padded, left_sum, right_sum, weights_ref, True
-    )
+    out, channels = weights_ref.shape[0] // 3, weights_ref.shape[1] // 3
+    step = pl.program_id(0)
+
+    @pl.when(step == 0)
+    def _():
+        left_sum[...] = side_sums(left_ref[-channels:], weights_ref[:out])
+        right_sum[...] = side_sums(right_ref[-channels:], weights_ref[2 * out :])
+        for index, ref in enumerate((up_ref, down_ref)):
+            taps = weights_ref[:, 2 * channels * index : 2 * channels * index + channels]
+            parts = jnp.dot(taps, packed_row(ref, skip), preferred_element_type=jnp.float32)
+            borders[index] = joined(parts, out)
+
+    lanes = lane_of((out, 128))
     for k in range(STEP_ROWS):
-        pre_act = conv_row(pl.program_id(0) * STEP_ROWS + k, weights_ref, padded, left_sum, right_sum)
+        row = step * STEP_ROWS + k
+        left = jnp.where(lanes == 0, pltpu.roll(left_sum[...], (128 - row) % 128, 1), 0.0)
+        right = jnp.where(lanes == 127, pltpu.roll(right_sum[...], 127 - row, 1), 0.0)
+        pre_act = pre_ref[k]
+        pre_act = jnp.concatenate([pre_act[:, :128] + left, pre_act[:, 128:] + right], axis=1)
+        if k == 0:
+            pre_act = pre_act + jnp.where(step == 0, borders[0], 0.0)
+        if k == STEP_ROWS - 1:
+            pre_act = pre_act + jnp.where(step == pl.num_programs(0) - 1, borders[1], 0.0)
         logistic = 0.5 * jnp.tanh(0.5 * pre_act) + 0.5
         silu = pre_act * logistic
         slope_ref[k] = logistic + silu * (1.0 - logistic)
         hidden = silu.astype(jnp.bfloat16)
         hidden_ref[k] = hidden
         logit = jnp.dot(class_ref[...], hidden, preferred_element_type=jnp.float32)
-        guess_ref[k] = jax.nn.sigmoid(logit)
+        guess_ref[k] = 0.5 * jnp.tanh(0.5 * logit) + 0.5
 
 
 def back_kernel(guess_ref, refined_ref, slope_ref, class_ref, back_ref, error_ref):
@@ -427,14 +496,14 @@
     core_ref, up_ref, mid_ref, down_ref, left_ref, right_ref, back_ref, hidden_ref, error_ref,
     keep_ref, send_ref, padded, first_cols, last_cols, conv_ref, class_ref,
 ):
-    rows, _, cols = mid_ref.shape
+    rows, channels, cols = mid_ref.shape
     step = pl.program_id(0)
 
     @pl.when(step == 0)
     def _():
-        padded[0] = up_ref[0]
+        padded[0] = packed_row(up_ref, up_ref.shape[1] - channels // EDGE_ROWS)
         padded[pl.ds(1, rows)] = mid_ref[...]
-        padded[rows + 1] = down_ref[0]
+        padded[rows + 1] = packed_row(down_ref, down_ref.shape[1] - channels // EDGE_ROWS)
         conv_ref[...] = jnp.zeros(conv_ref.shape, jnp.float32)
         class_ref[...] = jnp.zeros(class_ref.shape, jnp.float32)
         first_cols[...] = jnp.zeros(first_cols.shape, jnp.float32)
@@ -466,7 +535,7 @@
     def _():
         hidden = back_ref.shape[1]
         for side_ref, cells, place in ((left_ref, first_cols, 0), (right_ref, last_cols, 2 * hidden)):
-            side = side_ref[...].astype(jnp.float32)
+            side = side_ref[-channels:].astype(jnp.float32)
             moved = [pltpu.roll(side, (1 - a) % 128, 1).astype(jnp.bfloat16) for a in range(3)]
             conv_ref[:, pl.ds(place, hidden)] += lax.dot_general(
                 jnp.concatenate(moved, axis=0), cells[...].astype(jnp.bfloat16), CONTRACT_LAST,
@@ -480,11 +549,15 @@
     up_ref, mid_ref, down_ref, left_ref, right_ref, taps_ref, out_ref, padded, left_sum, right_sum, weights_ref
 ):
     conv_start(
-        up_ref, mid_ref, down_ref, left_ref, right_ref, taps_ref, padded, left_sum, right_sum, weights_ref, False
+        up_ref, mid_ref, down_ref, left_ref, right_ref, taps_ref, padded, left_sum, right_sum, weights_ref
     )
     for k in range(STEP_ROWS):
         row = pl.program_id(0) * STEP_ROWS + k
         out_ref[k] = conv_row(row, weights_ref, padded, left_sum, right_sum).astype(out_ref.dtype)
+
+
+def in_hbm(*arrays):
+    return tuple(pltpu.with_memory_space_constraint(a, pltpu.HBM) for a in arrays)
 
 
 def whole(array):
@@ -539,23 +612,32 @@
     hidden_size, classes = class_weight.shape
     pixel_count = float(rows * cols)
     student = student_feats.transpose(1, 0, 2)
-    student_up, student_down = unit_rows(student)
-    mid, up, down = teacher_rows(teacher_feats, teacher_probs)
-    halo = (student_up, student, student_down) + unit_cols(student, student_up, student_down)
     f32, bf16 = jnp.float32, jnp.bfloat16
+    mid, up, down = share_rows(teacher_feats, teacher_probs, student)
+    pre_act, stacked = row_call(
+        convolve_kernel, rows, (student, conv_weight), [False] * 2,
+        [
+            jax.ShapeDtypeStruct((rows, hidden_size, cols), f32),
+            jax.ShapeDtypeStruct((3 * hidden_size, 3 * channels), bf16),
+        ],
+        [True, False], [pltpu.VMEM((rows + 2, channels, cols), bf16)], 16, 9,
+    )
+    left, right = share_cols(mid, up, down, student)
+    halo = (up, student, down, left, right)
+    current, weights = refine(mid, up, down, left, right, teacher_feats.shape[0], classes)
+    current_rows = pass_on(current[rows - EDGE_ROWS :], "row", 1), pass_on(current[:EDGE_ROWS], "row", -1)
     slope, hidden, guess = row_call(
-        forward_kernel, rows,
-        halo + (conv_weight, class_weight.T), [False] * 7,
+        functools.partial(activate_kernel, skip=mid.shape[1]), rows,
+        (up, down, left, right, stacked, class_weight.T, pre_act), [False] * 6 + [True],
         [
             jax.ShapeDtypeStruct((rows, hidden_size, cols), f32),
             jax.ShapeDtypeStruct((rows, hidden_size, cols), bf16),
             jax.ShapeDtypeStruct((rows, classes, cols), f32),
         ],
-        [True] * 3, conv_scratch(rows, channels, cols, hidden_size), 16, 12,
+        [True] * 3,
+        [pltpu.VMEM((hidden_size, 128), f32)] * 2 + [pltpu.VMEM((2, hidden_size, cols), f32)], 16, 7,
     )
-    up, down, guess = lax.optimization_barrier((up, down, guess))
-    current, weights = refine(mid, up, down, teacher_feats.shape[0], classes)
-    refined = finish(current, weights, cols)
+    refined = finish(current, weights, cols, *current_rows)
     back, error = row_call(
         back_kernel, rows, (guess, refined, slope, class_weight), [True, True, True, False],
         [
@@ -581,7 +663,7 @@
     back_left, back_right, packed = lax.optimization_barrier(back_cols + (packed,))
     (feature_grad,) = row_call(
         feature_kernel, rows,
-        (back_up, back, back_down, back_left, back_right, conv_weight), [False] * 6,
+        in_hbm(back_up, back, back_down, back_left, back_right, conv_weight), [False] * 6,
         [jax.ShapeDtypeStruct((rows, channels, cols), bf16)],
         [True], conv_scratch(rows, hidden_size, cols, channels), 16, 8,
     )

time: 180 us -> 165 us (0.917)
  local copies, waits for them, and re-layouts: 17.1 us -> 10.9 us
  waiting for transfers between devices: 19.2 us -> 15.6 us
  blocking collectives: 22.3 us -> 20.2 us
    ppermute x7 -> x5, waiting for transfers between devices: 17.7 us -> 11.3 us  [pass_on(): return lax.ppermute(cells, axis, [(i + 1, i) for i in range(ends)])]
    unnamed x59 -> x35, local copies, waits for them, and re-layouts: 16 us -> 10.7 us
    ppermute x7 -> x5, starting transfers between devices: 10.9 us -> 7.72 us  [pass_on(): return lax.ppermute(cells, axis, [(i + 1, i) for i in range(ends)])]
    all_to_all x1, waiting for transfers between devices: 0.73 us -> 3.24 us  [local_step(): lax.all_to_all(packed, CHIPS, split_axis=0, concat_axis=0, tiled=True)]
    all_to_all x1, starting transfers between devices: 12.2 us -> 14.6 us  [local_step(): lax.all_to_all(packed, CHIPS, split_axis=0, concat_axis=0, tiled=True)]
    all_to_all x1, blocking collectives: 22.3 us -> 20.2 us  [gather_all(): own = lax.all_to_all(spread, CHIPS, split_axis=0, concat_axis=0, tiled=True)]
    ppermute x7 -> x5, starting transfers between devices: 32 us -> 31.6 us  [pass_on(): return lax.ppermute(cells, axis, [(i, i + 1) for i in range(ends)])]
    pallas_call x4 -> x5, Pallas kernels: 33.8 us -> 34.1 us  [row_call(): pl.pallas_call(kernel, grid=(rows // STEP_ROWS,), in_specs=[pl.BlockSpec(...]
  transfers between devices with their start and end apart: 17 -> 13, of which waited for: 8 -> 5; matrix products, arithmetic and copies ran while one was open for 4% -> 3% of each run, Pallas kernels for 18% -> 20%
where the time goes in v3:
time: 165 us; the launch traced here: 164 us
  Pallas kernels  56.1 us (34%)
  starting transfers between devices  54 us (33%)
  blocking collectives  20.2 us (12%)
  waiting for transfers between devices  15.6 us (9%)
  local copies, waits for them, and re-layouts  10.9 us (7%)
  other arithmetic  4.68 us (3%)
  between operations  2.55 us (2%)
    pallas_call x5, Pallas kernels, row_call(): pl.pallas_call(kernel, grid=(rows // STEP_ROWS,), in_specs=[pl.BlockSpec(...  34.1 us
    ppermute x5, starting transfers between devices, pass_on(): return lax.ppermute(cells, axis, [(i, i + 1) for i in range(ends)])  31.6 us
    all_to_all x1, blocking collectives, gather_all(): own = lax.all_to_all(spread, CHIPS, split_axis=0, concat_axis=0, tiled=True)  20.2 us
    pallas_call x1, Pallas kernels, refine(): pl.pallas_call(functools.partial(affinity_kernel, full_rows=rows * lax.ax...  14.9 us
    all_to_all x1, starting transfers between devices, local_step(): lax.all_to_all(packed, CHIPS, split_axis=0, concat_axis=0, tiled=True)  14.6 us
    ppermute x5, waiting for transfers between devices, pass_on(): return lax.ppermute(cells, axis, [(i + 1, i) for i in range(ends)])  11.3 us
    unnamed x35, local copies, waits for them, and re-layouts  10.7 us
    ppermute x5, starting transfers between devices, pass_on(): return lax.ppermute(cells, axis, [(i + 1, i) for i in range(ends)])  7.72 us
  transfers between devices with their start and end apart: 13, of which 5 were waited for; matrix products, arithmetic and copies ran while one was open for 3% of the time, Pallas kernels for 20%

profile of v3, /device:TPU:1, one launch (start us, length us, event | category | flops | bytes accessed | tf_op | source)
XLA Modules:
  0.0 164.1 jit_solution(12666877209003600748)
XLA Ops:
  2.9 1.5 copy-done.12
  6.5 4.7 %collective-permute-start = (bf16[8,112,256]{2,1,0:T(8,128)(2,1)S(1)}, bf16[8,112,256]{2,1,0:T(8,128)(2,1)S(1)}, u32[]{:S(2)}, u32[]{:S(2)}) collective-permute-start(bf16[8,112,256]{2,1,0:T(8,128)(2,1)S(1)} %pad_maximum_fusion), channel_id=1, source_target_pairs={{0,16},{16,32},{32,48},{48,64},{64,80},{80,96},{96,112},{1,17},{17... | collective-permute-start | bytes 1376264 | tf_op jit(solution)/shard_map/ppermute | solution.py:201
  11.3 7.7 %collective-permute-done.1.down_ref = bf16[8,112,256]{2,1,0:T(8,128)(2,1)S(1)} collective-permute-done((bf16[8,112,256]{2,1,0:T(8,128)(2,1)S(1)}, bf16[8,112,256]{2,1,0:T(8,128)(2,1)S(1)}, u32[]{:S(2)}, u32[]{:S(2)}) %collective-permute-start.1) | collective-permute-done | bytes 458784 | tf_op jit(solution)/shard_map/ppermute | solution.py:202
  20.0 1.7 %edges.1 = (bf16[576,128]{1,0:T(8,128)(2,1)}, bf16[576,128]{1,0:T(8,128)(2,1)}) custom-call(bf16[8,112,256]{2,1,0:T(8,128)(2,1)S(1)} %collective-permute-done.up_ref, bf16[16,80,256]{2,1,0:T(8,128)(2,1)S(1)} %maximum_bitcast_fusion.mid_ref, bf16[8,112,256]{2,1,0:T(8,128)(2,1)S(1)} %collective-permute-done.1.down_ref, bf16[16,256,256]{2,1,0:T(8,128)(2,1)S(1)} %bitcast.18), custom_call_target="tpu_custom_call" | custom-call | flops 2000000000 | bytes 6000000 | tf_op jit(solution)/shard_map/edges/pallas_call | solution.py:227
  21.7 6.7 %collective-permute-start.2 = (bf16[576,128]{1,0:T(8,128)(2,1)}, bf16[576,128]{1,0:T(8,128)(2,1)S(1)}, u32[]{:S(2)}, u32[]{:S(2)}) collective-permute-start(bf16[576,128]{1,0:T(8,128)(2,1)} %get-tuple-element.29), channel_id=1, source_target_pairs={{0,1},{1,2},{2,3},{3,4},{4,5},{5,6},{6,7},{7,8},{8,9},{9,10},{10,1... | collective-permute-start | bytes 442376 | tf_op jit(solution)/shard_map/ppermute | solution.py:201
  28.4 1.9 %collective-permute-start.3 = (bf16[576,128]{1,0:T(8,128)(2,1)}, bf16[576,128]{1,0:T(8,128)(2,1)}, u32[]{:S(2)}, u32[]{:S(2)}) collective-permute-start(bf16[576,128]{1,0:T(8,128)(2,1)} %get-tuple-element.30), channel_id=1, source_target_pairs={{1,0},{2,1},{3,2},{4,3},{5,4},{6,5},{7,6},{8,7},{9,8},{10,9},{11,1... | collective-permute-start | bytes 442376 | tf_op jit(solution)/shard_map/ppermute | solution.py:202
  30.4 7.9 %shard_map.84 = (f32[16,256,256]{2,1,0:T(8,128)S(1)}, bf16[768,768]{1,0:T(8,128)(2,1)S(1)}) custom-call(bf16[16,256,256]{2,1,0:T(8,128)(2,1)S(1)} %bitcast.19, bf16[9,256,256]{2,1,0:T(8,128)(2,1)S(1)} %copy-done.2), custom_call_target="tpu_custom_call" | custom-call | flops 8999999488 | bytes 27000000 | tf_op jit(solution)/shard_map/pallas_call | solution.py:595
  38.3 1.9 %copy-done.8 = f32[16,256,256]{2,1,0:T(8,128)} copy-done((f32[16,256,256]{2,1,0:T(8,128)}, f32[16,256,256]{2,1,0:T(8,128)S(1)}, u32[]{:S(2)}) %copy-start.8) | copy-done | bytes 4194328
  42.5 14.9 %affinity.1 = (f32[16,8,384]{2,1,0:T(8,128)S(1)}, f32[25,24,384]{2,1,0:T(8,128)S(1)}) custom-call(s32[2]{0:T(128)S(1)} %pad_add_fusion.place_ref, bf16[8,112,256]{2,1,0:T(8,128)(2,1)S(1)} %copy-done.4, bf16[16,80,256]{2,1,0:T(8,128)(2,1)S(1)} %maximum_bitcast_fusion.mid_ref, bf16[8,112,256]{2,1,0:T(8,128)(2,1)S(1)} %collective-permute-done.1.down_ref, ...), custom_call_target="tpu_custom_call" | custom-call | flops 12000000000 | bytes 36000000 | tf_op jit(solution)/shard_map/affinity/pallas_call | solution.py:238
  57.4 9.0 %collective-permute-start.4 = (f32[8,8,384]{2,1,0:T(8,128)S(1)}, f32[8,8,384]{2,1,0:T(8,128)S(1)}, u32[]{:S(2)}, u32[]{:S(2)}) collective-permute-start(f32[8,8,384]{2,1,0:T(8,128)S(1)} %get-tuple-element.71), channel_id=1, source_target_pairs={{0,16},{16,32},{32,48},{48,64},{64,80},{80,96},{96,112},{1,17},{17... | collective-permute-start | bytes 294920 | tf_op jit(solution)/shard_map/ppermute | solution.py:201
  67.7 5.0 %shard_map.85 = (f32[16,256,256]{2,1,0:T(8,128)S(1)}, bf16[16,256,256]{2,1,0:T(8,128)(2,1)S(1)}, f32[16,8,256]{2,1,0:T(8,128)S(1)}) custom-call(bf16[8,112,256]{2,1,0:T(8,128)(2,1)S(1)} %copy-done.5, bf16[8,112,256]{2,1,0:T(8,128)(2,1)S(1)} %collective-permute-done.1.down_ref, bf16[576,128]{1,0:T(8,128)(2,1)S(1)} %collective-permute-done.2.left_ref, ...), custom_call_target="tpu_custom_call" | custom-call | flops 7000000000 | bytes 21000000 | tf_op jit(solution)/shard_map/pallas_call | solution.py:595
  74.0 3.0 %finish.1.refined_ref = f32[16,8,256]{2,1,0:T(8,128)S(1)} custom-call(f32[25,24,384]{2,1,0:T(8,128)S(1)} %get-tuple-element.31.weights_ref, f32[8,8,384]{2,1,0:T(8,128)S(1)} %collective-permute-done.4.up_ref, f32[16,8,384]{2,1,0:T(8,128)S(1)} %get-tuple-element.32.mid_ref, f32[8,8,384]{2,1,0:T(8,128)S(1)} %collective-permute-done.5.down_ref), custom_call_target="tpu_custom_call" | custom-call | flops 4000000000 | bytes 12000000 | tf_op jit(solution)/shard_map/finish/pallas_call | solution.py:269
  77.1 1.7 %shard_map.86 = (bf16[16,256,256]{2,1,0:T(8,128)(2,1)S(1)}, bf16[16,8,256]{2,1,0:T(8,128)(2,1)S(1)}) custom-call(f32[16,8,256]{2,1,0:T(8,128)S(1)} %get-tuple-element.35.guess_ref, f32[16,8,256]{2,1,0:T(8,128)S(1)} %finish.1.refined_ref, f32[16,256,256]{2,1,0:T(8,128)S(1)} %get-tuple-element.36.slope_ref, bf16[256,8]{1,0:T(8,128)(2,1)S(1)} %copy.20.class_ref), custom_call_target="tpu_custom_call" | custom-call | flops 2000000000 | bytes 6000000 | tf_op jit(solution)/shard_map/pallas_call | solution.py:595
  78.8 5.0 %collective-permute-start.6 = (bf16[1,256,256]{2,1,0:T(8,128)(2,1)S(1)}, bf16[1,256,256]{2,1,0:T(8,128)(2,1)S(1)}, u32[]{:S(2)}, u32[]{:S(2)}) collective-permute-start(bf16[1,256,256]{2,1,0:T(8,128)(2,1)S(1)} %get-tuple-element.65), channel_id=1, source_target_pairs={{0,16},{16,32},{32,48},{48,64},{64,80},{80,96},{96,112},{1,17},{17... | collective-permute-start | bytes 393224 | tf_op jit(solution)/shard_map/ppermute | solution.py:201
  85.1 9.5 %shard_map.87 = (f32[64,40,128]{2,1,0:T(8,128)S(1)}, f32[64,40,128]{2,1,0:T(8,128)S(1)}) custom-call(s32[1]{0:T(128)} %bitcast.8.core_ref, bf16[8,112,256]{2,1,0:T(8,128)(2,1)S(1)} %copy-done.5, bf16[16,256,256]{2,1,0:T(8,128)(2,1)S(1)} %bitcast.20, bf16[8,112,256]{2,1,0:T(8,128)(2,1)S(1)} %collective-permute-done.1.down_ref, ...), custom_call_target="tpu_custom_call" | custom-call | flops 8999999488 | bytes 27000000 | tf_op jit(solution)/shard_map/pallas_call | solution.py:595
  95.5 6.1 %collective-permute-start.8 = (bf16[256,128]{1,0:T(8,128)(2,1)S(1)}, bf16[256,128]{1,0:T(8,128)(2,1)S(1)}, u32[]{:S(2)}, u32[]{:S(2)}) collective-permute-start(bf16[256,128]{1,0:T(8,128)(2,1)S(1)} %get-tuple-element.43), channel_id=1, source_target_pairs={{0,1},{1,2},{2,3},{3,4},{4,5},{5,6},{6,7},{7,8},{8,9},{9,10},{10,1... | collective-permute-start | bytes 196616 | tf_op jit(solution)/shard_map/ppermute | solution.py:201
  101.6 1.9 %collective-permute-start.9 = (bf16[256,128]{1,0:T(8,128)(2,1)S(1)}, bf16[256,128]{1,0:T(8,128)(2,1)S(1)}, u32[]{:S(2)}, u32[]{:S(2)}) collective-permute-start(bf16[256,128]{1,0:T(8,128)(2,1)S(1)} %get-tuple-element.44), channel_id=1, source_target_pairs={{1,0},{2,1},{3,2},{4,3},{5,4},{6,5},{7,6},{8,7},{9,8},{10,9},{11,1... | collective-permute-start | bytes 196616 | tf_op jit(solution)/shard_map/ppermute | solution.py:202
  106.4 2.3 %collective-permute-done.9.right_ref = bf16[256,128]{1,0:T(8,128)(2,1)S(1)} collective-permute-done((bf16[256,128]{1,0:T(8,128)(2,1)S(1)}, bf16[256,128]{1,0:T(8,128)(2,1)S(1)}, u32[]{:S(2)}, u32[]{:S(2)}) %collective-permute-start.9) | collective-permute-done | bytes 65568 | tf_op jit(solution)/shard_map/ppermute | solution.py:202
  108.7 14.6 %all-to-all-start = ((f16[64,40,128]{2,1,0:T(8,128)(2,1)}), f16[64,40,128]{2,1,0:T(8,128)(2,1)S(1)}, u32[]{:S(2)}, u32[]{:S(2)}) async-start(f16[64,40,128]{2,1,0:T(8,128)(2,1)} %select_convert_fusion), calls=%async_computation | async-start | bytes 1310720 | tf_op jit(solution)/shard_map/all_to_all | solution.py:670
  123.3 10.1 %shard_map.88 = bf16[16,256,256]{2,1,0:T(8,128)(2,1)S(1)} custom-call(bf16[1,256,256]{2,1,0:T(8,128)(2,1)} %copy-done.6, bf16[16,256,256]{2,1,0:T(8,128)(2,1)} %copy-done, bf16[1,256,256]{2,1,0:T(8,128)(2,1)} %copy-done.7, bf16[256,128]{1,0:T(8,128)(2,1)} %copy-done.13, bf16[256,128]{1,0:T(8,128)(2,1)} %copy-done.14, bf16[9,256,256]{2,1,0:T(8,128)(2,1)} %taps_ref.3), custom_call_target="tpu_custom_call" | custom-call | flops 8000000000 | bytes 24000000 | tf_op jit(solution)/shard_map/pallas_call | solution.py:595
  133.4 3.2 %all-to-all-done = f16[64,40,128]{2,1,0:T(8,128)(2,1)S(1)} async-done(((f16[64,40,128]{2,1,0:T(8,128)(2,1)}), f16[64,40,128]{2,1,0:T(8,128)(2,1)S(1)}, u32[]{:S(2)}, u32[]{:S(2)}) %all-to-all-start) | async-done | bytes 655392 | tf_op jit(solution)/shard_map/all_to_all | solution.py:670
  138.5 20.2 %all_to_all.10 = f16[64,40,128]{2,1,0:T(8,128)(2,1)S(1)} all-to-all(f16[64,40,128]{2,1,0:T(8,128)(2,1)S(1)} %broadcast_in_dim.26), channel_id=1, replica_groups=mesh['row'=8,'pair'=8,'core'=2] {'row','pair'}, dimensions={0} | all-to-all | bytes 1310720 | tf_op jit(solution)/shard_map/all_to_all | solution.py:353
  159.4 2.5 %copy.22 = bf16[256,16,256]{2,1,0:T(8,128)(2,1)} copy(bf16[256,16,256]{2,0,1:T(8,128)(2,1)S(1)} %bitcast.21) | data formatting | bytes 4194304
  162.3 1.7 %place.1 = (f32[9,256,256]{2,1,0:T(8,128)}, f32[8,256]{1,0:T(8,128)}) custom-call(s32[1]{0:T(128)} %bitcast.8.core_ref, f32[64,40,128]{2,1,0:T(8,128)S(1)} %convert_multiply_fusion.1.own_ref, f32[64,40,128]{2,1,0:T(8,128)S(1)} %convert_multiply_fusion.other_ref), custom_call_target="tpu_custom_call" | custom-call | flops 2000000000 | bytes 6000000 | tf_op jit(solution)/shard_map/place/pallas_call | solution.py:356
  (69 shorter events, 16.7 us)
Async XLA Ops:
  2.8 1.6 copy-start.12
  5.2 13.7 %collective-permute-start.1 = (bf16[8,112,256]{2,1,0:T(8,128)(2,1)S(1)}, bf16[8,112,256]{2,1,0:T(8,128)(2,1)S(1)}, u32[]{:S(2)}, u32[]{:S(2)}) collective-permute-start(bf16[8,112,256]{2,1,0:T(8,128)(2,1)S(1)} %pad_maximum_fusion.1), channel_id=1, source_target_pairs={{16,0},{32,16},{48,32},{64,48},{80,64},{96,80},{112,96},{17,1},{33... | collective-permute-start | bytes 1376264 | tf_op jit(solution)/shard_map/ppermute | solution.py:202
  6.5 23.8 %copy-start.2 = (bf16[9,256,256]{2,1,0:T(8,128)(2,1)S(1)}, bf16[9,256,256]{2,1,0:T(8,128)(2,1)}, u32[]{:S(2)}) copy-start(bf16[9,256,256]{2,1,0:T(8,128)(2,1)} %taps_ref.3) | copy-start | bytes 3538948
  6.5 13.5 %collective-permute-start = (bf16[8,112,256]{2,1,0:T(8,128)(2,1)S(1)}, bf16[8,112,256]{2,1,0:T(8,128)(2,1)S(1)}, u32[]{:S(2)}, u32[]{:S(2)}) collective-permute-start(bf16[8,112,256]{2,1,0:T(8,128)(2,1)S(1)} %pad_maximum_fusion), channel_id=1, source_target_pairs={{0,16},{16,32},{32,48},{48,64},{64,80},{80,96},{96,112},{1,17},{17... | collective-permute-start | bytes 1376264 | tf_op jit(solution)/shard_map/ppermute | solution.py:201
  20.0 1.7 %copy-start.3 = (bf16[8,112,256]{2,1,0:T(8,128)(2,1)}, bf16[8,112,256]{2,1,0:T(8,128)(2,1)S(1)}, u32[]{:S(2)}) copy-start(bf16[8,112,256]{2,1,0:T(8,128)(2,1)S(1)} %collective-permute-done.up_ref) | copy-start | bytes 1376260
  21.7 19.7 %collective-permute-start.2 = (bf16[576,128]{1,0:T(8,128)(2,1)}, bf16[576,128]{1,0:T(8,128)(2,1)S(1)}, u32[]{:S(2)}, u32[]{:S(2)}) collective-permute-start(bf16[576,128]{1,0:T(8,128)(2,1)} %get-tuple-element.29), channel_id=1, source_target_pairs={{0,1},{1,2},{2,3},{3,4},{4,5},{5,6},{6,7},{7,8},{8,9},{9,10},{10,1... | collective-permute-start | bytes 442376 | tf_op jit(solution)/shard_map/ppermute | solution.py:201
  28.4 12.8 %copy-start.1 = (bf16[256,8]{0,1:T(8,128)(2,1)S(1)}, bf16[256,8]{0,1:T(8,128)(2,1)}, u32[]{:S(2)}) copy-start(bf16[256,8]{0,1:T(8,128)(2,1)} %param.9) | copy-start | bytes 12292
  28.4 13.0 %collective-permute-start.3 = (bf16[576,128]{1,0:T(8,128)(2,1)}, bf16[576,128]{1,0:T(8,128)(2,1)}, u32[]{:S(2)}, u32[]{:S(2)}) collective-permute-start(bf16[576,128]{1,0:T(8,128)(2,1)} %get-tuple-element.30), channel_id=1, source_target_pairs={{1,0},{2,1},{3,2},{4,3},{5,4},{6,5},{7,6},{8,7},{9,8},{10,9},{11,1... | collective-permute-start | bytes 442376 | tf_op jit(solution)/shard_map/ppermute | solution.py:202
  38.3 2.0 %copy-start.8 = (f32[16,256,256]{2,1,0:T(8,128)}, f32[16,256,256]{2,1,0:T(8,128)S(1)}, u32[]{:S(2)}) copy-start(f32[16,256,256]{2,1,0:T(8,128)S(1)} %get-tuple-element.34.pre_ref) | copy-start | bytes 12582916
  42.5 25.2 %copy-start.5 = (bf16[8,112,256]{2,1,0:T(8,128)(2,1)S(1)}, bf16[8,112,256]{2,1,0:T(8,128)(2,1)}, u32[]{:S(2)}) copy-start(bf16[8,112,256]{2,1,0:T(8,128)(2,1)} %copy-done.3) | copy-start | bytes 1376260
  42.5 25.2 %copy-start.9 = (f32[16,256,256]{2,1,0:T(8,128)S(1)}, f32[16,256,256]{2,1,0:T(8,128)}, u32[]{:S(2)}) copy-start(f32[16,256,256]{2,1,0:T(8,128)} %copy-done.8) | copy-start | bytes 12582916
  42.5 25.2 %copy-start.11 = (bf16[768,768]{1,0:T(8,128)(2,1)S(1)}, bf16[768,768]{1,0:T(8,128)(2,1)}, u32[]{:S(2)}) copy-start(bf16[768,768]{1,0:T(8,128)(2,1)} %copy-done.10) | copy-start | bytes 3538948
  57.4 15.4 %collective-permute-start.4 = (f32[8,8,384]{2,1,0:T(8,128)S(1)}, f32[8,8,384]{2,1,0:T(8,128)S(1)}, u32[]{:S(2)}, u32[]{:S(2)}) collective-permute-start(f32[8,8,384]{2,1,0:T(8,128)S(1)} %get-tuple-element.71), channel_id=1, source_target_pairs={{0,16},{16,32},{32,48},{48,64},{64,80},{80,96},{96,112},{1,17},{17... | collective-permute-start | bytes 294920 | tf_op jit(solution)/shard_map/ppermute | solution.py:201
  66.4 7.6 %collective-permute-start.5 = (f32[8,8,384]{2,1,0:T(8,128)S(1)}, f32[8,8,384]{2,1,0:T(8,128)S(1)}, u32[]{:S(2)}, u32[]{:S(2)}) collective-permute-start(f32[8,8,384]{2,1,0:T(8,128)S(1)} %get-tuple-element.70), channel_id=1, source_target_pairs={{16,0},{32,16},{48,32},{64,48},{80,64},{96,80},{112,96},{17,1},{33... | collective-permute-start | bytes 294920 | tf_op jit(solution)/shard_map/ppermute | solution.py:202
  78.8 16.0 %copy-start = (bf16[16,256,256]{2,1,0:T(8,128)(2,1)}, bf16[16,256,256]{2,1,0:T(8,128)(2,1)S(1)}, u32[]{:S(2)}) copy-start(bf16[16,256,256]{2,1,0:T(8,128)(2,1)S(1)} %get-tuple-element.37.back_ref.mid_ref) | copy-start | bytes 6291460
  78.8 15.8 %collective-permute-start.6 = (bf16[1,256,256]{2,1,0:T(8,128)(2,1)S(1)}, bf16[1,256,256]{2,1,0:T(8,128)(2,1)S(1)}, u32[]{:S(2)}, u32[]{:S(2)}) collective-permute-start(bf16[1,256,256]{2,1,0:T(8,128)(2,1)S(1)} %get-tuple-element.65), channel_id=1, source_target_pairs={{0,16},{16,32},{32,48},{48,64},{64,80},{80,96},{96,112},{1,17},{17... | collective-permute-start | bytes 393224 | tf_op jit(solution)/shard_map/ppermute | solution.py:201
  83.8 10.8 %collective-permute-start.7 = (bf16[1,256,256]{2,1,0:T(8,128)(2,1)S(1)}, bf16[1,256,256]{2,1,0:T(8,128)(2,1)S(1)}, u32[]{:S(2)}, u32[]{:S(2)}) collective-permute-start(bf16[1,256,256]{2,1,0:T(8,128)(2,1)S(1)} %get-tuple-element.64), channel_id=1, source_target_pairs={{16,0},{32,16},{48,32},{64,48},{80,64},{96,80},{112,96},{17,1},{33... | collective-permute-start | bytes 393224 | tf_op jit(solution)/shard_map/ppermute | solution.py:202
  94.6 8.9 %collective-permute-start.10 = (f32[64,40,128]{2,1,0:T(8,128)S(1)}, f32[64,40,128]{2,1,0:T(8,128)S(1)}, u32[]{:S(2)}, u32[]{:S(2)}) collective-permute-start(f32[64,40,128]{2,1,0:T(8,128)S(1)} %get-tuple-element.46), channel_id=1, source_target_pairs={{0,1},{1,0},{2,3},{3,2},{4,5},{5,4},{6,7},{7,6},{8,9},{9,8},{10,11... | collective-permute-start | bytes 3932168 | tf_op jit(solution)/shard_map/ppermute | solution.py:660
  95.5 10.9 %collective-permute-start.8 = (bf16[256,128]{1,0:T(8,128)(2,1)S(1)}, bf16[256,128]{1,0:T(8,128)(2,1)S(1)}, u32[]{:S(2)}, u32[]{:S(2)}) collective-permute-start(bf16[256,128]{1,0:T(8,128)(2,1)S(1)} %get-tuple-element.43), channel_id=1, source_target_pairs={{0,1},{1,2},{2,3},{3,4},{4,5},{5,6},{6,7},{7,8},{8,9},{9,10},{10,1... | collective-permute-start | bytes 196616 | tf_op jit(solution)/shard_map/ppermute | solution.py:201
  101.6 7.1 %collective-permute-start.9 = (bf16[256,128]{1,0:T(8,128)(2,1)S(1)}, bf16[256,128]{1,0:T(8,128)(2,1)S(1)}, u32[]{:S(2)}, u32[]{:S(2)}) collective-permute-start(bf16[256,128]{1,0:T(8,128)(2,1)S(1)} %get-tuple-element.44), channel_id=1, source_target_pairs={{1,0},{2,1},{3,2},{4,3},{5,4},{6,5},{7,6},{8,7},{9,8},{10,9},{11,1... | collective-permute-start | bytes 196616 | tf_op jit(solution)/shard_map/ppermute | solution.py:202
  106.4 16.9 %copy-start.13 = (bf16[256,128]{1,0:T(8,128)(2,1)}, bf16[256,128]{1,0:T(8,128)(2,1)S(1)}, u32[]{:S(2)}) copy-start(bf16[256,128]{1,0:T(8,128)(2,1)S(1)} %collective-permute-done.8.left_ref) | copy-start | bytes 196612
  108.7 14.6 %copy-start.14 = (bf16[256,128]{1,0:T(8,128)(2,1)}, bf16[256,128]{1,0:T(8,128)(2,1)S(1)}, u32[]{:S(2)}) copy-start(bf16[256,128]{1,0:T(8,128)(2,1)S(1)} %collective-permute-done.9.right_ref) | copy-start | bytes 196612
  108.7 27.9 %all-to-all-start = ((f16[64,40,128]{2,1,0:T(8,128)(2,1)}), f16[64,40,128]{2,1,0:T(8,128)(2,1)S(1)}, u32[]{:S(2)}, u32[]{:S(2)}) async-start(f16[64,40,128]{2,1,0:T(8,128)(2,1)} %select_convert_fusion), calls=%async_computation | async-start | bytes 1310720 | tf_op jit(solution)/shard_map/all_to_all | solution.py:670
  158.7 3.4 %collective-permute-start.11 = (f16[64,40,128]{2,1,0:T(8,128)(2,1)S(1)}, f16[64,40,128]{2,1,0:T(8,128)(2,1)S(1)}, u32[]{:S(2)}, u32[]{:S(2)}) collective-permute-start(f16[64,40,128]{2,1,0:T(8,128)(2,1)S(1)} %all_to_all.10), channel_id=1, source_target_pairs={{0,1},{1,0},{2,3},{3,2},{4,5},{5,4},{6,7},{7,6},{8,9},{9,8},{10,11... | collective-permute-start | bytes 1966088 | tf_op jit(solution)/shard_map/ppermute | solution.py:354
  (4 other events, 3.7 us)

commit v4 on v3

--- a/solution.py
+++ b/solution.py
@@ -13,6 +13,7 @@
 EDGE_ROWS = 8
 EDGE_COLS = 16
 SPAN = 384
+GROUP = 4
 PAIR_TAPS = [tap for s in (1, 2, 4) for tap in ((0, s), (s, -s), (s, 0), (s, s))]
 
 
@@ -111,21 +112,25 @@
     lax.fori_loop(0, 8, gather, 0)
     pairs[:, tall - 8 :, :] = jnp.zeros((len(PAIR_TAPS), 8, SPAN), jnp.float32)
 
-    def distances(row, carry):
-        sums = [None for _ in PAIR_TAPS]
-        for c in range(feat_channels // 8):
-            here = feats[row, 8 * c : 8 * c + 8, :]
-            there = {0: here}
-            for index, (off_y, off_x) in enumerate(PAIR_TAPS):
-                if off_y not in there:
-                    there[off_y] = feats[row + off_y, 8 * c : 8 * c + 8, :]
-                product = here * shifted_by(there[off_y], off_x)
-                sums[index] = product if c == 0 else sums[index] + product
-        for index in range(len(PAIR_TAPS)):
-            pairs[index, pl.ds(row, 1), :] = jnp.sum(sums[index], axis=0, keepdims=True)
-        return carry
-
-    lax.fori_loop(0, tall - 4, distances, 0)
+    for ring, radius in enumerate((1, 2, 4)):
+
+        def products(step, carry, ring=ring, radius=radius):
+            rows_at = [step * GROUP + g for g in range(GROUP)]
+            sums = [[None] * 4 for _ in rows_at]
+            for c in range(feat_channels // 8):
+                for g, row in enumerate(rows_at):
+                    here = feats[row, 8 * c : 8 * c + 8, :]
+                    there = feats[row + radius, 8 * c : 8 * c + 8, :]
+                    for k, (off_y, off_x) in enumerate(PAIR_TAPS[4 * ring : 4 * ring + 4]):
+                        product = here * shifted_by(there if off_y else here, off_x)
+                        sums[g][k] = product if c == 0 else sums[g][k] + product
+            totals = [[jnp.sum(cells, axis=0, keepdims=True) for cells in row_sums] for row_sums in sums]
+            for g, row in enumerate(rows_at):
+                for k in range(4):
+                    pairs[4 * ring + k, pl.ds(row, 1), :] = totals[g][k]
+            return carry
+
+        lax.fori_loop(0, (tall - 4) // GROUP, products, 0)
 
     def sizes(row, carry):
         cells = feats[row]
@@ -337,7 +342,7 @@
 
 def pack_half(values):
     marks = lax.broadcasted_iota(jnp.int32, values.shape, values.ndim - 2) == MARK_ROW
-    largest = jnp.max(jnp.where(marks, 0.0, jnp.abs(values)))
+    largest = jnp.max(jnp.where(marks, 0.0, jnp.abs(values)), axis=-2, keepdims=True)
     exponent = jnp.clip(jnp.ceil(jnp.log2(jnp.maximum(largest, 1e-30))), -100.0, 120.0)
     return jnp.where(marks, exponent, values * jnp.exp2(14.0 - exponent)).astype(jnp.float16)
 
@@ -379,40 +384,6 @@
     side = side.astype(jnp.float32)
     moved = [pltpu.roll(side, (128 - a) % 128, 1).astype(jnp.bfloat16) for a in range(3)]
     return jnp.dot(weights, jnp.concatenate(moved, axis=0), preferred_element_type=jnp.float32)
-
-
-def conv_start(
-    up_ref, mid_ref, down_ref, left_ref, right_ref, taps_ref, padded, left_sum, right_sum, weights_ref
-):
-    rows, channels, _ = mid_ref.shape
-    out = weights_ref.shape[0] // 3
-
-    @pl.when(pl.program_id(0) == 0)
-    def _():
-        for b in range(3):
-            for a in range(3):
-                tap = taps_ref[3 * (2 - a) + (2 - b)]
-                weights_ref[out * b : out * (b + 1), channels * a : channels * (a + 1)] = tap
-        padded[0] = up_ref[0]
-        padded[pl.ds(1, rows)] = mid_ref[...]
-        padded[rows + 1] = down_ref[0]
-        left_sum[...] = side_sums(left_ref[...], weights_ref[:out])
-        right_sum[...] = side_sums(right_ref[...], weights_ref[2 * out :])
-
-
-def conv_row(row, weights_ref, padded, left_sum, right_sum):
-    out = weights_ref.shape[0] // 3
-    cols = padded.shape[2]
-    stack = jnp.concatenate([padded[row], padded[row + 1], padded[row + 2]], axis=0)
-    parts = jnp.dot(weights_ref[...], stack, preferred_element_type=jnp.float32)
-    lanes = lane_of((out, 128))
-    before = pltpu.roll(parts[:out], 1, 1)
-    after = pltpu.roll(parts[2 * out :], cols - 1, 1)
-    left = pltpu.roll(left_sum[...], (128 - row) % 128, 1)
-    right = pltpu.roll(right_sum[...], 127 - row, 1)
-    before = jnp.concatenate([jnp.where(lanes == 0, left, before[:, :128]), before[:, 128:]], axis=1)
-    after = jnp.concatenate([after[:, :-128], jnp.where(lanes == 127, right, after[:, -128:])], axis=1)
-    return parts[out : 2 * out] + (before + after)
 
 
 STEP_ROWS = 2
@@ -546,14 +517,38 @@
 
 
 def feature_kernel(
-    up_ref, mid_ref, down_ref, left_ref, right_ref, taps_ref, out_ref, padded, left_sum, right_sum, weights_ref
+    up_ref, above_ref, mid_ref, below_ref, down_ref, left_ref, right_ref, taps_ref, out_ref,
+    left_sum, right_sum, weights_ref,
 ):
-    conv_start(
-        up_ref, mid_ref, down_ref, left_ref, right_ref, taps_ref, padded, left_sum, right_sum, weights_ref
-    )
+    out, channels = weights_ref.shape[0] // 3, weights_ref.shape[1] // 3
+    cols = mid_ref.shape[2]
+    step = pl.program_id(0)
+
+    @pl.when(step == 0)
+    def _():
+        for b in range(3):
+            for a in range(3):
+                tap = taps_ref[3 * (2 - a) + (2 - b)]
+                weights_ref[out * b : out * (b + 1), channels * a : channels * (a + 1)] = tap
+        left_sum[...] = side_sums(left_ref[...], weights_ref[:out])
+        right_sum[...] = side_sums(right_ref[...], weights_ref[2 * out :])
+
+    above = jnp.where(step == 0, up_ref[0], above_ref[STEP_ROWS - 1])
+    below = jnp.where(step == pl.num_programs(0) - 1, down_ref[0], below_ref[0])
+    cells = [above] + [mid_ref[k] for k in range(STEP_ROWS)] + [below]
+    lanes = lane_of((out, 128))
     for k in range(STEP_ROWS):
-        row = pl.program_id(0) * STEP_ROWS + k
-        out_ref[k] = conv_row(row, weights_ref, padded, left_sum, right_sum).astype(out_ref.dtype)
+        row = step * STEP_ROWS + k
+        parts = jnp.dot(
+            weights_ref[...], jnp.concatenate(cells[k : k + 3], axis=0), preferred_element_type=jnp.float32
+        )
+        before = pltpu.roll(parts[:out], 1, 1)
+        after = pltpu.roll(parts[2 * out :], cols - 1, 1)
+        left = pltpu.roll(left_sum[...], (128 - row) % 128, 1)
+        right = pltpu.roll(right_sum[...], 127 - row, 1)
+        before = jnp.concatenate([jnp.where(lanes == 0, left, before[:, :128]), before[:, 128:]], axis=1)
+        after = jnp.concatenate([after[:, :-128], jnp.where(lanes == 127, right, after[:, -128:])], axis=1)
+        out_ref[k] = (parts[out : 2 * out] + (before + after)).astype(out_ref.dtype)
 
 
 def in_hbm(*arrays):
@@ -580,15 +575,6 @@
         cost_estimate=cost_of(1),
     )(up, cells, down)
     return pass_on(to_right, COL, 1), pass_on(to_left, COL, -1)
-
-
-def conv_scratch(rows, channels, cols, out):
-    return [
-        pltpu.VMEM((rows + 2, channels, cols), jnp.bfloat16),
-        pltpu.VMEM((out, 128), jnp.float32),
-        pltpu.VMEM((out, 128), jnp.float32),
-        pltpu.VMEM((3 * out, 3 * channels), jnp.bfloat16),
-    ]
 
 
 def row_call(kernel, rows, args, arg_rows, outs, out_rows, scratch, vmem, micros):
@@ -661,12 +647,27 @@
     back_cols = unit_cols(back, back_up, back_down)
     packed = pack_half(keep + other)
     back_left, back_right, packed = lax.optimization_barrier(back_cols + (packed,))
-    (feature_grad,) = row_call(
-        feature_kernel, rows,
-        in_hbm(back_up, back, back_down, back_left, back_right, conv_weight), [False] * 6,
-        [jax.ShapeDtypeStruct((rows, channels, cols), bf16)],
-        [True], conv_scratch(rows, hidden_size, cols, channels), 16, 8,
-    )
+    steps = rows // STEP_ROWS
+    block = (STEP_ROWS, hidden_size, cols)
+    feature_args = in_hbm(back_up, back, back_down, back_left, back_right, conv_weight)
+    feature_grad = pl.pallas_call(
+        feature_kernel,
+        grid=(steps,),
+        in_specs=[
+            whole(back_up),
+            pl.BlockSpec(block, lambda i: (jnp.maximum(i - 1, 0), 0, 0)),
+            pl.BlockSpec(block, lambda i: (i, 0, 0)),
+            pl.BlockSpec(block, lambda i: (jnp.minimum(i + 1, steps - 1), 0, 0)),
+            whole(back_down), whole(back_left), whole(back_right), whole(conv_weight),
+        ],
+        out_specs=by_rows((rows, channels, cols)),
+        out_shape=jax.ShapeDtypeStruct((rows, channels, cols), bf16),
+        scratch_shapes=[pltpu.VMEM((channels, 128), f32)] * 2
+        + [pltpu.VMEM((3 * channels, 3 * hidden_size), bf16)],
+        name="feature",
+        compiler_params=vmem_of(16),
+        cost_estimate=cost_of(8),
+    )(feature_args[0], feature_args[1], feature_args[1], feature_args[1], *feature_args[2:])
     received = lax.all_to_all(packed, CHIPS, split_axis=0, concat_axis=0, tiled=True)
     total = jnp.sum(unpack_half(received), axis=0)
     total, feature_grad = lax.optimization_barrier((total, feature_grad))

time: 165 us -> 161 us (0.976)
    pallas_call x0 -> x1, Pallas kernels: none -> 10.2 us  [local_step(): pl.pallas_call(feature_kernel, grid=(steps,), in_specs=[whole(back_up), p...]
    pallas_call x5 -> x4, Pallas kernels: 34.1 us -> 24 us  [row_call(): pl.pallas_call(kernel, grid=(rows // STEP_ROWS,), in_specs=[pl.BlockSpec(...]
  transfers between devices with their start and end apart: 13 -> 13, of which waited for: 5 -> 5; matrix products, arithmetic and copies ran while one was open for 3% -> 3% of each run, Pallas kernels for 20% -> 21%
where the time goes in v4:
time: 161 us
  Pallas kernels  54.9 us (34%)
  starting transfers between devices  53.8 us (33%)
  blocking collectives  20.4 us (13%)
  waiting for transfers between devices  15.9 us (10%)
  local copies, waits for them, and re-layouts  10.9 us (7%)
  other arithmetic  3.55 us (2%)
    ppermute x5, starting transfers between devices, pass_on(): return lax.ppermute(cells, axis, [(i, i + 1) for i in range(ends)])  31.6 us
    pallas_call x4, Pallas kernels, row_call(): pl.pallas_call(kernel, grid=(rows // STEP_ROWS,), in_specs=[pl.BlockSpec(...  24 us
    all_to_all x1, blocking collectives, gather_all(): own = lax.all_to_all(spread, CHIPS, split_axis=0, concat_axis=0, tiled=True)  20.4 us
    all_to_all x1, starting transfers between devices, local_step(): lax.all_to_all(packed, CHIPS, split_axis=0, concat_axis=0, tiled=True)  14.4 us
    pallas_call x1, Pallas kernels, refine(): pl.pallas_call(functools.partial(affinity_kernel, full_rows=rows * lax.ax...  13.5 us
    ppermute x5, waiting for transfers between devices, pass_on(): return lax.ppermute(cells, axis, [(i + 1, i) for i in range(ends)])  12.5 us
    unnamed x35, local copies, waits for them, and re-layouts  10.7 us
    pallas_call x1, Pallas kernels, local_step(): pl.pallas_call(feature_kernel, grid=(steps,), in_specs=[whole(back_up), p...  10.2 us
  transfers between devices with their start and end apart: 13, of which 5 were waited for; matrix products, arithmetic and copies ran while one was open for 3% of the time, Pallas kernels for 21%

profile of v4, /device:TPU:1, one launch (start us, length us, event | category | flops | bytes accessed | tf_op | source)
XLA Modules:
  0.0 160.5 jit_solution(3349453154076522837)
XLA Ops:
  2.9 1.5 copy-done.12
  6.5 4.7 %collective-permute-start = (bf16[8,112,256]{2,1,0:T(8,128)(2,1)S(1)}, bf16[8,112,256]{2,1,0:T(8,128)(2,1)S(1)}, u32[]{:S(2)}, u32[]{:S(2)}) collective-permute-start(bf16[8,112,256]{2,1,0:T(8,128)(2,1)S(1)} %pad_maximum_fusion), channel_id=1, source_target_pairs={{0,16},{16,32},{32,48},{48,64},{64,80},{80,96},{96,112},{1,17},{17... | collective-permute-start | bytes 1376264 | tf_op jit(solution)/shard_map/ppermute | solution.py:206
  11.3 7.7 %collective-permute-done.1.down_ref = bf16[8,112,256]{2,1,0:T(8,128)(2,1)S(1)} collective-permute-done((bf16[8,112,256]{2,1,0:T(8,128)(2,1)S(1)}, bf16[8,112,256]{2,1,0:T(8,128)(2,1)S(1)}, u32[]{:S(2)}, u32[]{:S(2)}) %collective-permute-start.1) | collective-permute-done | bytes 458784 | tf_op jit(solution)/shard_map/ppermute | solution.py:207
  20.0 1.7 %edges.1 = (bf16[576,128]{1,0:T(8,128)(2,1)}, bf16[576,128]{1,0:T(8,128)(2,1)}) custom-call(bf16[8,112,256]{2,1,0:T(8,128)(2,1)S(1)} %collective-permute-done.up_ref, bf16[16,80,256]{2,1,0:T(8,128)(2,1)S(1)} %maximum_bitcast_fusion.mid_ref, bf16[8,112,256]{2,1,0:T(8,128)(2,1)S(1)} %collective-permute-done.1.down_ref, bf16[16,256,256]{2,1,0:T(8,128)(2,1)S(1)} %bitcast.18), custom_call_target="tpu_custom_call" | custom-call | flops 2000000000 | bytes 6000000 | tf_op jit(solution)/shard_map/edges/pallas_call | solution.py:232
  21.7 6.7 %collective-permute-start.2 = (bf16[576,128]{1,0:T(8,128)(2,1)}, bf16[576,128]{1,0:T(8,128)(2,1)S(1)}, u32[]{:S(2)}, u32[]{:S(2)}) collective-permute-start(bf16[576,128]{1,0:T(8,128)(2,1)} %get-tuple-element.29), channel_id=1, source_target_pairs={{0,1},{1,2},{2,3},{3,4},{4,5},{5,6},{6,7},{7,8},{8,9},{9,10},{10,1... | collective-permute-start | bytes 442376 | tf_op jit(solution)/shard_map/ppermute | solution.py:206
  28.5 1.9 %collective-permute-start.3 = (bf16[576,128]{1,0:T(8,128)(2,1)}, bf16[576,128]{1,0:T(8,128)(2,1)}, u32[]{:S(2)}, u32[]{:S(2)}) collective-permute-start(bf16[576,128]{1,0:T(8,128)(2,1)} %get-tuple-element.30), channel_id=1, source_target_pairs={{1,0},{2,1},{3,2},{4,3},{5,4},{6,5},{7,6},{8,7},{9,8},{10,9},{11,1... | collective-permute-start | bytes 442376 | tf_op jit(solution)/shard_map/ppermute | solution.py:207
  30.4 7.9 %shard_map.84 = (f32[16,256,256]{2,1,0:T(8,128)S(1)}, bf16[768,768]{1,0:T(8,128)(2,1)S(1)}) custom-call(bf16[16,256,256]{2,1,0:T(8,128)(2,1)S(1)} %bitcast.19, bf16[9,256,256]{2,1,0:T(8,128)(2,1)S(1)} %copy-done.2), custom_call_target="tpu_custom_call" | custom-call | flops 8999999488 | bytes 27000000 | tf_op jit(solution)/shard_map/pallas_call | solution.py:581
  38.3 2.0 %copy-done.8 = f32[16,256,256]{2,1,0:T(8,128)} copy-done((f32[16,256,256]{2,1,0:T(8,128)}, f32[16,256,256]{2,1,0:T(8,128)S(1)}, u32[]{:S(2)}) %copy-start.8) | copy-done | bytes 4194328
  42.5 13.5 %affinity.1 = (f32[16,8,384]{2,1,0:T(8,128)S(1)}, f32[25,24,384]{2,1,0:T(8,128)S(1)}) custom-call(s32[2]{0:T(128)S(1)} %pad_add_fusion.place_ref, bf16[8,112,256]{2,1,0:T(8,128)(2,1)S(1)} %copy-done.4, bf16[16,80,256]{2,1,0:T(8,128)(2,1)S(1)} %maximum_bitcast_fusion.mid_ref, bf16[8,112,256]{2,1,0:T(8,128)(2,1)S(1)} %collective-permute-done.1.down_ref, ...), custom_call_target="tpu_custom_call" | custom-call | flops 12000000000 | bytes 36000000 | tf_op jit(solution)/shard_map/affinity/pallas_call | solution.py:243
  56.0 9.0 %collective-permute-start.4 = (f32[8,8,384]{2,1,0:T(8,128)S(1)}, f32[8,8,384]{2,1,0:T(8,128)S(1)}, u32[]{:S(2)}, u32[]{:S(2)}) collective-permute-start(f32[8,8,384]{2,1,0:T(8,128)S(1)} %get-tuple-element.73), channel_id=1, source_target_pairs={{0,16},{16,32},{32,48},{48,64},{64,80},{80,96},{96,112},{1,17},{17... | collective-permute-start | bytes 294920 | tf_op jit(solution)/shard_map/ppermute | solution.py:206
  66.4 5.0 %shard_map.85 = (f32[16,256,256]{2,1,0:T(8,128)S(1)}, bf16[16,256,256]{2,1,0:T(8,128)(2,1)S(1)}, f32[16,8,256]{2,1,0:T(8,128)S(1)}) custom-call(bf16[8,112,256]{2,1,0:T(8,128)(2,1)S(1)} %copy-done.5, bf16[8,112,256]{2,1,0:T(8,128)(2,1)S(1)} %collective-permute-done.1.down_ref, bf16[576,128]{1,0:T(8,128)(2,1)S(1)} %collective-permute-done.2.left_ref, ...), custom_call_target="tpu_custom_call" | custom-call | flops 7000000000 | bytes 21000000 | tf_op jit(solution)/shard_map/pallas_call | solution.py:581
  72.6 3.0 %finish.1.refined_ref = f32[16,8,256]{2,1,0:T(8,128)S(1)} custom-call(f32[25,24,384]{2,1,0:T(8,128)S(1)} %get-tuple-element.31.weights_ref, f32[8,8,384]{2,1,0:T(8,128)S(1)} %collective-permute-done.4.up_ref, f32[16,8,384]{2,1,0:T(8,128)S(1)} %get-tuple-element.32.mid_ref, f32[8,8,384]{2,1,0:T(8,128)S(1)} %collective-permute-done.5.down_ref), custom_call_target="tpu_custom_call" | custom-call | flops 4000000000 | bytes 12000000 | tf_op jit(solution)/shard_map/finish/pallas_call | solution.py:274
  75.7 1.7 %shard_map.86 = (bf16[16,256,256]{2,1,0:T(8,128)(2,1)S(1)}, bf16[16,8,256]{2,1,0:T(8,128)(2,1)S(1)}) custom-call(f32[16,8,256]{2,1,0:T(8,128)S(1)} %get-tuple-element.35.guess_ref, f32[16,8,256]{2,1,0:T(8,128)S(1)} %finish.1.refined_ref, f32[16,256,256]{2,1,0:T(8,128)S(1)} %get-tuple-element.36.slope_ref, bf16[256,8]{1,0:T(8,128)(2,1)S(1)} %copy.20.class_ref), custom_call_target="tpu_custom_call" | custom-call | flops 2000000000 | bytes 6000000 | tf_op jit(solution)/shard_map/pallas_call | solution.py:581
  77.4 5.0 %collective-permute-start.6 = (bf16[1,256,256]{2,1,0:T(8,128)(2,1)S(1)}, bf16[1,256,256]{2,1,0:T(8,128)(2,1)S(1)}, u32[]{:S(2)}, u32[]{:S(2)}) collective-permute-start(bf16[1,256,256]{2,1,0:T(8,128)(2,1)S(1)} %get-tuple-element.67), channel_id=1, source_target_pairs={{0,16},{16,32},{32,48},{48,64},{64,80},{80,96},{96,112},{1,17},{17... | collective-permute-start | bytes 393224 | tf_op jit(solution)/shard_map/ppermute | solution.py:206
  83.7 9.5 %shard_map.87 = (f32[64,40,128]{2,1,0:T(8,128)S(1)}, f32[64,40,128]{2,1,0:T(8,128)S(1)}) custom-call(s32[1]{0:T(128)} %bitcast.8.core_ref, bf16[8,112,256]{2,1,0:T(8,128)(2,1)S(1)} %copy-done.5, bf16[16,256,256]{2,1,0:T(8,128)(2,1)S(1)} %bitcast.20, bf16[8,112,256]{2,1,0:T(8,128)(2,1)S(1)} %collective-permute-done.1.down_ref, ...), custom_call_target="tpu_custom_call" | custom-call | flops 8999999488 | bytes 27000000 | tf_op jit(solution)/shard_map/pallas_call | solution.py:581
  94.1 6.1 %collective-permute-start.8 = (bf16[256,128]{1,0:T(8,128)(2,1)S(1)}, bf16[256,128]{1,0:T(8,128)(2,1)S(1)}, u32[]{:S(2)}, u32[]{:S(2)}) collective-permute-start(bf16[256,128]{1,0:T(8,128)(2,1)S(1)} %get-tuple-element.43), channel_id=1, source_target_pairs={{0,1},{1,2},{2,3},{3,4},{4,5},{5,6},{6,7},{7,8},{8,9},{9,10},{10,1... | collective-permute-start | bytes 196616 | tf_op jit(solution)/shard_map/ppermute | solution.py:206
  100.2 1.9 %collective-permute-start.9 = (bf16[256,128]{1,0:T(8,128)(2,1)S(1)}, bf16[256,128]{1,0:T(8,128)(2,1)S(1)}, u32[]{:S(2)}, u32[]{:S(2)}) collective-permute-start(bf16[256,128]{1,0:T(8,128)(2,1)S(1)} %get-tuple-element.44), channel_id=1, source_target_pairs={{1,0},{2,1},{3,2},{4,3},{5,4},{6,5},{7,6},{8,7},{9,8},{10,9},{11,1... | collective-permute-start | bytes 196616 | tf_op jit(solution)/shard_map/ppermute | solution.py:207
  103.7 3.6 %collective-permute-done.9.right_ref = bf16[256,128]{1,0:T(8,128)(2,1)S(1)} collective-permute-done((bf16[256,128]{1,0:T(8,128)(2,1)S(1)}, bf16[256,128]{1,0:T(8,128)(2,1)S(1)}, u32[]{:S(2)}, u32[]{:S(2)}) %collective-permute-start.9) | collective-permute-done | bytes 65568 | tf_op jit(solution)/shard_map/ppermute | solution.py:207
  107.3 14.4 %all-to-all-start = ((f16[64,40,128]{2,1,0:T(8,128)(2,1)}), f16[64,40,128]{2,1,0:T(8,128)(2,1)S(1)}, u32[]{:S(2)}, u32[]{:S(2)}) async-start(f16[64,40,128]{2,1,0:T(8,128)(2,1)} %select_convert_fusion), calls=%async_computation | async-start | bytes 1310720 | tf_op jit(solution)/shard_map/all_to_all | solution.py:671
  121.7 10.2 %feature.1 = bf16[16,256,256]{2,1,0:T(8,128)(2,1)S(1)} custom-call(bf16[1,256,256]{2,1,0:T(8,128)(2,1)} %copy-done.6, bf16[16,256,256]{2,1,0:T(8,128)(2,1)} %copy-done, bf16[16,256,256]{2,1,0:T(8,128)(2,1)} %copy-done, bf16[16,256,256]{2,1,0:T(8,128)(2,1)} %copy-done, bf16[1,256,256]{2,1,0:T(8,128)(2,1)} %copy-done.7, bf16[256,128]{1,0:T(8,128)(2,1)} %copy-done.13, ...), custom_call_target="tpu_custom_call" | custom-call | flops 8000000000 | bytes 24000000 | tf_op jit(solution)/shard_map/feature/pallas_call | solution.py:653
  132.0 2.3 %all-to-all-done = f16[64,40,128]{2,1,0:T(8,128)(2,1)S(1)} async-done(((f16[64,40,128]{2,1,0:T(8,128)(2,1)}), f16[64,40,128]{2,1,0:T(8,128)(2,1)S(1)}, u32[]{:S(2)}, u32[]{:S(2)}) %all-to-all-start) | async-done | bytes 655392 | tf_op jit(solution)/shard_map/all_to_all | solution.py:671
  134.8 20.4 %all_to_all.10 = f16[64,40,128]{2,1,0:T(8,128)(2,1)S(1)} all-to-all(f16[64,40,128]{2,1,0:T(8,128)(2,1)S(1)} %broadcast_in_dim.36), channel_id=1, replica_groups=mesh['row'=8,'pair'=8,'core'=2] {'row','pair'}, dimensions={0} | all-to-all | bytes 1310720 | tf_op jit(solution)/shard_map/all_to_all | solution.py:358
  155.9 2.5 %copy.22 = bf16[256,16,256]{2,1,0:T(8,128)(2,1)} copy(bf16[256,16,256]{2,0,1:T(8,128)(2,1)S(1)} %bitcast.21) | data formatting | bytes 4194304
  158.8 1.7 %place.1 = (f32[9,256,256]{2,1,0:T(8,128)}, f32[8,256]{1,0:T(8,128)}) custom-call(s32[1]{0:T(128)} %bitcast.8.core_ref, f32[64,40,128]{2,1,0:T(8,128)S(1)} %convert_multiply_fusion.1.own_ref, f32[64,40,128]{2,1,0:T(8,128)S(1)} %convert_multiply_fusion.other_ref), custom_call_target="tpu_custom_call" | custom-call | flops 2000000000 | bytes 6000000 | tf_op jit(solution)/shard_map/place/pallas_call | solution.py:361
  (71 shorter events, 15.6 us)
Async XLA Ops:
  2.8 1.6 copy-start.12
  5.2 13.7 %collective-permute-start.1 = (bf16[8,112,256]{2,1,0:T(8,128)(2,1)S(1)}, bf16[8,112,256]{2,1,0:T(8,128)(2,1)S(1)}, u32[]{:S(2)}, u32[]{:S(2)}) collective-permute-start(bf16[8,112,256]{2,1,0:T(8,128)(2,1)S(1)} %pad_maximum_fusion.1), channel_id=1, source_target_pairs={{16,0},{32,16},{48,32},{64,48},{80,64},{96,80},{112,96},{17,1},{33... | collective-permute-start | bytes 1376264 | tf_op jit(solution)/shard_map/ppermute | solution.py:207
  6.5 23.9 %copy-start.2 = (bf16[9,256,256]{2,1,0:T(8,128)(2,1)S(1)}, bf16[9,256,256]{2,1,0:T(8,128)(2,1)}, u32[]{:S(2)}) copy-start(bf16[9,256,256]{2,1,0:T(8,128)(2,1)} %taps_ref.3) | copy-start | bytes 3538948
  6.5 13.5 %collective-permute-start = (bf16[8,112,256]{2,1,0:T(8,128)(2,1)S(1)}, bf16[8,112,256]{2,1,0:T(8,128)(2,1)S(1)}, u32[]{:S(2)}, u32[]{:S(2)}) collective-permute-start(bf16[8,112,256]{2,1,0:T(8,128)(2,1)S(1)} %pad_maximum_fusion), channel_id=1, source_target_pairs={{0,16},{16,32},{32,48},{48,64},{64,80},{80,96},{96,112},{1,17},{17... | collective-permute-start | bytes 1376264 | tf_op jit(solution)/shard_map/ppermute | solution.py:206
  20.0 1.7 %copy-start.3 = (bf16[8,112,256]{2,1,0:T(8,128)(2,1)}, bf16[8,112,256]{2,1,0:T(8,128)(2,1)S(1)}, u32[]{:S(2)}) copy-start(bf16[8,112,256]{2,1,0:T(8,128)(2,1)S(1)} %collective-permute-done.up_ref) | copy-start | bytes 1376260
  21.7 19.7 %collective-permute-start.2 = (bf16[576,128]{1,0:T(8,128)(2,1)}, bf16[576,128]{1,0:T(8,128)(2,1)S(1)}, u32[]{:S(2)}, u32[]{:S(2)}) collective-permute-start(bf16[576,128]{1,0:T(8,128)(2,1)} %get-tuple-element.29), channel_id=1, source_target_pairs={{0,1},{1,2},{2,3},{3,4},{4,5},{5,6},{6,7},{7,8},{8,9},{9,10},{10,1... | collective-permute-start | bytes 442376 | tf_op jit(solution)/shard_map/ppermute | solution.py:206
  28.4 12.8 %copy-start.1 = (bf16[256,8]{0,1:T(8,128)(2,1)S(1)}, bf16[256,8]{0,1:T(8,128)(2,1)}, u32[]{:S(2)}) copy-start(bf16[256,8]{0,1:T(8,128)(2,1)} %param.9) | copy-start | bytes 12292
  28.5 13.0 %collective-permute-start.3 = (bf16[576,128]{1,0:T(8,128)(2,1)}, bf16[576,128]{1,0:T(8,128)(2,1)}, u32[]{:S(2)}, u32[]{:S(2)}) collective-permute-start(bf16[576,128]{1,0:T(8,128)(2,1)} %get-tuple-element.30), channel_id=1, source_target_pairs={{1,0},{2,1},{3,2},{4,3},{5,4},{6,5},{7,6},{8,7},{9,8},{10,9},{11,1... | collective-permute-start | bytes 442376 | tf_op jit(solution)/shard_map/ppermute | solution.py:207
  38.3 2.0 %copy-start.8 = (f32[16,256,256]{2,1,0:T(8,128)}, f32[16,256,256]{2,1,0:T(8,128)S(1)}, u32[]{:S(2)}) copy-start(f32[16,256,256]{2,1,0:T(8,128)S(1)} %get-tuple-element.34.pre_ref) | copy-start | bytes 12582916
  42.5 23.9 %copy-start.5 = (bf16[8,112,256]{2,1,0:T(8,128)(2,1)S(1)}, bf16[8,112,256]{2,1,0:T(8,128)(2,1)}, u32[]{:S(2)}) copy-start(bf16[8,112,256]{2,1,0:T(8,128)(2,1)} %copy-done.3) | copy-start | bytes 1376260
  42.5 23.9 %copy-start.9 = (f32[16,256,256]{2,1,0:T(8,128)S(1)}, f32[16,256,256]{2,1,0:T(8,128)}, u32[]{:S(2)}) copy-start(f32[16,256,256]{2,1,0:T(8,128)} %copy-done.8) | copy-start | bytes 12582916
  42.5 23.9 %copy-start.11 = (bf16[768,768]{1,0:T(8,128)(2,1)S(1)}, bf16[768,768]{1,0:T(8,128)(2,1)}, u32[]{:S(2)}) copy-start(bf16[768,768]{1,0:T(8,128)(2,1)} %copy-done.10) | copy-start | bytes 3538948
  56.0 15.4 %collective-permute-start.4 = (f32[8,8,384]{2,1,0:T(8,128)S(1)}, f32[8,8,384]{2,1,0:T(8,128)S(1)}, u32[]{:S(2)}, u32[]{:S(2)}) collective-permute-start(f32[8,8,384]{2,1,0:T(8,128)S(1)} %get-tuple-element.73), channel_id=1, source_target_pairs={{0,16},{16,32},{32,48},{48,64},{64,80},{80,96},{96,112},{1,17},{17... | collective-permute-start | bytes 294920 | tf_op jit(solution)/shard_map/ppermute | solution.py:206
  65.0 7.6 %collective-permute-start.5 = (f32[8,8,384]{2,1,0:T(8,128)S(1)}, f32[8,8,384]{2,1,0:T(8,128)S(1)}, u32[]{:S(2)}, u32[]{:S(2)}) collective-permute-start(f32[8,8,384]{2,1,0:T(8,128)S(1)} %get-tuple-element.72), channel_id=1, source_target_pairs={{16,0},{32,16},{48,32},{64,48},{80,64},{96,80},{112,96},{17,1},{33... | collective-permute-start | bytes 294920 | tf_op jit(solution)/shard_map/ppermute | solution.py:207
  77.4 16.0 %copy-start = (bf16[16,256,256]{2,1,0:T(8,128)(2,1)}, bf16[16,256,256]{2,1,0:T(8,128)(2,1)S(1)}, u32[]{:S(2)}) copy-start(bf16[16,256,256]{2,1,0:T(8,128)(2,1)S(1)} %get-tuple-element.37.back_ref.mid_ref.above_ref.below_ref) | copy-start | bytes 6291460
  77.4 15.8 %collective-permute-start.6 = (bf16[1,256,256]{2,1,0:T(8,128)(2,1)S(1)}, bf16[1,256,256]{2,1,0:T(8,128)(2,1)S(1)}, u32[]{:S(2)}, u32[]{:S(2)}) collective-permute-start(bf16[1,256,256]{2,1,0:T(8,128)(2,1)S(1)} %get-tuple-element.67), channel_id=1, source_target_pairs={{0,16},{16,32},{32,48},{48,64},{64,80},{80,96},{96,112},{1,17},{17... | collective-permute-start | bytes 393224 | tf_op jit(solution)/shard_map/ppermute | solution.py:206
  82.4 10.8 %collective-permute-start.7 = (bf16[1,256,256]{2,1,0:T(8,128)(2,1)S(1)}, bf16[1,256,256]{2,1,0:T(8,128)(2,1)S(1)}, u32[]{:S(2)}, u32[]{:S(2)}) collective-permute-start(bf16[1,256,256]{2,1,0:T(8,128)(2,1)S(1)} %get-tuple-element.66), channel_id=1, source_target_pairs={{16,0},{32,16},{48,32},{64,48},{80,64},{96,80},{112,96},{17,1},{33... | collective-permute-start | bytes 393224 | tf_op jit(solution)/shard_map/ppermute | solution.py:207
  93.3 8.9 %collective-permute-start.10 = (f32[64,40,128]{2,1,0:T(8,128)S(1)}, f32[64,40,128]{2,1,0:T(8,128)S(1)}, u32[]{:S(2)}, u32[]{:S(2)}) collective-permute-start(f32[64,40,128]{2,1,0:T(8,128)S(1)} %get-tuple-element.46), channel_id=1, source_target_pairs={{0,1},{1,0},{2,3},{3,2},{4,5},{5,4},{6,7},{7,6},{8,9},{9,8},{10,11... | collective-permute-start | bytes 3932168 | tf_op jit(solution)/shard_map/ppermute | solution.py:646
  94.1 9.6 %collective-permute-start.8 = (bf16[256,128]{1,0:T(8,128)(2,1)S(1)}, bf16[256,128]{1,0:T(8,128)(2,1)S(1)}, u32[]{:S(2)}, u32[]{:S(2)}) collective-permute-start(bf16[256,128]{1,0:T(8,128)(2,1)S(1)} %get-tuple-element.43), channel_id=1, source_target_pairs={{0,1},{1,2},{2,3},{3,4},{4,5},{5,6},{6,7},{7,8},{8,9},{9,10},{10,1... | collective-permute-start | bytes 196616 | tf_op jit(solution)/shard_map/ppermute | solution.py:206
  100.2 7.1 %collective-permute-start.9 = (bf16[256,128]{1,0:T(8,128)(2,1)S(1)}, bf16[256,128]{1,0:T(8,128)(2,1)S(1)}, u32[]{:S(2)}, u32[]{:S(2)}) collective-permute-start(bf16[256,128]{1,0:T(8,128)(2,1)S(1)} %get-tuple-element.44), channel_id=1, source_target_pairs={{1,0},{2,1},{3,2},{4,3},{5,4},{6,5},{7,6},{8,7},{9,8},{10,9},{11,1... | collective-permute-start | bytes 196616 | tf_op jit(solution)/shard_map/ppermute | solution.py:207
  103.7 18.0 %copy-start.13 = (bf16[256,128]{1,0:T(8,128)(2,1)}, bf16[256,128]{1,0:T(8,128)(2,1)S(1)}, u32[]{:S(2)}) copy-start(bf16[256,128]{1,0:T(8,128)(2,1)S(1)} %collective-permute-done.8.left_ref) | copy-start | bytes 196612
  107.3 14.4 %copy-start.14 = (bf16[256,128]{1,0:T(8,128)(2,1)}, bf16[256,128]{1,0:T(8,128)(2,1)S(1)}, u32[]{:S(2)}) copy-start(bf16[256,128]{1,0:T(8,128)(2,1)S(1)} %collective-permute-done.9.right_ref) | copy-start | bytes 196612
  107.3 26.9 %all-to-all-start = ((f16[64,40,128]{2,1,0:T(8,128)(2,1)}), f16[64,40,128]{2,1,0:T(8,128)(2,1)S(1)}, u32[]{:S(2)}, u32[]{:S(2)}) async-start(f16[64,40,128]{2,1,0:T(8,128)(2,1)} %select_convert_fusion), calls=%async_computation | async-start | bytes 1310720 | tf_op jit(solution)/shard_map/all_to_all | solution.py:671
  155.2 3.4 %collective-permute-start.11 = (f16[64,40,128]{2,1,0:T(8,128)(2,1)S(1)}, f16[64,40,128]{2,1,0:T(8,128)(2,1)S(1)}, u32[]{:S(2)}, u32[]{:S(2)}) collective-permute-start(f16[64,40,128]{2,1,0:T(8,128)(2,1)S(1)} %all_to_all.10), channel_id=1, source_target_pairs={{0,1},{1,0},{2,3},{3,2},{4,5},{5,4},{6,7},{7,6},{8,9},{9,8},{10,11... | collective-permute-start | bytes 1966088 | tf_op jit(solution)/shard_map/ppermute | solution.py:359
  (4 other events, 3.7 us)

commit v5 on v4

--- a/solution.py
+++ b/solution.py
@@ -386,7 +386,7 @@
     return jnp.dot(weights, jnp.concatenate(moved, axis=0), preferred_element_type=jnp.float32)
 
 
-STEP_ROWS = 2
+STEP_ROWS = 4
 
 
 def joined(parts, out):
@@ -571,7 +571,7 @@
     edge = jax.ShapeDtypeStruct((cells.shape[1], 128), cells.dtype)
     to_left, to_right = pl.pallas_call(
         unit_edges_kernel, out_shape=(edge, edge), name="unit_edges",
-        compiler_params=vmem_of(16),
+        compiler_params=vmem_of(24),
         cost_estimate=cost_of(1),
     )(up, cells, down)
     return pass_on(to_right, COL, 1), pass_on(to_left, COL, -1)
@@ -606,7 +606,7 @@
             jax.ShapeDtypeStruct((rows, hidden_size, cols), f32),
             jax.ShapeDtypeStruct((3 * hidden_size, 3 * channels), bf16),
         ],
-        [True, False], [pltpu.VMEM((rows + 2, channels, cols), bf16)], 16, 9,
+        [True, False], [pltpu.VMEM((rows + 2, channels, cols), bf16)], 24, 9,
     )
     left, right = share_cols(mid, up, down, student)
     halo = (up, student, down, left, right)
@@ -621,7 +621,7 @@
             jax.ShapeDtypeStruct((rows, classes, cols), f32),
         ],
         [True] * 3,
-        [pltpu.VMEM((hidden_size, 128), f32)] * 2 + [pltpu.VMEM((2, hidden_size, cols), f32)], 16, 7,
+        [pltpu.VMEM((hidden_size, 128), f32)] * 2 + [pltpu.VMEM((2, hidden_size, cols), f32)], 24, 7,
     )
     refined = finish(current, weights, cols, *current_rows)
     back, error = row_call(
@@ -630,7 +630,7 @@
             jax.ShapeDtypeStruct((rows, hidden_size, cols), bf16),
             jax.ShapeDtypeStruct((rows, classes, cols), bf16),
         ],
-        [True] * 2, [], 16, 2,
+        [True] * 2, [], 24, 2,
     )
     back_up, back_down = unit_rows(back)
     core = lax.axis_index("core").astype(jnp.int32).reshape(1)
@@ -640,16 +640,15 @@
         [chunks, chunks], [False] * 2,
         [pltpu.VMEM((rows + 2, channels, cols), bf16)]
         + [pltpu.VMEM((hidden_size, 128), f32)] * 2
-        + [pltpu.VMEM((3 * channels, 3 * hidden_size), f32), pltpu.VMEM((classes, hidden_size), f32)], 28, 9,
+        + [pltpu.VMEM((3 * channels, 3 * hidden_size), f32), pltpu.VMEM((classes, hidden_size), f32)], 36, 9,
     )
     back_up, back_down, sent = lax.optimization_barrier((back_up, back_down, sent))
     other = lax.ppermute(sent, "core", PARTNER)
-    back_cols = unit_cols(back, back_up, back_down)
+    back_left, back_right = unit_cols(back, back_up, back_down)
     packed = pack_half(keep + other)
-    back_left, back_right, packed = lax.optimization_barrier(back_cols + (packed,))
     steps = rows // STEP_ROWS
     block = (STEP_ROWS, hidden_size, cols)
-    feature_args = in_hbm(back_up, back, back_down, back_left, back_right, conv_weight)
+    feature_args = in_hbm(back_up, back, back_down) + (back_left, back_right) + in_hbm(conv_weight)
     feature_grad = pl.pallas_call(
         feature_kernel,
         grid=(steps,),
@@ -665,7 +664,7 @@
         scratch_shapes=[pltpu.VMEM((channels, 128), f32)] * 2
         + [pltpu.VMEM((3 * channels, 3 * hidden_size), bf16)],
         name="feature",
-        compiler_params=vmem_of(16),
+        compiler_params=vmem_of(24),
         cost_estimate=cost_of(8),
     )(feature_args[0], feature_args[1], feature_args[1], feature_args[1], *feature_args[2:])
     received = lax.all_to_all(packed, CHIPS, split_axis=0, concat_axis=0, tiled=True)

time: 161 us -> 154 us (0.957)
  Pallas kernels: 54.9 us -> 49.5 us
    pallas_call x4, Pallas kernels: 24 us -> 20.2 us  [row_call(): pl.pallas_call(kernel, grid=(rows // STEP_ROWS,), in_specs=[pl.BlockSpec(...]
    ppermute x5, waiting for transfers between devices: 12.5 us -> 9.88 us  [pass_on(): return lax.ppermute(cells, axis, [(i + 1, i) for i in range(ends)])]
    all_to_all x1, waiting for transfers between devices: 2.28 us -> 4.16 us  [local_step(): lax.all_to_all(packed, CHIPS, split_axis=0, concat_axis=0, tiled=True)]
    unnamed x35 -> x31, local copies, waits for them, and re-layouts: 10.7 us -> 10.7 us
  transfers between devices with their start and end apart: 13 -> 13, of which waited for: 5 -> 4; matrix products, arithmetic and copies ran while one was open for 3% -> 3% of each run, Pallas kernels for 21% -> 19%
where the time goes in v5:
time: 154 us
  starting transfers between devices  54.2 us (35%)
  Pallas kernels  49.5 us (32%)
  blocking collectives  19.4 us (13%)
  waiting for transfers between devices  15.1 us (10%)
  local copies, waits for them, and re-layouts  10.9 us (7%)
  other arithmetic  3.52 us (2%)
    ppermute x5, starting transfers between devices, pass_on(): return lax.ppermute(cells, axis, [(i, i + 1) for i in range(ends)])  31.1 us
    pallas_call x4, Pallas kernels, row_call(): pl.pallas_call(kernel, grid=(rows // STEP_ROWS,), in_specs=[pl.BlockSpec(...  20.2 us
    all_to_all x1, blocking collectives, gather_all(): own = lax.all_to_all(spread, CHIPS, split_axis=0, concat_axis=0, tiled=True)  19.4 us
    all_to_all x1, starting transfers between devices, local_step(): lax.all_to_all(packed, CHIPS, split_axis=0, concat_axis=0, tiled=True)  14.6 us
    pallas_call x1, Pallas kernels, refine(): pl.pallas_call(functools.partial(affinity_kernel, full_rows=rows * lax.ax...  13.5 us
    unnamed x31, local copies, waits for them, and re-layouts  10.7 us
    ppermute x5, waiting for transfers between devices, pass_on(): return lax.ppermute(cells, axis, [(i + 1, i) for i in range(ends)])  9.88 us
    pallas_call x1, Pallas kernels, local_step(): pl.pallas_call(feature_kernel, grid=(steps,), in_specs=[whole(back_up), p...  8.73 us
  transfers between devices with their start and end apart: 13, of which 4 were waited for; matrix products, arithmetic and copies ran while one was open for 3% of the time, Pallas kernels for 19%

profile of v5, /device:TPU:1, one launch (start us, length us, event | category | flops | bytes accessed | tf_op | source)
XLA Modules:
  0.0 153.8 jit_solution(12666354414396074271)
XLA Ops:
  2.9 1.5 copy-done.12
  5.2 1.3 collective-permute-start.1
  6.5 4.7 %collective-permute-start = (bf16[8,112,256]{2,1,0:T(8,128)(2,1)S(1)}, bf16[8,112,256]{2,1,0:T(8,128)(2,1)S(1)}, u32[]{:S(2)}, u32[]{:S(2)}) collective-permute-start(bf16[8,112,256]{2,1,0:T(8,128)(2,1)S(1)} %pad_maximum_fusion), channel_id=1, source_target_pairs={{0,16},{16,32},{32,48},{48,64},{64,80},{80,96},{96,112},{1,17},{17... | collective-permute-start | bytes 1376264 | tf_op jit(solution)/shard_map/ppermute | solution.py:206
  11.3 7.7 %collective-permute-done.1.down_ref = bf16[8,112,256]{2,1,0:T(8,128)(2,1)S(1)} collective-permute-done((bf16[8,112,256]{2,1,0:T(8,128)(2,1)S(1)}, bf16[8,112,256]{2,1,0:T(8,128)(2,1)S(1)}, u32[]{:S(2)}, u32[]{:S(2)}) %collective-permute-start.1) | collective-permute-done | bytes 458784 | tf_op jit(solution)/shard_map/ppermute | solution.py:207
  20.0 1.7 %edges.1 = (bf16[576,128]{1,0:T(8,128)(2,1)}, bf16[576,128]{1,0:T(8,128)(2,1)}) custom-call(bf16[8,112,256]{2,1,0:T(8,128)(2,1)S(1)} %collective-permute-done.up_ref, bf16[16,80,256]{2,1,0:T(8,128)(2,1)S(1)} %maximum_bitcast_fusion.mid_ref, bf16[8,112,256]{2,1,0:T(8,128)(2,1)S(1)} %collective-permute-done.1.down_ref, bf16[16,256,256]{2,1,0:T(8,128)(2,1)S(1)} %bitcast.18), custom_call_target="tpu_custom_call" | custom-call | flops 2000000000 | bytes 6000000 | tf_op jit(solution)/shard_map/edges/pallas_call | solution.py:232
  21.7 6.7 %collective-permute-start.2 = (bf16[576,128]{1,0:T(8,128)(2,1)}, bf16[576,128]{1,0:T(8,128)(2,1)S(1)}, u32[]{:S(2)}, u32[]{:S(2)}) collective-permute-start(bf16[576,128]{1,0:T(8,128)(2,1)} %get-tuple-element.26), channel_id=1, source_target_pairs={{0,1},{1,2},{2,3},{3,4},{4,5},{5,6},{6,7},{7,8},{8,9},{9,10},{10,1... | collective-permute-start | bytes 442376 | tf_op jit(solution)/shard_map/ppermute | solution.py:206
  28.4 1.9 %collective-permute-start.3 = (bf16[576,128]{1,0:T(8,128)(2,1)}, bf16[576,128]{1,0:T(8,128)(2,1)}, u32[]{:S(2)}, u32[]{:S(2)}) collective-permute-start(bf16[576,128]{1,0:T(8,128)(2,1)} %get-tuple-element.27), channel_id=1, source_target_pairs={{1,0},{2,1},{3,2},{4,3},{5,4},{6,5},{7,6},{8,7},{9,8},{10,9},{11,1... | collective-permute-start | bytes 442376 | tf_op jit(solution)/shard_map/ppermute | solution.py:207
  30.4 6.6 %shard_map.84 = (f32[16,256,256]{2,1,0:T(8,128)S(1)}, bf16[768,768]{1,0:T(8,128)(2,1)S(1)}) custom-call(bf16[16,256,256]{2,1,0:T(8,128)(2,1)S(1)} %bitcast.19, bf16[9,256,256]{2,1,0:T(8,128)(2,1)S(1)} %copy-done.2), custom_call_target="tpu_custom_call" | custom-call | flops 8999999488 | bytes 27000000 | tf_op jit(solution)/shard_map/pallas_call | solution.py:581
  37.0 1.9 %copy-done.8 = f32[16,256,256]{2,1,0:T(8,128)} copy-done((f32[16,256,256]{2,1,0:T(8,128)}, f32[16,256,256]{2,1,0:T(8,128)S(1)}, u32[]{:S(2)}) %copy-start.8) | copy-done | bytes 4194328
  41.2 13.5 %affinity.1 = (f32[16,8,384]{2,1,0:T(8,128)S(1)}, f32[25,24,384]{2,1,0:T(8,128)S(1)}) custom-call(s32[2]{0:T(128)S(1)} %pad_add_fusion.place_ref, bf16[8,112,256]{2,1,0:T(8,128)(2,1)S(1)} %copy-done.4, bf16[16,80,256]{2,1,0:T(8,128)(2,1)S(1)} %maximum_bitcast_fusion.mid_ref, bf16[8,112,256]{2,1,0:T(8,128)(2,1)S(1)} %collective-permute-done.1.down_ref, ...), custom_call_target="tpu_custom_call" | custom-call | flops 12000000000 | bytes 36000000 | tf_op jit(solution)/shard_map/affinity/pallas_call | solution.py:243
  54.7 9.0 %collective-permute-start.4 = (f32[8,8,384]{2,1,0:T(8,128)S(1)}, f32[8,8,384]{2,1,0:T(8,128)S(1)}, u32[]{:S(2)}, u32[]{:S(2)}) collective-permute-start(f32[8,8,384]{2,1,0:T(8,128)S(1)} %get-tuple-element.67), channel_id=1, source_target_pairs={{0,16},{16,32},{32,48},{48,64},{64,80},{80,96},{96,112},{1,17},{17... | collective-permute-start | bytes 294920 | tf_op jit(solution)/shard_map/ppermute | solution.py:206
  65.1 4.1 %shard_map.85 = (f32[16,256,256]{2,1,0:T(8,128)S(1)}, bf16[16,256,256]{2,1,0:T(8,128)(2,1)S(1)}, f32[16,8,256]{2,1,0:T(8,128)S(1)}) custom-call(bf16[8,112,256]{2,1,0:T(8,128)(2,1)S(1)} %copy-done.5, bf16[8,112,256]{2,1,0:T(8,128)(2,1)S(1)} %collective-permute-done.1.down_ref, bf16[576,128]{1,0:T(8,128)(2,1)S(1)} %collective-permute-done.2.left_ref, ...), custom_call_target="tpu_custom_call" | custom-call | flops 7000000000 | bytes 21000000 | tf_op jit(solution)/shard_map/pallas_call | solution.py:581
  69.2 2.2 %collective-permute-done.5.down_ref = f32[8,8,384]{2,1,0:T(8,128)S(1)} collective-permute-done((f32[8,8,384]{2,1,0:T(8,128)S(1)}, f32[8,8,384]{2,1,0:T(8,128)S(1)}, u32[]{:S(2)}, u32[]{:S(2)}) %collective-permute-start.5) | collective-permute-done | bytes 98336 | tf_op jit(solution)/shard_map/ppermute | solution.py:207
  71.4 3.0 %finish.1.refined_ref = f32[16,8,256]{2,1,0:T(8,128)S(1)} custom-call(f32[25,24,384]{2,1,0:T(8,128)S(1)} %get-tuple-element.28.weights_ref, f32[8,8,384]{2,1,0:T(8,128)S(1)} %collective-permute-done.4.up_ref, f32[16,8,384]{2,1,0:T(8,128)S(1)} %get-tuple-element.29.mid_ref, f32[8,8,384]{2,1,0:T(8,128)S(1)} %collective-permute-done.5.down_ref), custom_call_target="tpu_custom_call" | custom-call | flops 4000000000 | bytes 12000000 | tf_op jit(solution)/shard_map/finish/pallas_call | solution.py:274
  75.6 4.3 %collective-permute-start.6 = (bf16[1,256,256]{2,1,0:T(8,128)(2,1)S(1)}, bf16[1,256,256]{2,1,0:T(8,128)(2,1)S(1)}, u32[]{:S(2)}, u32[]{:S(2)}) collective-permute-start(bf16[1,256,256]{2,1,0:T(8,128)(2,1)S(1)} %get-tuple-element.61), channel_id=1, source_target_pairs={{0,16},{16,32},{32,48},{48,64},{64,80},{80,96},{96,112},{1,17},{17... | collective-permute-start | bytes 393224 | tf_op jit(solution)/shard_map/ppermute | solution.py:206
  81.2 8.4 %shard_map.87 = (f32[64,40,128]{2,1,0:T(8,128)S(1)}, f32[64,40,128]{2,1,0:T(8,128)S(1)}) custom-call(s32[1]{0:T(128)} %bitcast.7.core_ref, bf16[8,112,256]{2,1,0:T(8,128)(2,1)S(1)} %copy-done.5, bf16[16,256,256]{2,1,0:T(8,128)(2,1)S(1)} %bitcast.20, bf16[8,112,256]{2,1,0:T(8,128)(2,1)S(1)} %collective-permute-done.1.down_ref, ...), custom_call_target="tpu_custom_call" | custom-call | flops 8999999488 | bytes 27000000 | tf_op jit(solution)/shard_map/pallas_call | solution.py:581
  90.6 2.4 %collective-permute-start.10 = (bf16[256,128]{1,0:T(8,128)(2,1)S(1)}, bf16[256,128]{1,0:T(8,128)(2,1)S(1)}, u32[]{:S(2)}, u32[]{:S(2)}) collective-permute-start(bf16[256,128]{1,0:T(8,128)(2,1)S(1)} %get-tuple-element.43), channel_id=1, source_target_pairs={{1,0},{2,1},{3,2},{4,3},{5,4},{6,5},{7,6},{8,7},{9,8},{10,9},{11,1... | collective-permute-start | bytes 196616 | tf_op jit(solution)/shard_map/ppermute | solution.py:207
  93.0 6.4 %collective-permute-start.9 = (bf16[256,128]{1,0:T(8,128)(2,1)S(1)}, bf16[256,128]{1,0:T(8,128)(2,1)S(1)}, u32[]{:S(2)}, u32[]{:S(2)}) collective-permute-start(bf16[256,128]{1,0:T(8,128)(2,1)S(1)} %get-tuple-element.42), channel_id=1, source_target_pairs={{0,1},{1,2},{2,3},{3,4},{4,5},{5,6},{6,7},{7,8},{8,9},{9,10},{10,1... | collective-permute-start | bytes 196616 | tf_op jit(solution)/shard_map/ppermute | solution.py:206
  100.9 14.6 %all-to-all-start = ((f16[64,40,128]{2,1,0:T(8,128)(2,1)}), f16[64,40,128]{2,1,0:T(8,128)(2,1)S(1)}, u32[]{:S(2)}, u32[]{:S(2)}) async-start(f16[64,40,128]{2,1,0:T(8,128)(2,1)} %select_convert_fusion), calls=%async_computation | async-start | bytes 1310720 | tf_op jit(solution)/shard_map/all_to_all | solution.py:670
  115.6 8.7 %feature.1 = bf16[16,256,256]{2,1,0:T(8,128)(2,1)S(1)} custom-call(bf16[1,256,256]{2,1,0:T(8,128)(2,1)} %copy-done.6, bf16[16,256,256]{2,1,0:T(8,128)(2,1)} %copy-done, bf16[16,256,256]{2,1,0:T(8,128)(2,1)} %copy-done, bf16[16,256,256]{2,1,0:T(8,128)(2,1)} %copy-done, bf16[1,256,256]{2,1,0:T(8,128)(2,1)} %copy-done.7, ...), custom_call_target="tpu_custom_call" | custom-call | flops 8000000000 | bytes 24000000 | tf_op jit(solution)/shard_map/feature/pallas_call | solution.py:652
  124.3 4.2 %all-to-all-done = f16[64,40,128]{2,1,0:T(8,128)(2,1)S(1)} async-done(((f16[64,40,128]{2,1,0:T(8,128)(2,1)}), f16[64,40,128]{2,1,0:T(8,128)(2,1)S(1)}, u32[]{:S(2)}, u32[]{:S(2)}) %all-to-all-start) | async-done | bytes 655392 | tf_op jit(solution)/shard_map/all_to_all | solution.py:670
  129.0 19.4 %all_to_all.10 = f16[64,40,128]{2,1,0:T(8,128)(2,1)S(1)} all-to-all(f16[64,40,128]{2,1,0:T(8,128)(2,1)S(1)} %broadcast_in_dim.36), channel_id=1, replica_groups=mesh['row'=8,'pair'=8,'core'=2] {'row','pair'}, dimensions={0} | all-to-all | bytes 1310720 | tf_op jit(solution)/shard_map/all_to_all | solution.py:358
  149.1 2.5 %copy.22 = bf16[256,16,256]{2,1,0:T(8,128)(2,1)} copy(bf16[256,16,256]{2,0,1:T(8,128)(2,1)S(1)} %bitcast.21) | data formatting | bytes 4194304
  152.0 1.7 %place.1 = (f32[9,256,256]{2,1,0:T(8,128)}, f32[8,256]{1,0:T(8,128)}) custom-call(s32[1]{0:T(128)} %bitcast.7.core_ref, f32[64,40,128]{2,1,0:T(8,128)S(1)} %convert_multiply_fusion.1.own_ref, f32[64,40,128]{2,1,0:T(8,128)S(1)} %convert_multiply_fusion.other_ref), custom_call_target="tpu_custom_call" | custom-call | flops 2000000000 | bytes 6000000 | tf_op jit(solution)/shard_map/place/pallas_call | solution.py:361
  (67 shorter events, 14.3 us)
Async XLA Ops:
  2.8 1.6 %copy-start.12 = (bf16[256,16,256]{2,1,0:T(8,128)(2,1)S(1)}, bf16[256,16,256]{2,1,0:T(8,128)(2,1)}, u32[]{:S(2)}) copy-start(bf16[256,16,256]{2,1,0:T(8,128)(2,1)} %param.7) | copy-start | bytes 6291460
  5.2 13.7 %collective-permute-start.1 = (bf16[8,112,256]{2,1,0:T(8,128)(2,1)S(1)}, bf16[8,112,256]{2,1,0:T(8,128)(2,1)S(1)}, u32[]{:S(2)}, u32[]{:S(2)}) collective-permute-start(bf16[8,112,256]{2,1,0:T(8,128)(2,1)S(1)} %pad_maximum_fusion.1), channel_id=1, source_target_pairs={{16,0},{32,16},{48,32},{64,48},{80,64},{96,80},{112,96},{17,1},{33... | collective-permute-start | bytes 1376264 | tf_op jit(solution)/shard_map/ppermute | solution.py:207
  6.5 23.8 %copy-start.2 = (bf16[9,256,256]{2,1,0:T(8,128)(2,1)S(1)}, bf16[9,256,256]{2,1,0:T(8,128)(2,1)}, u32[]{:S(2)}) copy-start(bf16[9,256,256]{2,1,0:T(8,128)(2,1)} %taps_ref.3) | copy-start | bytes 3538948
  6.5 13.5 %collective-permute-start = (bf16[8,112,256]{2,1,0:T(8,128)(2,1)S(1)}, bf16[8,112,256]{2,1,0:T(8,128)(2,1)S(1)}, u32[]{:S(2)}, u32[]{:S(2)}) collective-permute-start(bf16[8,112,256]{2,1,0:T(8,128)(2,1)S(1)} %pad_maximum_fusion), channel_id=1, source_target_pairs={{0,16},{16,32},{32,48},{48,64},{64,80},{80,96},{96,112},{1,17},{17... | collective-permute-start | bytes 1376264 | tf_op jit(solution)/shard_map/ppermute | solution.py:206
  20.0 1.7 %copy-start.3 = (bf16[8,112,256]{2,1,0:T(8,128)(2,1)}, bf16[8,112,256]{2,1,0:T(8,128)(2,1)S(1)}, u32[]{:S(2)}) copy-start(bf16[8,112,256]{2,1,0:T(8,128)(2,1)S(1)} %collective-permute-done.up_ref) | copy-start | bytes 1376260
  21.7 18.5 %collective-permute-start.2 = (bf16[576,128]{1,0:T(8,128)(2,1)}, bf16[576,128]{1,0:T(8,128)(2,1)S(1)}, u32[]{:S(2)}, u32[]{:S(2)}) collective-permute-start(bf16[576,128]{1,0:T(8,128)(2,1)} %get-tuple-element.26), channel_id=1, source_target_pairs={{0,1},{1,2},{2,3},{3,4},{4,5},{5,6},{6,7},{7,8},{8,9},{9,10},{10,1... | collective-permute-start | bytes 442376 | tf_op jit(solution)/shard_map/ppermute | solution.py:206
  28.4 11.5 %copy-start.1 = (bf16[256,8]{0,1:T(8,128)(2,1)S(1)}, bf16[256,8]{0,1:T(8,128)(2,1)}, u32[]{:S(2)}) copy-start(bf16[256,8]{0,1:T(8,128)(2,1)} %param.9) | copy-start | bytes 12292
  28.4 11.7 %collective-permute-start.3 = (bf16[576,128]{1,0:T(8,128)(2,1)}, bf16[576,128]{1,0:T(8,128)(2,1)}, u32[]{:S(2)}, u32[]{:S(2)}) collective-permute-start(bf16[576,128]{1,0:T(8,128)(2,1)} %get-tuple-element.27), channel_id=1, source_target_pairs={{1,0},{2,1},{3,2},{4,3},{5,4},{6,5},{7,6},{8,7},{9,8},{10,9},{11,1... | collective-permute-start | bytes 442376 | tf_op jit(solution)/shard_map/ppermute | solution.py:207
  37.0 2.0 %copy-start.8 = (f32[16,256,256]{2,1,0:T(8,128)}, f32[16,256,256]{2,1,0:T(8,128)S(1)}, u32[]{:S(2)}) copy-start(f32[16,256,256]{2,1,0:T(8,128)S(1)} %get-tuple-element.31.pre_ref) | copy-start | bytes 12582916
  40.2 1.0 copy-start.4
  41.2 23.9 %copy-start.5 = (bf16[8,112,256]{2,1,0:T(8,128)(2,1)S(1)}, bf16[8,112,256]{2,1,0:T(8,128)(2,1)}, u32[]{:S(2)}) copy-start(bf16[8,112,256]{2,1,0:T(8,128)(2,1)} %copy-done.3) | copy-start | bytes 1376260
  41.2 23.9 %copy-start.9 = (f32[16,256,256]{2,1,0:T(8,128)S(1)}, f32[16,256,256]{2,1,0:T(8,128)}, u32[]{:S(2)}) copy-start(f32[16,256,256]{2,1,0:T(8,128)} %copy-done.8) | copy-start | bytes 12582916
  41.2 23.9 %copy-start.11 = (bf16[768,768]{1,0:T(8,128)(2,1)S(1)}, bf16[768,768]{1,0:T(8,128)(2,1)}, u32[]{:S(2)}) copy-start(bf16[768,768]{1,0:T(8,128)(2,1)} %copy-done.10) | copy-start | bytes 3538948
  54.7 14.4 %collective-permute-start.4 = (f32[8,8,384]{2,1,0:T(8,128)S(1)}, f32[8,8,384]{2,1,0:T(8,128)S(1)}, u32[]{:S(2)}, u32[]{:S(2)}) collective-permute-start(f32[8,8,384]{2,1,0:T(8,128)S(1)} %get-tuple-element.67), channel_id=1, source_target_pairs={{0,16},{16,32},{32,48},{48,64},{64,80},{80,96},{96,112},{1,17},{17... | collective-permute-start | bytes 294920 | tf_op jit(solution)/shard_map/ppermute | solution.py:206
  63.8 7.6 %collective-permute-start.5 = (f32[8,8,384]{2,1,0:T(8,128)S(1)}, f32[8,8,384]{2,1,0:T(8,128)S(1)}, u32[]{:S(2)}, u32[]{:S(2)}) collective-permute-start(f32[8,8,384]{2,1,0:T(8,128)S(1)} %get-tuple-element.66), channel_id=1, source_target_pairs={{16,0},{32,16},{48,32},{64,48},{80,64},{96,80},{112,96},{17,1},{33... | collective-permute-start | bytes 294920 | tf_op jit(solution)/shard_map/ppermute | solution.py:207
  75.6 14.3 %copy-start = (bf16[16,256,256]{2,1,0:T(8,128)(2,1)}, bf16[16,256,256]{2,1,0:T(8,128)(2,1)S(1)}, u32[]{:S(2)}) copy-start(bf16[16,256,256]{2,1,0:T(8,128)(2,1)S(1)} %get-tuple-element.34.back_ref.mid_ref.above_ref.below_ref) | copy-start | bytes 6291460
  75.6 14.0 %collective-permute-start.6 = (bf16[1,256,256]{2,1,0:T(8,128)(2,1)S(1)}, bf16[1,256,256]{2,1,0:T(8,128)(2,1)S(1)}, u32[]{:S(2)}, u32[]{:S(2)}) collective-permute-start(bf16[1,256,256]{2,1,0:T(8,128)(2,1)S(1)} %get-tuple-element.61), channel_id=1, source_target_pairs={{0,16},{16,32},{32,48},{48,64},{64,80},{80,96},{96,112},{1,17},{17... | collective-permute-start | bytes 393224 | tf_op jit(solution)/shard_map/ppermute | solution.py:206
  79.9 9.7 %collective-permute-start.7 = (bf16[1,256,256]{2,1,0:T(8,128)(2,1)S(1)}, bf16[1,256,256]{2,1,0:T(8,128)(2,1)S(1)}, u32[]{:S(2)}, u32[]{:S(2)}) collective-permute-start(bf16[1,256,256]{2,1,0:T(8,128)(2,1)S(1)} %get-tuple-element.60), channel_id=1, source_target_pairs={{16,0},{32,16},{48,32},{64,48},{80,64},{96,80},{112,96},{17,1},{33... | collective-permute-start | bytes 393224 | tf_op jit(solution)/shard_map/ppermute | solution.py:207
  89.6 1.0 copy-start.6
  89.6 9.8 %collective-permute-start.8 = (f32[64,40,128]{2,1,0:T(8,128)S(1)}, f32[64,40,128]{2,1,0:T(8,128)S(1)}, u32[]{:S(2)}, u32[]{:S(2)}) collective-permute-start(f32[64,40,128]{2,1,0:T(8,128)S(1)} %get-tuple-element.39), channel_id=1, source_target_pairs={{0,1},{1,0},{2,3},{3,2},{4,5},{5,4},{6,7},{7,6},{8,9},{9,8},{10,11... | collective-permute-start | bytes 3932168 | tf_op jit(solution)/shard_map/ppermute | solution.py:646
  90.6 24.9 %collective-permute-start.10 = (bf16[256,128]{1,0:T(8,128)(2,1)S(1)}, bf16[256,128]{1,0:T(8,128)(2,1)S(1)}, u32[]{:S(2)}, u32[]{:S(2)}) collective-permute-start(bf16[256,128]{1,0:T(8,128)(2,1)S(1)} %get-tuple-element.43), channel_id=1, source_target_pairs={{1,0},{2,1},{3,2},{4,3},{5,4},{6,5},{7,6},{8,7},{9,8},{10,9},{11,1... | collective-permute-start | bytes 196616 | tf_op jit(solution)/shard_map/ppermute | solution.py:207
  93.0 22.6 %collective-permute-start.9 = (bf16[256,128]{1,0:T(8,128)(2,1)S(1)}, bf16[256,128]{1,0:T(8,128)(2,1)S(1)}, u32[]{:S(2)}, u32[]{:S(2)}) collective-permute-start(bf16[256,128]{1,0:T(8,128)(2,1)S(1)} %get-tuple-element.42), channel_id=1, source_target_pairs={{0,1},{1,2},{2,3},{3,4},{4,5},{5,6},{6,7},{7,8},{8,9},{9,10},{10,1... | collective-permute-start | bytes 196616 | tf_op jit(solution)/shard_map/ppermute | solution.py:206
  100.9 27.5 %all-to-all-start = ((f16[64,40,128]{2,1,0:T(8,128)(2,1)}), f16[64,40,128]{2,1,0:T(8,128)(2,1)S(1)}, u32[]{:S(2)}, u32[]{:S(2)}) async-start(f16[64,40,128]{2,1,0:T(8,128)(2,1)} %select_convert_fusion), calls=%async_computation | async-start | bytes 1310720 | tf_op jit(solution)/shard_map/all_to_all | solution.py:670
  148.4 3.4 %collective-permute-start.11 = (f16[64,40,128]{2,1,0:T(8,128)(2,1)S(1)}, f16[64,40,128]{2,1,0:T(8,128)(2,1)S(1)}, u32[]{:S(2)}, u32[]{:S(2)}) collective-permute-start(f16[64,40,128]{2,1,0:T(8,128)(2,1)S(1)} %all_to_all.10), channel_id=1, source_target_pairs={{0,1},{1,0},{2,3},{3,2},{4,5},{5,4},{6,7},{7,6},{8,9},{9,8},{10,11... | collective-permute-start | bytes 1966088 | tf_op jit(solution)/shard_map/ppermute | solution.py:359
  (2 other events, 2.0 us)

commit v6 on v5

--- a/solution.py
+++ b/solution.py
@@ -175,14 +175,14 @@
         middle[row] = sweep_row(lambda o: weights_ref[o, pl.ds(row, 1), :], row + 4, read_row)
         return carry
 
-    lax.fori_loop(0, rows + 8, first, 0, unroll=4)
+    lax.fori_loop(0, rows + 8, first, 0, unroll=8)
 
     def second(row, carry):
         value = sweep_row(lambda o: weights_ref[o, pl.ds(row + 4, 1), :], row + 4, lambda r: middle[r])
         out_ref[row] = value[:, : out_ref.shape[2]]
         return carry
 
-    lax.fori_loop(0, rows, second, 0, unroll=4)
+    lax.fori_loop(0, rows, second, 0, unroll=8)
 
 
 def finish_kernel(weights_ref, up_ref, mid_ref, down_ref, out_ref, probs, next_probs):
@@ -264,7 +264,7 @@
         name="affinity",
         compiler_params=vmem_of(20),
         cost_estimate=cost_of(12),
-    )(place, up, mid, down, left, right)
+    )(place, *in_hbm(up, mid, down), left, right)
     return current, weights
 
 

time: 154 us -> 152 us (0.987)
  Pallas kernels: 49.5 us -> 46.7 us
    pallas_call x4, Pallas kernels: 20.2 us -> 18.4 us  [row_call(): pl.pallas_call(kernel, grid=(rows // STEP_ROWS,), in_specs=[pl.BlockSpec(...]
    unnamed x31 -> x35, local copies, waits for them, and re-layouts: 10.7 us -> 9.95 us
  transfers between devices with their start and end apart: 13 -> 13, of which waited for: 4 -> 4; matrix products, arithmetic and copies ran while one was open for 3% -> 3% of each run, Pallas kernels for 19% -> 18%
where the time goes in v6:
time: 152 us
  starting transfers between devices  54.7 us (36%)
  Pallas kernels  46.7 us (31%)
  blocking collectives  18.7 us (12%)
  waiting for transfers between devices  16.6 us (11%)
  local copies, waits for them, and re-layouts  10.2 us (7%)
  other arithmetic  3.55 us (2%)
    ppermute x5, starting transfers between devices, pass_on(): return lax.ppermute(cells, axis, [(i, i + 1) for i in range(ends)])  31.1 us
    all_to_all x1, blocking collectives, gather_all(): own = lax.all_to_all(spread, CHIPS, split_axis=0, concat_axis=0, tiled=True)  18.7 us
    pallas_call x4, Pallas kernels, row_call(): pl.pallas_call(kernel, grid=(rows // STEP_ROWS,), in_specs=[pl.BlockSpec(...  18.4 us
    all_to_all x1, starting transfers between devices, local_step(): lax.all_to_all(packed, CHIPS, split_axis=0, concat_axis=0, tiled=True)  13.7 us
    pallas_call x1, Pallas kernels, refine(): pl.pallas_call(functools.partial(affinity_kernel, full_rows=rows * lax.ax...  13.6 us
    ppermute x5, waiting for transfers between devices, pass_on(): return lax.ppermute(cells, axis, [(i + 1, i) for i in range(ends)])  10.8 us
    unnamed x35, local copies, waits for them, and re-layouts  9.95 us
    pallas_call x1, Pallas kernels, local_step(): pl.pallas_call(feature_kernel, grid=(steps,), in_specs=[whole(back_up), p...  8.73 us
  transfers between devices with their start and end apart: 13, of which 4 were waited for; matrix products, arithmetic and copies ran while one was open for 3% of the time, Pallas kernels for 18%

profile of v6, /device:TPU:1, one launch (start us, length us, event | category | flops | bytes accessed | tf_op | source)
XLA Modules:
  0.0 151.5 jit_solution(9341223779945591318)
XLA Ops:
  3.0 1.7 %copy-done.14 = bf16[256,16,256]{2,1,0:T(8,128)(2,1)S(1)} copy-done((bf16[256,16,256]{2,1,0:T(8,128)(2,1)S(1)}, bf16[256,16,256]{2,1,0:T(8,128)(2,1)}, u32[]{:S(2)}) %copy-start.14) | copy-done | bytes 2097176
  6.8 4.7 %collective-permute-start = (bf16[8,112,256]{2,1,0:T(8,128)(2,1)S(1)}, bf16[8,112,256]{2,1,0:T(8,128)(2,1)S(1)}, u32[]{:S(2)}, u32[]{:S(2)}) collective-permute-start(bf16[8,112,256]{2,1,0:T(8,128)(2,1)S(1)} %pad_maximum_fusion), channel_id=1, source_target_pairs={{0,16},{16,32},{32,48},{48,64},{64,80},{80,96},{96,112},{1,17},{17... | collective-permute-start | bytes 1376264 | tf_op jit(solution)/shard_map/ppermute | solution.py:206
  11.5 7.7 %collective-permute-done.1.down_ref = bf16[8,112,256]{2,1,0:T(8,128)(2,1)S(1)} collective-permute-done((bf16[8,112,256]{2,1,0:T(8,128)(2,1)S(1)}, bf16[8,112,256]{2,1,0:T(8,128)(2,1)S(1)}, u32[]{:S(2)}, u32[]{:S(2)}) %collective-permute-start.1) | collective-permute-done | bytes 458784 | tf_op jit(solution)/shard_map/ppermute | solution.py:207
  21.3 6.7 %collective-permute-start.2 = (bf16[576,128]{1,0:T(8,128)(2,1)S(1)}, bf16[576,128]{1,0:T(8,128)(2,1)S(1)}, u32[]{:S(2)}, u32[]{:S(2)}) collective-permute-start(bf16[576,128]{1,0:T(8,128)(2,1)S(1)} %get-tuple-element.26), channel_id=1, source_target_pairs={{0,1},{1,2},{2,3},{3,4},{4,5},{5,6},{6,7},{7,8},{8,9},{9,10},{10,1... | collective-permute-start | bytes 442376 | tf_op jit(solution)/shard_map/ppermute | solution.py:206
  28.0 1.9 %collective-permute-start.3 = (bf16[576,128]{1,0:T(8,128)(2,1)S(1)}, bf16[576,128]{1,0:T(8,128)(2,1)S(1)}, u32[]{:S(2)}, u32[]{:S(2)}) collective-permute-start(bf16[576,128]{1,0:T(8,128)(2,1)S(1)} %get-tuple-element.27), channel_id=1, source_target_pairs={{1,0},{2,1},{3,2},{4,3},{5,4},{6,5},{7,6},{8,7},{9,8},{10,9},{11,1... | collective-permute-start | bytes 442376 | tf_op jit(solution)/shard_map/ppermute | solution.py:207
  29.9 6.6 %shard_map.84 = (f32[16,256,256]{2,1,0:T(8,128)S(1)}, bf16[768,768]{1,0:T(8,128)(2,1)S(1)}) custom-call(bf16[16,256,256]{2,1,0:T(8,128)(2,1)S(1)} %bitcast.19, bf16[9,256,256]{2,1,0:T(8,128)(2,1)S(1)} %copy-done.3), custom_call_target="tpu_custom_call" | custom-call | flops 8999999488 | bytes 27000000 | tf_op jit(solution)/shard_map/pallas_call | solution.py:581
  36.6 2.0 %copy-done.10 = f32[16,256,256]{2,1,0:T(8,128)} copy-done((f32[16,256,256]{2,1,0:T(8,128)}, f32[16,256,256]{2,1,0:T(8,128)S(1)}, u32[]{:S(2)}) %copy-start.10) | copy-done | bytes 4194328
  39.8 13.6 %affinity.1 = (f32[16,8,384]{2,1,0:T(8,128)S(1)}, f32[25,24,384]{2,1,0:T(8,128)S(1)}) custom-call(s32[2]{0:T(128)S(1)} %pad_add_fusion.place_ref, bf16[8,112,256]{2,1,0:T(8,128)(2,1)} %copy-done.6, bf16[16,80,256]{2,1,0:T(8,128)(2,1)} %copy-done, bf16[8,112,256]{2,1,0:T(8,128)(2,1)} %copy-done.4, bf16[576,128]{1,0:T(8,128)(2,1)S(1)} %collective-permute-done.2.left_ref, ...), custom_call_target="tpu_custom_call" | custom-call | flops 12000000000 | bytes 36000000 | tf_op jit(solution)/shard_map/affinity/pallas_call | solution.py:243
  53.4 9.0 %collective-permute-start.4 = (f32[8,8,384]{2,1,0:T(8,128)S(1)}, f32[8,8,384]{2,1,0:T(8,128)S(1)}, u32[]{:S(2)}, u32[]{:S(2)}) collective-permute-start(f32[8,8,384]{2,1,0:T(8,128)S(1)} %get-tuple-element.67), channel_id=1, source_target_pairs={{0,16},{16,32},{32,48},{48,64},{64,80},{80,96},{96,112},{1,17},{17... | collective-permute-start | bytes 294920 | tf_op jit(solution)/shard_map/ppermute | solution.py:206
  62.4 1.3 collective-permute-start.5
  63.8 3.1 %shard_map.85 = (f32[16,256,256]{2,1,0:T(8,128)S(1)}, bf16[16,256,256]{2,1,0:T(8,128)(2,1)S(1)}, f32[16,8,256]{2,1,0:T(8,128)S(1)}) custom-call(bf16[8,112,256]{2,1,0:T(8,128)(2,1)S(1)} %copy-done.7, bf16[8,112,256]{2,1,0:T(8,128)(2,1)S(1)} %copy-done.5, bf16[576,128]{1,0:T(8,128)(2,1)S(1)} %collective-permute-done.2.left_ref, ...), custom_call_target="tpu_custom_call" | custom-call | flops 7000000000 | bytes 21000000 | tf_op jit(solution)/shard_map/pallas_call | solution.py:581
  66.9 3.1 %collective-permute-done.5.down_ref = f32[8,8,384]{2,1,0:T(8,128)S(1)} collective-permute-done((f32[8,8,384]{2,1,0:T(8,128)S(1)}, f32[8,8,384]{2,1,0:T(8,128)S(1)}, u32[]{:S(2)}, u32[]{:S(2)}) %collective-permute-start.5) | collective-permute-done | bytes 98336 | tf_op jit(solution)/shard_map/ppermute | solution.py:207
  70.0 2.7 %finish.1.refined_ref = f32[16,8,256]{2,1,0:T(8,128)S(1)} custom-call(f32[25,24,384]{2,1,0:T(8,128)S(1)} %get-tuple-element.28.weights_ref, f32[8,8,384]{2,1,0:T(8,128)S(1)} %collective-permute-done.4.up_ref, f32[16,8,384]{2,1,0:T(8,128)S(1)} %get-tuple-element.29.mid_ref, f32[8,8,384]{2,1,0:T(8,128)S(1)} %collective-permute-done.5.down_ref), custom_call_target="tpu_custom_call" | custom-call | flops 4000000000 | bytes 12000000 | tf_op jit(solution)/shard_map/finish/pallas_call | solution.py:274
  73.9 4.3 %collective-permute-start.6 = (bf16[1,256,256]{2,1,0:T(8,128)(2,1)S(1)}, bf16[1,256,256]{2,1,0:T(8,128)(2,1)S(1)}, u32[]{:S(2)}, u32[]{:S(2)}) collective-permute-start(bf16[1,256,256]{2,1,0:T(8,128)(2,1)S(1)} %get-tuple-element.61), channel_id=1, source_target_pairs={{0,16},{16,32},{32,48},{48,64},{64,80},{80,96},{96,112},{1,17},{17... | collective-permute-start | bytes 393224 | tf_op jit(solution)/shard_map/ppermute | solution.py:206
  79.5 7.5 %shard_map.87 = (f32[64,40,128]{2,1,0:T(8,128)S(1)}, f32[64,40,128]{2,1,0:T(8,128)S(1)}) custom-call(s32[1]{0:T(128)} %bitcast.7.core_ref, bf16[8,112,256]{2,1,0:T(8,128)(2,1)S(1)} %copy-done.7, bf16[16,256,256]{2,1,0:T(8,128)(2,1)S(1)} %bitcast.20, bf16[8,112,256]{2,1,0:T(8,128)(2,1)S(1)} %copy-done.5, ...), custom_call_target="tpu_custom_call" | custom-call | flops 8999999488 | bytes 27000000 | tf_op jit(solution)/shard_map/pallas_call | solution.py:581
  88.0 2.4 %collective-permute-start.10 = (bf16[256,128]{1,0:T(8,128)(2,1)S(1)}, bf16[256,128]{1,0:T(8,128)(2,1)S(1)}, u32[]{:S(2)}, u32[]{:S(2)}) collective-permute-start(bf16[256,128]{1,0:T(8,128)(2,1)S(1)} %get-tuple-element.43), channel_id=1, source_target_pairs={{1,0},{2,1},{3,2},{4,3},{5,4},{6,5},{7,6},{8,7},{9,8},{10,9},{11,1... | collective-permute-start | bytes 196616 | tf_op jit(solution)/shard_map/ppermute | solution.py:207
  90.4 6.4 %collective-permute-start.9 = (bf16[256,128]{1,0:T(8,128)(2,1)S(1)}, bf16[256,128]{1,0:T(8,128)(2,1)S(1)}, u32[]{:S(2)}, u32[]{:S(2)}) collective-permute-start(bf16[256,128]{1,0:T(8,128)(2,1)S(1)} %get-tuple-element.42), channel_id=1, source_target_pairs={{0,1},{1,2},{2,3},{3,4},{4,5},{5,6},{6,7},{7,8},{8,9},{9,10},{10,1... | collective-permute-start | bytes 196616 | tf_op jit(solution)/shard_map/ppermute | solution.py:206
  98.4 13.7 %all-to-all-start = ((f16[64,40,128]{2,1,0:T(8,128)(2,1)}), f16[64,40,128]{2,1,0:T(8,128)(2,1)S(1)}, u32[]{:S(2)}, u32[]{:S(2)}) async-start(f16[64,40,128]{2,1,0:T(8,128)(2,1)} %select_convert_fusion), calls=%async_computation | async-start | bytes 1310720 | tf_op jit(solution)/shard_map/all_to_all | solution.py:670
  112.1 8.7 %feature.1 = bf16[16,256,256]{2,1,0:T(8,128)(2,1)S(1)} custom-call(bf16[1,256,256]{2,1,0:T(8,128)(2,1)} %copy-done.8, bf16[16,256,256]{2,1,0:T(8,128)(2,1)} %copy-done.1, bf16[16,256,256]{2,1,0:T(8,128)(2,1)} %copy-done.1, bf16[16,256,256]{2,1,0:T(8,128)(2,1)} %copy-done.1, bf16[1,256,256]{2,1,0:T(8,128)(2,1)} %copy-done.9, ...), custom_call_target="tpu_custom_call" | custom-call | flops 8000000000 | bytes 24000000 | tf_op jit(solution)/shard_map/feature/pallas_call | solution.py:652
  120.8 4.7 %all-to-all-done = f16[64,40,128]{2,1,0:T(8,128)(2,1)S(1)} async-done(((f16[64,40,128]{2,1,0:T(8,128)(2,1)}), f16[64,40,128]{2,1,0:T(8,128)(2,1)S(1)}, u32[]{:S(2)}, u32[]{:S(2)}) %all-to-all-start) | async-done | bytes 655392 | tf_op jit(solution)/shard_map/all_to_all | solution.py:670
  126.1 18.7 %all_to_all.10 = f16[64,40,128]{2,1,0:T(8,128)(2,1)S(1)} all-to-all(f16[64,40,128]{2,1,0:T(8,128)(2,1)S(1)} %broadcast_in_dim.36), channel_id=1, replica_groups=mesh['row'=8,'pair'=8,'core'=2] {'row','pair'}, dimensions={0} | all-to-all | bytes 1310720 | tf_op jit(solution)/shard_map/all_to_all | solution.py:358
  144.8 1.4 collective-permute-start.11
  146.9 2.5 %copy.22 = bf16[256,16,256]{2,1,0:T(8,128)(2,1)} copy(bf16[256,16,256]{2,0,1:T(8,128)(2,1)S(1)} %bitcast.21) | data formatting | bytes 4194304
  149.8 1.7 %place.1 = (f32[9,256,256]{2,1,0:T(8,128)}, f32[8,256]{1,0:T(8,128)}) custom-call(s32[1]{0:T(128)} %bitcast.7.core_ref, f32[64,40,128]{2,1,0:T(8,128)S(1)} %convert_multiply_fusion.1.own_ref, f32[64,40,128]{2,1,0:T(8,128)S(1)} %convert_multiply_fusion.other_ref), custom_call_target="tpu_custom_call" | custom-call | flops 2000000000 | bytes 6000000 | tf_op jit(solution)/shard_map/place/pallas_call | solution.py:361
  (71 shorter events, 14.3 us)
Async XLA Ops:
  2.8 1.8 %copy-start.14 = (bf16[256,16,256]{2,1,0:T(8,128)(2,1)S(1)}, bf16[256,16,256]{2,1,0:T(8,128)(2,1)}, u32[]{:S(2)}) copy-start(bf16[256,16,256]{2,1,0:T(8,128)(2,1)} %param.7) | copy-start | bytes 6291460
  2.9 17.4 %copy-start = (bf16[16,80,256]{2,1,0:T(8,128)(2,1)}, bf16[16,80,256]{2,1,0:T(8,128)(2,1)S(1)}, u32[]{:S(2)}) copy-start(bf16[16,80,256]{2,1,0:T(8,128)(2,1)S(1)} %maximum_bitcast_fusion.mid_ref) | copy-start | bytes 1966084
  5.4 13.7 %collective-permute-start.1 = (bf16[8,112,256]{2,1,0:T(8,128)(2,1)S(1)}, bf16[8,112,256]{2,1,0:T(8,128)(2,1)S(1)}, u32[]{:S(2)}, u32[]{:S(2)}) collective-permute-start(bf16[8,112,256]{2,1,0:T(8,128)(2,1)S(1)} %pad_maximum_fusion.1), channel_id=1, source_target_pairs={{16,0},{32,16},{48,32},{64,48},{80,64},{96,80},{112,96},{17,1},{33... | collective-permute-start | bytes 1376264 | tf_op jit(solution)/shard_map/ppermute | solution.py:207
  6.8 23.2 %copy-start.3 = (bf16[9,256,256]{2,1,0:T(8,128)(2,1)S(1)}, bf16[9,256,256]{2,1,0:T(8,128)(2,1)}, u32[]{:S(2)}) copy-start(bf16[9,256,256]{2,1,0:T(8,128)(2,1)} %taps_ref.3) | copy-start | bytes 3538948
  6.8 13.5 %collective-permute-start = (bf16[8,112,256]{2,1,0:T(8,128)(2,1)S(1)}, bf16[8,112,256]{2,1,0:T(8,128)(2,1)S(1)}, u32[]{:S(2)}, u32[]{:S(2)}) collective-permute-start(bf16[8,112,256]{2,1,0:T(8,128)(2,1)S(1)} %pad_maximum_fusion), channel_id=1, source_target_pairs={{0,16},{16,32},{32,48},{48,64},{64,80},{80,96},{96,112},{1,17},{17... | collective-permute-start | bytes 1376264 | tf_op jit(solution)/shard_map/ppermute | solution.py:206
  19.2 2.1 %copy-start.4 = (bf16[8,112,256]{2,1,0:T(8,128)(2,1)}, bf16[8,112,256]{2,1,0:T(8,128)(2,1)S(1)}, u32[]{:S(2)}) copy-start(bf16[8,112,256]{2,1,0:T(8,128)(2,1)S(1)} %collective-permute-done.1.down_ref) | copy-start | bytes 1376260
  21.3 18.5 %collective-permute-start.2 = (bf16[576,128]{1,0:T(8,128)(2,1)S(1)}, bf16[576,128]{1,0:T(8,128)(2,1)S(1)}, u32[]{:S(2)}, u32[]{:S(2)}) collective-permute-start(bf16[576,128]{1,0:T(8,128)(2,1)S(1)} %get-tuple-element.26), channel_id=1, source_target_pairs={{0,1},{1,2},{2,3},{3,4},{4,5},{5,6},{6,7},{7,8},{8,9},{9,10},{10,1... | collective-permute-start | bytes 442376 | tf_op jit(solution)/shard_map/ppermute | solution.py:206
  28.0 11.5 %copy-start.2 = (bf16[256,8]{0,1:T(8,128)(2,1)S(1)}, bf16[256,8]{0,1:T(8,128)(2,1)}, u32[]{:S(2)}) copy-start(bf16[256,8]{0,1:T(8,128)(2,1)} %param.9) | copy-start | bytes 12292
  28.0 11.8 %collective-permute-start.3 = (bf16[576,128]{1,0:T(8,128)(2,1)S(1)}, bf16[576,128]{1,0:T(8,128)(2,1)S(1)}, u32[]{:S(2)}, u32[]{:S(2)}) collective-permute-start(bf16[576,128]{1,0:T(8,128)(2,1)S(1)} %get-tuple-element.27), channel_id=1, source_target_pairs={{1,0},{2,1},{3,2},{4,3},{5,4},{6,5},{7,6},{8,7},{9,8},{10,9},{11,1... | collective-permute-start | bytes 442376 | tf_op jit(solution)/shard_map/ppermute | solution.py:207
  36.6 2.0 %copy-start.10 = (f32[16,256,256]{2,1,0:T(8,128)}, f32[16,256,256]{2,1,0:T(8,128)S(1)}, u32[]{:S(2)}) copy-start(f32[16,256,256]{2,1,0:T(8,128)S(1)} %get-tuple-element.31.pre_ref) | copy-start | bytes 12582916
  39.7 24.0 %copy-start.5 = (bf16[8,112,256]{2,1,0:T(8,128)(2,1)S(1)}, bf16[8,112,256]{2,1,0:T(8,128)(2,1)}, u32[]{:S(2)}) copy-start(bf16[8,112,256]{2,1,0:T(8,128)(2,1)} %copy-done.4) | copy-start | bytes 1376260
  39.7 24.0 %copy-start.7 = (bf16[8,112,256]{2,1,0:T(8,128)(2,1)S(1)}, bf16[8,112,256]{2,1,0:T(8,128)(2,1)}, u32[]{:S(2)}) copy-start(bf16[8,112,256]{2,1,0:T(8,128)(2,1)} %copy-done.6) | copy-start | bytes 1376260
  39.7 24.0 %copy-start.11 = (f32[16,256,256]{2,1,0:T(8,128)S(1)}, f32[16,256,256]{2,1,0:T(8,128)}, u32[]{:S(2)}) copy-start(f32[16,256,256]{2,1,0:T(8,128)} %copy-done.10) | copy-start | bytes 12582916
  39.7 24.0 %copy-start.13 = (bf16[768,768]{1,0:T(8,128)(2,1)S(1)}, bf16[768,768]{1,0:T(8,128)(2,1)}, u32[]{:S(2)}) copy-start(bf16[768,768]{1,0:T(8,128)(2,1)} %copy-done.12) | copy-start | bytes 3538948
  53.4 13.5 %collective-permute-start.4 = (f32[8,8,384]{2,1,0:T(8,128)S(1)}, f32[8,8,384]{2,1,0:T(8,128)S(1)}, u32[]{:S(2)}, u32[]{:S(2)}) collective-permute-start(f32[8,8,384]{2,1,0:T(8,128)S(1)} %get-tuple-element.67), channel_id=1, source_target_pairs={{0,16},{16,32},{32,48},{48,64},{64,80},{80,96},{96,112},{1,17},{17... | collective-permute-start | bytes 294920 | tf_op jit(solution)/shard_map/ppermute | solution.py:206
  62.4 7.6 %collective-permute-start.5 = (f32[8,8,384]{2,1,0:T(8,128)S(1)}, f32[8,8,384]{2,1,0:T(8,128)S(1)}, u32[]{:S(2)}, u32[]{:S(2)}) collective-permute-start(f32[8,8,384]{2,1,0:T(8,128)S(1)} %get-tuple-element.66), channel_id=1, source_target_pairs={{16,0},{32,16},{48,32},{64,48},{80,64},{96,80},{112,96},{17,1},{33... | collective-permute-start | bytes 294920 | tf_op jit(solution)/shard_map/ppermute | solution.py:207
  73.9 13.4 %copy-start.1 = (bf16[16,256,256]{2,1,0:T(8,128)(2,1)}, bf16[16,256,256]{2,1,0:T(8,128)(2,1)S(1)}, u32[]{:S(2)}) copy-start(bf16[16,256,256]{2,1,0:T(8,128)(2,1)S(1)} %get-tuple-element.34.back_ref.mid_ref.above_ref.below_ref) | copy-start | bytes 6291460
  73.9 13.0 %collective-permute-start.6 = (bf16[1,256,256]{2,1,0:T(8,128)(2,1)S(1)}, bf16[1,256,256]{2,1,0:T(8,128)(2,1)S(1)}, u32[]{:S(2)}, u32[]{:S(2)}) collective-permute-start(bf16[1,256,256]{2,1,0:T(8,128)(2,1)S(1)} %get-tuple-element.61), channel_id=1, source_target_pairs={{0,16},{16,32},{32,48},{48,64},{64,80},{80,96},{96,112},{1,17},{17... | collective-permute-start | bytes 393224 | tf_op jit(solution)/shard_map/ppermute | solution.py:206
  78.2 8.8 %collective-permute-start.7 = (bf16[1,256,256]{2,1,0:T(8,128)(2,1)S(1)}, bf16[1,256,256]{2,1,0:T(8,128)(2,1)S(1)}, u32[]{:S(2)}, u32[]{:S(2)}) collective-permute-start(bf16[1,256,256]{2,1,0:T(8,128)(2,1)S(1)} %get-tuple-element.60), channel_id=1, source_target_pairs={{16,0},{32,16},{48,32},{64,48},{80,64},{96,80},{112,96},{17,1},{33... | collective-permute-start | bytes 393224 | tf_op jit(solution)/shard_map/ppermute | solution.py:207
  87.0 9.8 %collective-permute-start.8 = (f32[64,40,128]{2,1,0:T(8,128)S(1)}, f32[64,40,128]{2,1,0:T(8,128)S(1)}, u32[]{:S(2)}, u32[]{:S(2)}) collective-permute-start(f32[64,40,128]{2,1,0:T(8,128)S(1)} %get-tuple-element.39), channel_id=1, source_target_pairs={{0,1},{1,0},{2,3},{3,2},{4,5},{5,4},{6,7},{7,6},{8,9},{9,8},{10,11... | collective-permute-start | bytes 3932168 | tf_op jit(solution)/shard_map/ppermute | solution.py:646
  88.0 24.1 %collective-permute-start.10 = (bf16[256,128]{1,0:T(8,128)(2,1)S(1)}, bf16[256,128]{1,0:T(8,128)(2,1)S(1)}, u32[]{:S(2)}, u32[]{:S(2)}) collective-permute-start(bf16[256,128]{1,0:T(8,128)(2,1)S(1)} %get-tuple-element.43), channel_id=1, source_target_pairs={{1,0},{2,1},{3,2},{4,3},{5,4},{6,5},{7,6},{8,7},{9,8},{10,9},{11,1... | collective-permute-start | bytes 196616 | tf_op jit(solution)/shard_map/ppermute | solution.py:207
  90.4 21.7 %collective-permute-start.9 = (bf16[256,128]{1,0:T(8,128)(2,1)S(1)}, bf16[256,128]{1,0:T(8,128)(2,1)S(1)}, u32[]{:S(2)}, u32[]{:S(2)}) collective-permute-start(bf16[256,128]{1,0:T(8,128)(2,1)S(1)} %get-tuple-element.42), channel_id=1, source_target_pairs={{0,1},{1,2},{2,3},{3,4},{4,5},{5,6},{6,7},{7,8},{8,9},{9,10},{10,1... | collective-permute-start | bytes 196616 | tf_op jit(solution)/shard_map/ppermute | solution.py:206
  98.4 27.2 %all-to-all-start = ((f16[64,40,128]{2,1,0:T(8,128)(2,1)}), f16[64,40,128]{2,1,0:T(8,128)(2,1)S(1)}, u32[]{:S(2)}, u32[]{:S(2)}) async-start(f16[64,40,128]{2,1,0:T(8,128)(2,1)} %select_convert_fusion), calls=%async_computation | async-start | bytes 1310720 | tf_op jit(solution)/shard_map/all_to_all | solution.py:670
  144.8 4.8 %collective-permute-start.11 = (f16[64,40,128]{2,1,0:T(8,128)(2,1)S(1)}, f16[64,40,128]{2,1,0:T(8,128)(2,1)S(1)}, u32[]{:S(2)}, u32[]{:S(2)}) collective-permute-start(f16[64,40,128]{2,1,0:T(8,128)(2,1)S(1)} %all_to_all.10), channel_id=1, source_target_pairs={{0,1},{1,0},{2,3},{3,2},{4,5},{5,4},{6,7},{7,6},{8,9},{9,8},{10,11... | collective-permute-start | bytes 1966088 | tf_op jit(solution)/shard_map/ppermute | solution.py:359
  (4 other events, 4.0 us)

commit v7 on v6

--- a/solution.py
+++ b/solution.py
@@ -386,7 +386,7 @@
     return jnp.dot(weights, jnp.concatenate(moved, axis=0), preferred_element_type=jnp.float32)
 
 
-STEP_ROWS = 4
+STEP_ROWS = 8
 
 
 def joined(parts, out):
@@ -571,7 +571,7 @@
     edge = jax.ShapeDtypeStruct((cells.shape[1], 128), cells.dtype)
     to_left, to_right = pl.pallas_call(
         unit_edges_kernel, out_shape=(edge, edge), name="unit_edges",
-        compiler_params=vmem_of(24),
+        compiler_params=vmem_of(40),
         cost_estimate=cost_of(1),
     )(up, cells, down)
     return pass_on(to_right, COL, 1), pass_on(to_left, COL, -1)
@@ -606,7 +606,7 @@
             jax.ShapeDtypeStruct((rows, hidden_size, cols), f32),
             jax.ShapeDtypeStruct((3 * hidden_size, 3 * channels), bf16),
         ],
-        [True, False], [pltpu.VMEM((rows + 2, channels, cols), bf16)], 24, 9,
+        [True, False], [pltpu.VMEM((rows + 2, channels, cols), bf16)], 44, 9,
     )
     left, right = share_cols(mid, up, down, student)
     halo = (up, student, down, left, right)
@@ -621,7 +621,7 @@
             jax.ShapeDtypeStruct((rows, classes, cols), f32),
         ],
         [True] * 3,
-        [pltpu.VMEM((hidden_size, 128), f32)] * 2 + [pltpu.VMEM((2, hidden_size, cols), f32)], 24, 7,
+        [pltpu.VMEM((hidden_size, 128), f32)] * 2 + [pltpu.VMEM((2, hidden_size, cols), f32)], 48, 7,
     )
     refined = finish(current, weights, cols, *current_rows)
     back, error = row_call(
@@ -630,7 +630,7 @@
             jax.ShapeDtypeStruct((rows, hidden_size, cols), bf16),
             jax.ShapeDtypeStruct((rows, classes, cols), bf16),
         ],
-        [True] * 2, [], 24, 2,
+        [True] * 2, [], 40, 2,
     )
     back_up, back_down = unit_rows(back)
     core = lax.axis_index("core").astype(jnp.int32).reshape(1)
@@ -640,7 +640,7 @@
         [chunks, chunks], [False] * 2,
         [pltpu.VMEM((rows + 2, channels, cols), bf16)]
         + [pltpu.VMEM((hidden_size, 128), f32)] * 2
-        + [pltpu.VMEM((3 * channels, 3 * hidden_size), f32), pltpu.VMEM((classes, hidden_size), f32)], 36, 9,
+        + [pltpu.VMEM((3 * channels, 3 * hidden_size), f32), pltpu.VMEM((classes, hidden_size), f32)], 56, 9,
     )
     back_up, back_down, sent = lax.optimization_barrier((back_up, back_down, sent))
     other = lax.ppermute(sent, "core", PARTNER)
@@ -664,7 +664,7 @@
         scratch_shapes=[pltpu.VMEM((channels, 128), f32)] * 2
         + [pltpu.VMEM((3 * channels, 3 * hidden_size), bf16)],
         name="feature",
-        compiler_params=vmem_of(24),
+        compiler_params=vmem_of(40),
         cost_estimate=cost_of(8),
     )(feature_args[0], feature_args[1], feature_args[1], feature_args[1], *feature_args[2:])
     received = lax.all_to_all(packed, CHIPS, split_axis=0, concat_axis=0, tiled=True)

time: 152 us -> 158 us (1.039)
  Pallas kernels: 46.7 us -> 52.1 us
  waiting for transfers between devices: 16.6 us -> 13.6 us
  local copies, waits for them, and re-layouts: 10.2 us -> 11.8 us
    pallas_call x4, Pallas kernels: 18.4 us -> 23.7 us  [row_call(): pl.pallas_call(kernel, grid=(rows // STEP_ROWS,), in_specs=[pl.BlockSpec(...]
    ppermute x5, waiting for transfers between devices: 10.8 us -> 8.36 us  [pass_on(): return lax.ppermute(cells, axis, [(i + 1, i) for i in range(ends)])]
    all_to_all x1, starting transfers between devices: 13.7 us -> 16 us  [local_step(): lax.all_to_all(packed, CHIPS, split_axis=0, concat_axis=0, tiled=True)]
    unnamed x35 -> x49, local copies, waits for them, and re-layouts: 9.95 us -> 11.6 us
  transfers between devices with their start and end apart: 13 -> 13, of which waited for: 4 -> 4; matrix products, arithmetic and copies ran while one was open for 3% -> 3% of each run, Pallas kernels for 18% -> 20%
where the time goes in v7:
time: 158 us; the launch traced here: 157 us
  starting transfers between devices  55.9 us (35%)
  Pallas kernels  52.1 us (33%)
  blocking collectives  19.4 us (12%)
  waiting for transfers between devices  13.6 us (9%)
  local copies, waits for them, and re-layouts  11.8 us (7%)
  other arithmetic  3.49 us (2%)
    ppermute x5, starting transfers between devices, pass_on(): return lax.ppermute(cells, axis, [(i, i + 1) for i in range(ends)])  31.5 us
    pallas_call x4, Pallas kernels, row_call(): pl.pallas_call(kernel, grid=(rows // STEP_ROWS,), in_specs=[pl.BlockSpec(...  23.7 us
    all_to_all x1, blocking collectives, gather_all(): own = lax.all_to_all(spread, CHIPS, split_axis=0, concat_axis=0, tiled=True)  19.4 us
    all_to_all x1, starting transfers between devices, local_step(): lax.all_to_all(packed, CHIPS, split_axis=0, concat_axis=0, tiled=True)  16 us
    pallas_call x1, Pallas kernels, refine(): pl.pallas_call(functools.partial(affinity_kernel, full_rows=rows * lax.ax...  13.6 us
    unnamed x49, local copies, waits for them, and re-layouts  11.6 us
    pallas_call x1, Pallas kernels, local_step(): pl.pallas_call(feature_kernel, grid=(steps,), in_specs=[whole(back_up), p...  8.73 us
    ppermute x5, starting transfers between devices, pass_on(): return lax.ppermute(cells, axis, [(i + 1, i) for i in range(ends)])  8.37 us
  transfers between devices with their start and end apart: 13, of which 4 were waited for; matrix products, arithmetic and copies ran while one was open for 3% of the time, Pallas kernels for 20%

profile of v7, /device:TPU:1, one launch (start us, length us, event | category | flops | bytes accessed | tf_op | source)
XLA Modules:
  0.0 157.5 jit_solution(9827087637710729350)
XLA Ops:
  2.9 1.7 %copy-done.20 = bf16[256,16,256]{2,1,0:T(8,128)(2,1)S(1)} copy-done((bf16[256,16,256]{2,1,0:T(8,128)(2,1)S(1)}, bf16[256,16,256]{2,1,0:T(8,128)(2,1)}, u32[]{:S(2)}) %copy-start.20) | copy-done | bytes 2097176
  5.4 1.3 collective-permute-start.1
  6.8 4.7 %collective-permute-start = (bf16[8,112,256]{2,1,0:T(8,128)(2,1)S(1)}, bf16[8,112,256]{2,1,0:T(8,128)(2,1)S(1)}, u32[]{:S(2)}, u32[]{:S(2)}) collective-permute-start(bf16[8,112,256]{2,1,0:T(8,128)(2,1)S(1)} %pad_maximum_fusion), channel_id=1, source_target_pairs={{0,16},{16,32},{32,48},{48,64},{64,80},{80,96},{96,112},{1,17},{17... | collective-permute-start | bytes 1376264 | tf_op jit(solution)/shard_map/ppermute | solution.py:206
  11.5 7.7 %collective-permute-done.1.down_ref = bf16[8,112,256]{2,1,0:T(8,128)(2,1)S(1)} collective-permute-done((bf16[8,112,256]{2,1,0:T(8,128)(2,1)S(1)}, bf16[8,112,256]{2,1,0:T(8,128)(2,1)S(1)}, u32[]{:S(2)}, u32[]{:S(2)}) %collective-permute-start.1) | collective-permute-done | bytes 458784 | tf_op jit(solution)/shard_map/ppermute | solution.py:207
  21.3 6.7 %collective-permute-start.2 = (bf16[576,128]{1,0:T(8,128)(2,1)S(1)}, bf16[576,128]{1,0:T(8,128)(2,1)S(1)}, u32[]{:S(2)}, u32[]{:S(2)}) collective-permute-start(bf16[576,128]{1,0:T(8,128)(2,1)S(1)} %get-tuple-element.26), channel_id=1, source_target_pairs={{0,1},{1,2},{2,3},{3,4},{4,5},{5,6},{6,7},{7,8},{8,9},{9,10},{10,1... | collective-permute-start | bytes 442376 | tf_op jit(solution)/shard_map/ppermute | solution.py:206
  28.0 1.9 %collective-permute-start.3 = (bf16[576,128]{1,0:T(8,128)(2,1)S(1)}, bf16[576,128]{1,0:T(8,128)(2,1)S(1)}, u32[]{:S(2)}, u32[]{:S(2)}) collective-permute-start(bf16[576,128]{1,0:T(8,128)(2,1)S(1)} %get-tuple-element.27), channel_id=1, source_target_pairs={{1,0},{2,1},{3,2},{4,3},{5,4},{6,5},{7,6},{8,7},{9,8},{10,9},{11,1... | collective-permute-start | bytes 442376 | tf_op jit(solution)/shard_map/ppermute | solution.py:207
  30.0 6.0 %shard_map.84 = (f32[16,256,256]{2,1,0:T(8,128)S(1)}, bf16[768,768]{1,0:T(8,128)(2,1)S(1)}) custom-call(bf16[16,256,256]{2,1,0:T(8,128)(2,1)S(1)} %bitcast.19, bf16[9,256,256]{2,1,0:T(8,128)(2,1)S(1)} %copy-done.5), custom_call_target="tpu_custom_call" | custom-call | flops 8999999488 | bytes 27000000 | tf_op jit(solution)/shard_map/pallas_call | solution.py:581
  36.0 2.0 %copy-done.15 = f32[16,256,256]{2,1,0:T(8,128)} copy-done((f32[16,256,256]{2,1,0:T(8,128)}, f32[16,256,256]{2,1,0:T(8,128)S(1)}, u32[]{:S(2)}) %copy-start.15) | copy-done | bytes 4194328
  39.2 13.6 %affinity.1 = (f32[16,8,384]{2,1,0:T(8,128)S(1)}, f32[25,24,384]{2,1,0:T(8,128)S(1)}) custom-call(s32[2]{0:T(128)S(1)} %pad_add_fusion.place_ref, bf16[8,112,256]{2,1,0:T(8,128)(2,1)} %copy-done.8, bf16[16,80,256]{2,1,0:T(8,128)(2,1)} %copy-done.1, bf16[8,112,256]{2,1,0:T(8,128)(2,1)} %copy-done.6, bf16[576,128]{1,0:T(8,128)(2,1)S(1)} %collective-permute-done.2.left_ref, ...), custom_call_target="tpu_custom_call" | custom-call | flops 12000000000 | bytes 36000000 | tf_op jit(solution)/shard_map/affinity/pallas_call | solution.py:243
  52.8 9.0 %collective-permute-start.4 = (f32[8,8,384]{2,1,0:T(8,128)S(1)}, f32[8,8,384]{2,1,0:T(8,128)S(1)}, u32[]{:S(2)}, u32[]{:S(2)}) collective-permute-start(f32[8,8,384]{2,1,0:T(8,128)S(1)} %get-tuple-element.67), channel_id=1, source_target_pairs={{0,16},{16,32},{32,48},{48,64},{64,80},{80,96},{96,112},{1,17},{17... | collective-permute-start | bytes 294920 | tf_op jit(solution)/shard_map/ppermute | solution.py:206
  63.2 5.6 %shard_map.85 = (f32[16,256,256]{2,1,0:T(8,128)}, bf16[16,256,256]{2,1,0:T(8,128)(2,1)S(1)}, f32[16,8,256]{2,1,0:T(8,128)S(1)}) custom-call(bf16[8,112,256]{2,1,0:T(8,128)(2,1)S(1)} %copy-done.9, bf16[8,112,256]{2,1,0:T(8,128)(2,1)S(1)} %copy-done.7, bf16[576,128]{1,0:T(8,128)(2,1)S(1)} %collective-permute-done.2.left_ref, ...), custom_call_target="tpu_custom_call" | custom-call | flops 7000000000 | bytes 21000000 | tf_op jit(solution)/shard_map/pallas_call | solution.py:581
  69.5 2.7 %finish.1.refined_ref = f32[16,8,256]{2,1,0:T(8,128)S(1)} custom-call(f32[25,24,384]{2,1,0:T(8,128)S(1)} %get-tuple-element.28.weights_ref, f32[8,8,384]{2,1,0:T(8,128)S(1)} %collective-permute-done.4.up_ref, f32[16,8,384]{2,1,0:T(8,128)S(1)} %get-tuple-element.29.mid_ref, f32[8,8,384]{2,1,0:T(8,128)S(1)} %collective-permute-done.5.down_ref), custom_call_target="tpu_custom_call" | custom-call | flops 4000000000 | bytes 12000000 | tf_op jit(solution)/shard_map/finish/pallas_call | solution.py:274
  73.1 5.8 %collective-permute-start.6 = (bf16[1,256,256]{2,1,0:T(8,128)(2,1)S(1)}, bf16[1,256,256]{2,1,0:T(8,128)(2,1)S(1)}, u32[]{:S(2)}, u32[]{:S(2)}) collective-permute-start(bf16[1,256,256]{2,1,0:T(8,128)(2,1)S(1)} %get-tuple-element.61), channel_id=1, source_target_pairs={{0,16},{16,32},{32,48},{48,64},{64,80},{80,96},{96,112},{1,17},{17... | collective-permute-start | bytes 393224 | tf_op jit(solution)/shard_map/ppermute | solution.py:206
  78.9 1.5 collective-permute-start.7
  80.4 11.3 %shard_map.87 = (f32[64,40,128]{2,1,0:T(8,128)}, f32[64,40,128]{2,1,0:T(8,128)}) custom-call(s32[1]{0:T(128)} %bitcast.7.core_ref, bf16[8,112,256]{2,1,0:T(8,128)(2,1)} %copy-done.8, bf16[16,256,256]{2,1,0:T(8,128)(2,1)} %bitcast.20, bf16[8,112,256]{2,1,0:T(8,128)(2,1)} %copy-done.6, bf16[576,128]{1,0:T(8,128)(2,1)} %copy-done.10, ...), custom_call_target="tpu_custom_call" | custom-call | flops 8999999488 | bytes 27000000 | tf_op jit(solution)/shard_map/pallas_call | solution.py:581
  91.8 1.6 %copy-done.3 = bf16[16,256,256]{2,1,0:T(8,128)(2,1)S(1)} copy-done((bf16[16,256,256]{2,1,0:T(8,128)(2,1)S(1)}, bf16[16,256,256]{2,1,0:T(8,128)(2,1)}, u32[]{:S(2)}) %copy-start.3) | copy-done | bytes 2097176
  94.1 2.4 %collective-permute-start.10 = (bf16[256,128]{1,0:T(8,128)(2,1)S(1)}, bf16[256,128]{1,0:T(8,128)(2,1)S(1)}, u32[]{:S(2)}, u32[]{:S(2)}) collective-permute-start(bf16[256,128]{1,0:T(8,128)(2,1)S(1)} %get-tuple-element.43), channel_id=1, source_target_pairs={{1,0},{2,1},{3,2},{4,3},{5,4},{6,5},{7,6},{8,7},{9,8},{10,9},{11,1... | collective-permute-start | bytes 196616 | tf_op jit(solution)/shard_map/ppermute | solution.py:207
  96.5 5.2 %collective-permute-start.9 = (bf16[256,128]{1,0:T(8,128)(2,1)S(1)}, bf16[256,128]{1,0:T(8,128)(2,1)S(1)}, u32[]{:S(2)}, u32[]{:S(2)}) collective-permute-start(bf16[256,128]{1,0:T(8,128)(2,1)S(1)} %get-tuple-element.42), channel_id=1, source_target_pairs={{0,1},{1,2},{2,3},{3,4},{4,5},{5,6},{6,7},{7,8},{8,9},{9,10},{10,1... | collective-permute-start | bytes 196616 | tf_op jit(solution)/shard_map/ppermute | solution.py:206
  103.2 16.0 %all-to-all-start = ((f16[64,40,128]{2,1,0:T(8,128)(2,1)}), f16[64,40,128]{2,1,0:T(8,128)(2,1)S(1)}, u32[]{:S(2)}, u32[]{:S(2)}) async-start(f16[64,40,128]{2,1,0:T(8,128)(2,1)} %select_convert_fusion), calls=%async_computation | async-start | bytes 1310720 | tf_op jit(solution)/shard_map/all_to_all | solution.py:670
  119.2 8.7 %feature.1 = bf16[16,256,256]{2,1,0:T(8,128)(2,1)S(1)} custom-call(bf16[1,256,256]{2,1,0:T(8,128)(2,1)} %copy-done.12, bf16[16,256,256]{2,1,0:T(8,128)(2,1)} %copy-done.2, bf16[16,256,256]{2,1,0:T(8,128)(2,1)} %copy-done.2, bf16[16,256,256]{2,1,0:T(8,128)(2,1)} %copy-done.2, bf16[1,256,256]{2,1,0:T(8,128)(2,1)} %copy-done.13, ...), custom_call_target="tpu_custom_call" | custom-call | flops 8000000000 | bytes 24000000 | tf_op jit(solution)/shard_map/feature/pallas_call | solution.py:652
  128.0 4.2 %all-to-all-done = f16[64,40,128]{2,1,0:T(8,128)(2,1)S(1)} async-done(((f16[64,40,128]{2,1,0:T(8,128)(2,1)}), f16[64,40,128]{2,1,0:T(8,128)(2,1)S(1)}, u32[]{:S(2)}, u32[]{:S(2)}) %all-to-all-start) | async-done | bytes 655392 | tf_op jit(solution)/shard_map/all_to_all | solution.py:670
  132.7 19.4 %all_to_all.10 = f16[64,40,128]{2,1,0:T(8,128)(2,1)S(1)} all-to-all(f16[64,40,128]{2,1,0:T(8,128)(2,1)S(1)} %broadcast_in_dim.36), channel_id=1, replica_groups=mesh['row'=8,'pair'=8,'core'=2] {'row','pair'}, dimensions={0} | all-to-all | bytes 1310720 | tf_op jit(solution)/shard_map/all_to_all | solution.py:358
  152.8 2.5 %copy.22 = bf16[256,16,256]{2,1,0:T(8,128)(2,1)} copy(bf16[256,16,256]{2,0,1:T(8,128)(2,1)S(1)} %bitcast.21) | data formatting | bytes 4194304
  155.7 1.7 %place.1 = (f32[9,256,256]{2,1,0:T(8,128)}, f32[8,256]{1,0:T(8,128)}) custom-call(s32[1]{0:T(128)} %bitcast.7.core_ref, f32[64,40,128]{2,1,0:T(8,128)S(1)} %convert_multiply_fusion.1.own_ref, f32[64,40,128]{2,1,0:T(8,128)S(1)} %convert_multiply_fusion.other_ref), custom_call_target="tpu_custom_call" | custom-call | flops 2000000000 | bytes 6000000 | tf_op jit(solution)/shard_map/place/pallas_call | solution.py:361
  (85 shorter events, 13.2 us)
Async XLA Ops:
  2.9 17.4 %copy-start.1 = (bf16[16,80,256]{2,1,0:T(8,128)(2,1)}, bf16[16,80,256]{2,1,0:T(8,128)(2,1)S(1)}, u32[]{:S(2)}) copy-start(bf16[16,80,256]{2,1,0:T(8,128)(2,1)S(1)} %maximum_bitcast_fusion.mid_ref) | copy-start | bytes 1966084
  5.4 24.6 %copy-start = (bf16[256,16,256]{2,0,1:T(8,128)(2,1)}, bf16[256,16,256]{2,0,1:T(8,128)(2,1)S(1)}, u32[]{:S(2)}) copy-start(bf16[256,16,256]{2,0,1:T(8,128)(2,1)S(1)} %copy.26) | copy-start | bytes 6291460
  5.4 13.7 %collective-permute-start.1 = (bf16[8,112,256]{2,1,0:T(8,128)(2,1)S(1)}, bf16[8,112,256]{2,1,0:T(8,128)(2,1)S(1)}, u32[]{:S(2)}, u32[]{:S(2)}) collective-permute-start(bf16[8,112,256]{2,1,0:T(8,128)(2,1)S(1)} %pad_maximum_fusion.1), channel_id=1, source_target_pairs={{16,0},{32,16},{48,32},{64,48},{80,64},{96,80},{112,96},{17,1},{33... | collective-permute-start | bytes 1376264 | tf_op jit(solution)/shard_map/ppermute | solution.py:207
  6.8 23.2 %copy-start.5 = (bf16[9,256,256]{2,1,0:T(8,128)(2,1)S(1)}, bf16[9,256,256]{2,1,0:T(8,128)(2,1)}, u32[]{:S(2)}) copy-start(bf16[9,256,256]{2,1,0:T(8,128)(2,1)} %taps_ref.3) | copy-start | bytes 3538948
  6.8 13.5 %collective-permute-start = (bf16[8,112,256]{2,1,0:T(8,128)(2,1)S(1)}, bf16[8,112,256]{2,1,0:T(8,128)(2,1)S(1)}, u32[]{:S(2)}, u32[]{:S(2)}) collective-permute-start(bf16[8,112,256]{2,1,0:T(8,128)(2,1)S(1)} %pad_maximum_fusion), channel_id=1, source_target_pairs={{0,16},{16,32},{32,48},{48,64},{64,80},{80,96},{96,112},{1,17},{17... | collective-permute-start | bytes 1376264 | tf_op jit(solution)/shard_map/ppermute | solution.py:206
  21.3 17.9 %collective-permute-start.2 = (bf16[576,128]{1,0:T(8,128)(2,1)S(1)}, bf16[576,128]{1,0:T(8,128)(2,1)S(1)}, u32[]{:S(2)}, u32[]{:S(2)}) collective-permute-start(bf16[576,128]{1,0:T(8,128)(2,1)S(1)} %get-tuple-element.26), channel_id=1, source_target_pairs={{0,1},{1,2},{2,3},{3,4},{4,5},{5,6},{6,7},{7,8},{8,9},{9,10},{10,1... | collective-permute-start | bytes 442376 | tf_op jit(solution)/shard_map/ppermute | solution.py:206
  28.0 10.9 %copy-start.4 = (bf16[256,8]{0,1:T(8,128)(2,1)S(1)}, bf16[256,8]{0,1:T(8,128)(2,1)}, u32[]{:S(2)}) copy-start(bf16[256,8]{0,1:T(8,128)(2,1)} %param.9) | copy-start | bytes 12292
  28.0 11.2 %collective-permute-start.3 = (bf16[576,128]{1,0:T(8,128)(2,1)S(1)}, bf16[576,128]{1,0:T(8,128)(2,1)S(1)}, u32[]{:S(2)}, u32[]{:S(2)}) collective-permute-start(bf16[576,128]{1,0:T(8,128)(2,1)S(1)} %get-tuple-element.27), channel_id=1, source_target_pairs={{1,0},{2,1},{3,2},{4,3},{5,4},{6,5},{7,6},{8,7},{9,8},{10,9},{11,1... | collective-permute-start | bytes 442376 | tf_op jit(solution)/shard_map/ppermute | solution.py:207
  39.2 24.0 %copy-start.7 = (bf16[8,112,256]{2,1,0:T(8,128)(2,1)S(1)}, bf16[8,112,256]{2,1,0:T(8,128)(2,1)}, u32[]{:S(2)}) copy-start(bf16[8,112,256]{2,1,0:T(8,128)(2,1)} %copy-done.6) | copy-start | bytes 1376260
  39.2 24.0 %copy-start.9 = (bf16[8,112,256]{2,1,0:T(8,128)(2,1)S(1)}, bf16[8,112,256]{2,1,0:T(8,128)(2,1)}, u32[]{:S(2)}) copy-start(bf16[8,112,256]{2,1,0:T(8,128)(2,1)} %copy-done.8) | copy-start | bytes 1376260
  39.2 24.0 %copy-start.19 = (bf16[768,768]{1,0:T(8,128)(2,1)S(1)}, bf16[768,768]{1,0:T(8,128)(2,1)}, u32[]{:S(2)}) copy-start(bf16[768,768]{1,0:T(8,128)(2,1)} %copy-done.18) | copy-start | bytes 3538948
  39.2 24.0 %copy-start.10 = (bf16[576,128]{1,0:T(8,128)(2,1)}, bf16[576,128]{1,0:T(8,128)(2,1)S(1)}, u32[]{:S(2)}) copy-start(bf16[576,128]{1,0:T(8,128)(2,1)S(1)} %collective-permute-done.2.left_ref) | copy-start | bytes 442372
  39.2 24.0 %copy-start.11 = (bf16[576,128]{1,0:T(8,128)(2,1)}, bf16[576,128]{1,0:T(8,128)(2,1)S(1)}, u32[]{:S(2)}) copy-start(bf16[576,128]{1,0:T(8,128)(2,1)S(1)} %collective-permute-done.3.right_ref) | copy-start | bytes 442372
  52.8 16.0 %collective-permute-start.4 = (f32[8,8,384]{2,1,0:T(8,128)S(1)}, f32[8,8,384]{2,1,0:T(8,128)S(1)}, u32[]{:S(2)}, u32[]{:S(2)}) collective-permute-start(f32[8,8,384]{2,1,0:T(8,128)S(1)} %get-tuple-element.67), channel_id=1, source_target_pairs={{0,16},{16,32},{32,48},{48,64},{64,80},{80,96},{96,112},{1,17},{17... | collective-permute-start | bytes 294920 | tf_op jit(solution)/shard_map/ppermute | solution.py:206
  61.9 7.6 %collective-permute-start.5 = (f32[8,8,384]{2,1,0:T(8,128)S(1)}, f32[8,8,384]{2,1,0:T(8,128)S(1)}, u32[]{:S(2)}, u32[]{:S(2)}) collective-permute-start(f32[8,8,384]{2,1,0:T(8,128)S(1)} %get-tuple-element.66), channel_id=1, source_target_pairs={{16,0},{32,16},{48,32},{64,48},{80,64},{96,80},{112,96},{17,1},{33... | collective-permute-start | bytes 294920 | tf_op jit(solution)/shard_map/ppermute | solution.py:207
  73.0 7.3 %copy-start.2 = (bf16[16,256,256]{2,1,0:T(8,128)(2,1)}, bf16[16,256,256]{2,1,0:T(8,128)(2,1)S(1)}, u32[]{:S(2)}) copy-start(bf16[16,256,256]{2,1,0:T(8,128)(2,1)S(1)} %get-tuple-element.34.back_ref.mid_ref.above_ref.below_ref) | copy-start | bytes 6291460
  73.1 18.6 %collective-permute-start.6 = (bf16[1,256,256]{2,1,0:T(8,128)(2,1)S(1)}, bf16[1,256,256]{2,1,0:T(8,128)(2,1)S(1)}, u32[]{:S(2)}, u32[]{:S(2)}) collective-permute-start(bf16[1,256,256]{2,1,0:T(8,128)(2,1)S(1)} %get-tuple-element.61), channel_id=1, source_target_pairs={{0,16},{16,32},{32,48},{48,64},{64,80},{80,96},{96,112},{1,17},{17... | collective-permute-start | bytes 393224 | tf_op jit(solution)/shard_map/ppermute | solution.py:206
  78.9 12.8 %collective-permute-start.7 = (bf16[1,256,256]{2,1,0:T(8,128)(2,1)S(1)}, bf16[1,256,256]{2,1,0:T(8,128)(2,1)S(1)}, u32[]{:S(2)}, u32[]{:S(2)}) collective-permute-start(bf16[1,256,256]{2,1,0:T(8,128)(2,1)S(1)} %get-tuple-element.60), channel_id=1, source_target_pairs={{16,0},{32,16},{48,32},{64,48},{80,64},{96,80},{112,96},{17,1},{33... | collective-permute-start | bytes 393224 | tf_op jit(solution)/shard_map/ppermute | solution.py:207
  91.7 10.1 %collective-permute-start.8 = (f32[64,40,128]{2,1,0:T(8,128)}, f32[64,40,128]{2,1,0:T(8,128)S(1)}, u32[]{:S(2)}, u32[]{:S(2)}) collective-permute-start(f32[64,40,128]{2,1,0:T(8,128)} %get-tuple-element.39), channel_id=1, source_target_pairs={{0,1},{1,0},{2,3},{3,2},{4,5},{5,4},{6,7},{7,6},{8,9},{9,8},{10,11... | collective-permute-start | bytes 3932168 | tf_op jit(solution)/shard_map/ppermute | solution.py:646
  93.4 8.4 %copy-start.21 = (f32[64,40,128]{2,1,0:T(8,128)S(1)}, f32[64,40,128]{2,1,0:T(8,128)}, u32[]{:S(2)}) copy-start(f32[64,40,128]{2,1,0:T(8,128)} %get-tuple-element.37) | copy-start | bytes 3932164
  94.1 25.1 %collective-permute-start.10 = (bf16[256,128]{1,0:T(8,128)(2,1)S(1)}, bf16[256,128]{1,0:T(8,128)(2,1)S(1)}, u32[]{:S(2)}, u32[]{:S(2)}) collective-permute-start(bf16[256,128]{1,0:T(8,128)(2,1)S(1)} %get-tuple-element.43), channel_id=1, source_target_pairs={{1,0},{2,1},{3,2},{4,3},{5,4},{6,5},{7,6},{8,7},{9,8},{10,9},{11,1... | collective-permute-start | bytes 196616 | tf_op jit(solution)/shard_map/ppermute | solution.py:207
  96.5 22.7 %collective-permute-start.9 = (bf16[256,128]{1,0:T(8,128)(2,1)S(1)}, bf16[256,128]{1,0:T(8,128)(2,1)S(1)}, u32[]{:S(2)}, u32[]{:S(2)}) collective-permute-start(bf16[256,128]{1,0:T(8,128)(2,1)S(1)} %get-tuple-element.42), channel_id=1, source_target_pairs={{0,1},{1,2},{2,3},{3,4},{4,5},{5,6},{6,7},{7,8},{8,9},{9,10},{10,1... | collective-permute-start | bytes 196616 | tf_op jit(solution)/shard_map/ppermute | solution.py:206
  103.2 28.9 %all-to-all-start = ((f16[64,40,128]{2,1,0:T(8,128)(2,1)}), f16[64,40,128]{2,1,0:T(8,128)(2,1)S(1)}, u32[]{:S(2)}, u32[]{:S(2)}) async-start(f16[64,40,128]{2,1,0:T(8,128)(2,1)} %select_convert_fusion), calls=%async_computation | async-start | bytes 1310720 | tf_op jit(solution)/shard_map/all_to_all | solution.py:670
  152.1 3.4 %collective-permute-start.11 = (f16[64,40,128]{2,1,0:T(8,128)(2,1)S(1)}, f16[64,40,128]{2,1,0:T(8,128)(2,1)S(1)}, u32[]{:S(2)}, u32[]{:S(2)}) collective-permute-start(f16[64,40,128]{2,1,0:T(8,128)(2,1)S(1)} %all_to_all.10), channel_id=1, source_target_pairs={{0,1},{1,0},{2,3},{3,2},{4,5},{5,4},{6,7},{7,6},{8,9},{9,8},{10,11... | collective-permute-start | bytes 1966088 | tf_op jit(solution)/shard_map/ppermute | solution.py:359
  (11 other events, 27.7 us)
